TPU v7x, 32 devices: a whole 2x2x4 slice. The times are simulated.
32 devices in a mesh: section: 4 (over z), dp: 8 (over y, x, core).
Axes of the slice: x: 2, y: 2, z: 4, core: 2. Of those that a mesh axis runs over, the one named last changes fastest.
Arguments:
- block_input: bfloat16 [4, 8, 8, 64, 768], P('section', 'dp'), may hold values from -6 to 6
- grad_output: bfloat16 [4, 8, 8, 64, 768], P('section', 'dp'), may hold values from -6 to 6
- depth_weight: bfloat16 [4, 49, 768], P('section'), may hold values from -0.875 to 0.875
- depth_bias: float32 [4, 768], P('section'), may hold values from -0.5 to 0.5
- norm_gain: float32 [4, 768], P('section'), may hold values from 0.25 to 1.75
- norm_shift: float32 [4, 768], P('section'), may hold values from -0.5 to 0.5
- pw1_weight: bfloat16 [4, 3072, 768], P('section'), may hold values from -0.21875 to 0.21875
- pw1_bias: float32 [4, 3072], P('section'), may hold values from -1 to 1
- pw2_weight: bfloat16 [4, 768, 3072], P('section'), may hold values from -0.109375 to 0.109375
- pw2_bias: float32 [4, 768], P('section'), may hold values from -0.5 to 0.5
- layer_scale: float32 [4, 768], P('section'), may hold values from 0.2 to 2
Outputs:
- grad_pw1: float32 [4, 3072, 768], P('section', 'dp')
- grad_pw2: float32 [4, 768, 3072], P('section', None, 'dp')
- grad_bias1: float32 [4, 3072], P('section')
- grad_small: float32 [4, 54, 768], P('section')
- received: bfloat16 [4, 8, 8, 64, 768], P('section', 'dp')
All inputs are finite; a program needn't handle non-finite values.
Results may differ from a plain program's by a relative error of at most 0.0061.
Values may be sent and summed in bfloat16 or wider, within the bound.
No kernel may reach another device: no remote copies, remote signals or barrier semaphores. Data moves between devices by JAX's collectives and lax.ppermute only.
A program may use at most 256 MiB of HBM per device.

v0:
```python
import jax
import jax.numpy as jnp
from jax import lax
from jax.sharding import PartitionSpec as P

root_half = 0.7071067811865476
inv_root_two_pi = 0.3989422804014327


def shifted(block, axis, distance):
    devices = range(lax.axis_size(axis))
    route = [(i - distance, i) for i in devices if i - distance in devices]
    return lax.ppermute(block, axis, route)


def contract_last(left, right):
    return lax.dot_general(
        left, right, (((1,), (1,)), ((), ())), preferred_element_type=jnp.float32
    )


def contract_first(left, right):
    return lax.dot_general(
        left, right, (((0,), (0,)), ((), ())), preferred_element_type=jnp.float32
    )


def tap_apply(padded, weights, rows, cols, flip):
    total = jnp.zeros((rows, cols, weights.shape[1]), jnp.float32)
    for i in range(7):
        for j in range(7):
            if flip:
                window = padded[6 - i : 6 - i + rows, 6 - j : 6 - j + cols]
            else:
                window = padded[i : i + rows, j : j + cols]
            total = total + window * weights[7 * i + j]
    return total


def tap_grads(padded, grad, rows, cols):
    pieces = []
    for i in range(7):
        for j in range(7):
            pieces.append(jnp.sum(grad * padded[i : i + rows, j : j + cols], axis=(0, 1)))
    return jnp.stack(pieces)


def shards(
    block_input,
    grad_output,
    depth_weight,
    depth_bias,
    norm_gain,
    norm_shift,
    pw1_weight,
    pw1_bias,
    pw2_weight,
    pw2_bias,
    layer_scale,
):
    block_x = block_input[0, 0]
    block_g = grad_output[0, 0]
    rows, cols, chans = block_x.shape
    cells = rows * cols
    w_one = pw1_weight[0]
    w_two = pw2_weight[0]
    gain = norm_gain[0]
    replicas = lax.axis_size("dp")
    factor = 1.0 / replicas
    inputs = block_x.astype(jnp.float32)
    padded = jnp.pad(inputs, ((3, 3), (3, 3), (0, 0)))
    weights = depth_weight[0].astype(jnp.float32)
    depthwise = tap_apply(padded, weights, rows, cols, False) + depth_bias[0]
    centered = depthwise - jnp.mean(depthwise, axis=-1, keepdims=True)
    rstd = lax.rsqrt(jnp.mean(centered * centered, axis=-1, keepdims=True) + 1e-06)
    normed = (centered * rstd).reshape(cells, chans)
    ynorm = (normed * gain + norm_shift[0]).astype(jnp.bfloat16)
    preact = contract_last(ynorm, w_one) + pw1_bias[0]
    cdf = 0.5 * (1.0 + lax.erf(preact * root_half))
    hidden = (preact * cdf).astype(jnp.bfloat16)
    branch = contract_last(hidden, w_two) + pw2_bias[0]
    grads = block_g.reshape(cells, chans).astype(jnp.float32)
    gscale_term = jnp.sum(grads * branch, axis=0)
    gproj = (grads * layer_scale[0]).astype(jnp.bfloat16)
    b2_term = jnp.sum(gproj.astype(jnp.float32), axis=0)
    ghidden = jnp.dot(gproj, w_two, preferred_element_type=jnp.float32)
    density = jnp.exp(-0.5 * preact * preact) * inv_root_two_pi
    gpre = (ghidden * (cdf + preact * density)).astype(jnp.bfloat16)
    b1_term = jnp.sum(gpre.astype(jnp.float32), axis=0)
    gnorm = jnp.dot(gpre, w_one, preferred_element_type=jnp.float32)
    gpre_cols, hidden_cols = (
        lax.all_to_all(gpre, "dp", split_axis=1, concat_axis=0, tiled=True),
        lax.all_to_all(hidden, "dp", split_axis=1, concat_axis=0, tiled=True),
    )
    w1_share = contract_first(gpre_cols, lax.all_gather(ynorm, "dp", axis=0, tiled=True))
    w2_share = contract_first(lax.all_gather(gproj, "dp", axis=0, tiled=True), hidden_cols)
    gain_term = jnp.sum(gnorm * normed, axis=0)
    shift_term = jnp.sum(gnorm, axis=0)
    scaled_g = gnorm * gain
    gdepth = rstd.reshape(cells, 1) * (
        scaled_g
        - jnp.mean(scaled_g, axis=-1, keepdims=True)
        - normed * jnp.mean(scaled_g * normed, axis=-1, keepdims=True)
    )
    gdepth = gdepth.reshape(rows, cols, chans)
    tap_term = tap_grads(padded, gdepth, rows, cols)
    dbias_term = jnp.sum(gdepth, axis=(0, 1))
    gpadded = jnp.pad(gdepth, ((3, 3), (3, 3), (0, 0)))
    ginput = (block_g.astype(jnp.float32) + tap_apply(gpadded, weights, rows, cols, True)).astype(
        jnp.bfloat16
    )
    received = shifted(ginput, "section", -1)
    small = jnp.concatenate(
        [tap_term, jnp.stack([dbias_term, gain_term, shift_term, b2_term, gscale_term])], axis=0
    )
    small_sum, b1_sum = lax.psum((small, b1_term), "dp")
    return (
        (w1_share * factor)[None],
        (w2_share * factor)[None],
        (b1_sum * factor)[None],
        (small_sum * factor)[None],
        received[None, None],
    )


def solution(mesh):
    in_specs = (
        P("section", "dp", None, None, None),
        P("section", "dp", None, None, None),
        P("section", None, None),
        P("section", None),
        P("section", None),
        P("section", None),
        P("section", None, None),
        P("section", None),
        P("section", None, None),
        P("section", None),
        P("section", None),
    )
    out_specs = (
        P("section", "dp", None),
        P("section", None, "dp"),
        P("section", None),
        P("section", None, None),
        P("section", "dp", None, None, None),
    )
    return jax.shard_map(shards, mesh=mesh, in_specs=in_specs, out_specs=out_specs, check_vma=False)
```

profile of v0, /device:TPU:0, one launch (start us, length us, event | category | flops | bytes accessed | tf_op | source)
XLA Modules:
  0.0 252.6 jit_solution(18249807545230620662)
XLA Ops:
  7.2 0.9 convert_element_type.73
  8.6 1.3 convert_bitcast_fusion
  9.9 10.3 %fusion.128 = (f32[8,64]{1,0:T(8,128)S(1)}, f32[8,64,768]{2,1,0:T(8,128)S(1)}) fusion(f32[768]{0:T(1024)S(1)} %reduce.53, f32[768]{0:T(1024)S(1)} %get-tuple-element.60, f32[768]{0:T(1024)S(1)} %get-tuple-element.61, f32[768]{0:T(1024)S(1)} %get-tuple-element.62, f32[768]{0:T(1024)S(1)} %get-tuple-element.63, f32[768]{0:T(1024)S(1)} %get-tuple-element.64, ...), kind=kLoop, calls=%fused_computation.346 | loop fusion | flops 38927872 | bytes 3301376 | tf_op jit(solution)/shard_map/reduce_sum | solution.py:74
  21.4 0.8 copy-done
  22.4 1.2 copy-done.9
  23.6 4.7 %multiply_convert_fusion = (bf16[512,3072]{1,0:T(8,128)(2,1)}, f32[512,3072]{1,0:T(8,128)S(1)}) fusion(f32[3072]{0:T(1024)S(1)} %bitcast.142, bf16[512,768]{1,0:T(8,128)(2,1)S(1)} %bitcast.138, bf16[1,3072,768]{2,1,0:T(8,128)(2,1)S(1)} %copy-done.9), kind=kOutput, calls=%fused_computation.104 | convolution fusion | flops 2425356288 | bytes 14954496 | tf_op jit(solution)/shard_map/dot_general | solution.py:17
  28.3 4.8 %convert_reduce_fusion = (f32[3072]{0:T(1024)S(1)}, bf16[512,3072]{1,0:T(8,128)(2,1)S(1)}) fusion(f32[512,3072]{1,0:T(8,128)S(1)} %get-tuple-element.118, f32[3072]{0:T(1024)S(1)} %bitcast.143, bf16[512,768]{1,0:T(8,128)(2,1)S(1)} %bitcast.137, bf16[1,768,3072]{2,1,0:T(8,128)(2,1)S(1)} %bitcast.141), kind=kOutput, calls=%fused_computation.103 | convolution fusion | flops 2436363264 | bytes 14966784 | tf_op jit(solution)/shard_map/dot_general | solution.py:86
  33.1 2.9 %fusion.120 = (f32[768]{0:T(1024)S(1)}, f32[512]{0:T(512)S(1)}, f32[512]{0:T(512)S(1)}, f32[768]{0:T(1024)S(1)}, f32[512,768]{1,0:T(8,128)S(1)}) fusion(f32[8,64,768]{2,1,0:T(8,128)S(1)} %get-tuple-element.112, f32[768]{0:T(1024)S(1)} %reduce.54, bf16[512,3072]{1,0:T(8,128)(2,1)S(1)} %get-tuple-element.120, bf16[1,3072,768]{2,1,0:T(8,128)(2,1)S(1)} %copy-done.9), kind=kOutput, calls=%fused_computation.230 | convolution fusion | flops 2418669056 | bytes 11023360 | tf_op jit(solution)/shard_map/dot_general | solution.py:90
  36.1 1.5 fusion.125
  37.6 5.0 %multiply_reduce_fusion = (f32[768]{0:T(1024)S(1)}, f32[768]{0:T(1024)S(1)}, f32[768]{0:T(1024)S(1)}, f32[768]{0:T(1024)S(1)}, f32[768]{0:T(1024)S(1)}, /*index=...) fusion(f32[8,64,768]{2,1,0:T(8,128)S(1)} %convert_bitcast_fusio, ...), kind=kLoop, calls=%fused_computation.232 | loop fusion | flops 14141952 | bytes 3201024 | tf_op jit(solution)/shard_map/reduce_sum | solution.py:44
  42.7 5.3 %multiply_reduce_fusion.1 = (f32[768]{0:T(1024)S(1)}, f32[768]{0:T(1024)S(1)}, f32[768]{0:T(1024)S(1)}, f32[768]{0:T(1024)S(1)}, f32[768]{0:T(1024)S(1)}, /*inde...) fusion(f32[8,64,768]{2,1,0:T(8,128)S(1)} %convert_bitcast_fusio, ...), kind=kLoop, calls=%fused_computation.233 | loop fusion | flops 14141952 | bytes 3201024 | tf_op jit(solution)/shard_map/reduce_sum | solution.py:44
  48.0 2.1 multiply_reduce_fusion.2
  50.8 6.1 %fusion.114 = f32[768]{0:T(1024)S(1)} fusion(bf16[1,1,8,64,768]{4,3,2,1,0:T(8,128)(2,1)} %param.12, bf16[512,3072]{1,0:T(8,128)(2,1)} %get-tuple-element.117, bf16[1,768,3072]{2,1,0:T(8,128)(2,1)} %param.19, f32[768]{0:T(1024)S(1)} %reduce.56), kind=kOutput, calls=%fused_computation.220 | convolution fusion | flops 2417491200 | bytes 8656896 | tf_op jit(solution)/shard_map/dot_general | solution.py:17
  56.9 4.5 %concatenate.3 = f32[54,768]{1,0:T(8,128)} concatenate(f32[1,768]{1,0:T(1,128)S(1)} %stack.162, f32[1,768]{1,0:T(1,128)S(1)} %stack.163, f32[1,768]{1,0:T(1,128)S(1)} %stack.164, f32[1,768]{1,0:T(1,128)S(1)} %stack.165, f32[1,768]{1,0:T(1,128)S(1)} %stack.166, f32[1,768]{1,0:T(1,128)S(1)} %stack.167, f32[1,768]{1,0:T(1,128)S(1)} %stack.168, f32[1,768]{1,0:T(1,128)S(1)} %stack.169, ...), dimensions={0} | concatenate | bytes 331776 | tf_op jit(solution)/shard_map/concatenate | solution.py:113
  61.5 0.7 all-gather.3.cloned.1.call-update
  62.3 1.0 fusion.113
  63.3 3.9 %copy.23 = bf16[64,8,8,384]{3,2,0,1:T(8,128)(2,1)} copy(bf16[64,8,8,384]{3,2,1,0:T(8,128)(2,1)} %bitcast.135) | data formatting | bytes 6291456 | tf_op jit(solution)/shard_map/all_to_all | solution.py:92
  67.2 5.2 %all-to-all-start = ((bf16[512,8,384]{2,0,1:T(8,128)(2,1)}), bf16[512,8,384]{2,0,1:T(8,128)(2,1)}, u32[]{:S(2)}, u32[]{:S(2)}) async-start(bf16[512,8,384]{2,0,1:T(8,128)(2,1)} %bitcast.133), calls=%async_computation | async-start | bytes 6291456 | tf_op jit(solution)/shard_map/all_to_all | solution.py:92
  72.4 3.9 %copy.22 = bf16[64,8,8,384]{3,2,0,1:T(8,128)(2,1)} copy(bf16[64,8,8,384]{3,2,1,0:T(8,128)(2,1)} %bitcast.134) | data formatting | bytes 6291456 | tf_op jit(solution)/shard_map/all_to_all | solution.py:93
  76.3 34.6 %all-to-all-done = bf16[512,8,384]{2,0,1:T(8,128)(2,1)} async-done(((bf16[512,8,384]{2,0,1:T(8,128)(2,1)}), bf16[512,8,384]{2,0,1:T(8,128)(2,1)}, u32[]{:S(2)}, u32[]{:S(2)}) %all-to-all-start) | async-done | bytes 3145760 | tf_op jit(solution)/shard_map/all_to_all | solution.py:92
  111.0 4.5 %all-to-all-start.1 = ((bf16[512,8,384]{2,0,1:T(8,128)(2,1)}), bf16[512,8,384]{2,0,1:T(8,128)(2,1)}, u32[]{:S(2)}, u32[]{:S(2)}) async-start(bf16[512,8,384]{2,0,1:T(8,128)(2,1)} %bitcast.132), calls=%async_computation.1 | async-start | bytes 6291456 | tf_op jit(solution)/shard_map/all_to_all | solution.py:93
  115.4 9.6 %fusion.107 = bf16[8,64,768]{2,1,0:T(8,128)(2,1)S(1)} fusion(f32[8,64,768]{2,1,0:T(8,128)S(1)} %bitcast.131, bf16[1,1,8,64,768]{4,3,2,1,0:T(8,128)(2,1)S(1)} %copy-done.1, f32[768]{0:T(1024)S(1)} %get-tuple-element.60, f32[768]{0:T(1024)S(1)} %get-tuple-element.61, f32[768]{0:T(1024)S(1)} %get-tuple-element.62, f32[768]{0:T(1024)S(1)} %get-tuple-element.63, ...), kind=kLoop, calls=%fused_computation.209 | loop fusion | flops 39321600 | bytes 3296256 | tf_op jit(solution)/shard_map/convert_element_type | solution.py:109
  125.1 1.3 collective-permute-start
  126.4 47.5 %psum.14 = f32[3072]{0:T(1024)S(1)} all-reduce(f32[3072]{0:T(1024)S(1)} %get-tuple-element.119), channel_id=1, replica_groups=mesh['section'=4,'dp'=8] {'dp'}, use_global_device_ids=true, to_apply=%region_3.4 | all-reduce | flops 3072 | bytes 24576 | tf_op jit(solution)/shard_map/psum | solution.py:116
  173.9 0.6 broadcast_multiply_fusion.1
  174.5 0.9 broadcast_multiply_fusion
  175.5 0.8 broadcast_in_dim.22
  176.2 12.7 %all-gather.3.cloned.1.call-done = bf16[4096,768]{1,0:T(8,128)(2,1)} async-done(((bf16[512,768]{1,0:T(8,128)(2,1)}), bf16[4096,768]{1,0:T(8,128)(2,1)}) %all-gather.3.cloned.1.call-update) | async-done | bytes 6291472 | tf_op jit(solution)/shard_map/all_gather | solution.py:95
  189.0 7.4 %fusion.123 = f32[1,384,768]{2,1,0:T(8,128)} fusion(bf16[4096,384]{1,0:T(8,128)(2,1)} %bitcast.7, bf16[4096,768]{1,0:T(8,128)(2,1)} %all-gather.3.cloned.1.call-done), kind=kOutput, calls=%fused_computation.286 | convolution fusion | flops 2416214016 | bytes 10616832 | tf_op jit(solution)/shard_map/dot_general | solution.py:23
  196.4 40.6 %all-gather.5.cloned.1.call-done = bf16[4096,768]{1,0:T(8,128)(2,1)} async-done(((bf16[512,768]{1,0:T(8,128)(2,1)}), bf16[4096,768]{1,0:T(8,128)(2,1)}) %all-gather.5.cloned.1.call-update) | async-done | bytes 6291472 | tf_op jit(solution)/shard_map/all_gather | solution.py:96
  237.0 8.2 %fusion.124 = f32[1,768,384]{2,1,0:T(8,128)} fusion(bf16[4096,768]{1,0:T(8,128)(2,1)} %all-gather.5.cloned.1.call-done, bf16[4096,384]{1,0:T(8,128)(2,1)} %bitcast.12), kind=kOutput, calls=%fused_computation.287 | convolution fusion | flops 2416214016 | bytes 10616832 | tf_op jit(solution)/shard_map/dot_general | solution.py:23
  245.1 0.9 copy.26
  (102 shorter events, 2.2 us)
Async XLA Ops:
  7.2 2.7 %copy-start.4 = (f32[1,768]{1,0:T(1,128)S(1)}, f32[1,768]{1,0:T(1,128)}, u32[]{:S(2)}) copy-start(f32[1,768]{1,0:T(1,128)} %param.14) | copy-start | bytes 9220
  7.2 167.3 %all-reduce.4.cloned.1.call-start = ((), (), s32[]{:S(2)}) async-start(), calls=%async_computation.4 | async-start | bytes 344064 | tf_op jit(solution)/shard_map/psum | solution.py:116
  20.2 0.7 copy-start.5
  20.2 0.7 copy-start.6
  20.2 0.7 copy-start.7
  21.0 1.1 copy-start
  21.0 2.6 %copy-start.9 = (bf16[1,3072,768]{2,1,0:T(8,128)(2,1)S(1)}, bf16[1,3072,768]{2,1,0:T(8,128)(2,1)}, u32[]{:S(2)}) copy-start(bf16[1,3072,768]{2,1,0:T(8,128)(2,1)} %param.17) | copy-start | bytes 14155780
  21.0 2.6 %copy-start.10 = (f32[1,3072]{1,0:T(1,128)S(1)}, f32[1,3072]{1,0:T(1,128)}, u32[]{:S(2)}) copy-start(f32[1,3072]{1,0:T(1,128)} %param.18) | copy-start | bytes 36868
  22.1 6.1 %slice-start = ((s8[4718592]{0:T(1024)(128)(4,1)}), s8[4194304]{0:T(1024)(128)(4,1)S(1)}, s32[]{:S(2)}) async-start(s8[4718592]{0:T(1024)(128)(4,1)} %bitcast.140), calls=%async_computation.5 | async-start | bytes 8388608
  23.6 4.7 %slice-start.1 = ((s8[4718592]{0:T(1024)(128)(4,1)}), s8[524288]{0:T(1024)(128)(4,1)S(1)}, s32[]{:S(2)}) async-start(s8[4718592]{0:T(1024)(128)(4,1)} %bitcast.140), calls=%async_computation.6 | async-start | bytes 1048576
  33.1 3.0 %copy-start.2 = (bf16[512,3072]{1,0:T(8,128)(2,1)}, bf16[512,3072]{1,0:T(8,128)(2,1)S(1)}, u32[]{:S(2)}) copy-start(bf16[512,3072]{1,0:T(8,128)(2,1)S(1)} %get-tuple-element.120) | copy-start | bytes 9437188
  33.1 3.0 %copy-start.3 = (bf16[1,1,8,64,768]{4,3,2,1,0:T(8,128)(2,1)S(1)}, bf16[1,1,8,64,768]{4,3,2,1,0:T(8,128)(2,1)}, u32[]{:S(2)}) copy-start(bf16[1,1,8,64,768]{4,3,2,1,0:T(8,128)(2,1)} %param.11) | copy-start | bytes 2359300
  48.0 2.8 %copy-start.8 = (f32[1,768]{1,0:T(1,128)S(1)}, f32[1,768]{1,0:T(1,128)}, u32[]{:S(2)}) copy-start(f32[1,768]{1,0:T(1,128)} %param.20) | copy-start | bytes 9220
  56.9 5.4 %copy-start.1 = (bf16[1,1,8,64,768]{4,3,2,1,0:T(8,128)(2,1)S(1)}, bf16[1,1,8,64,768]{4,3,2,1,0:T(8,128)(2,1)}, u32[]{:S(2)}) copy-start(bf16[1,1,8,64,768]{4,3,2,1,0:T(8,128)(2,1)} %param.12) | copy-start | bytes 2359300
  61.5 127.5 %all-gather.3.cloned.1.call-start = ((), (), s32[]{:S(2)}) async-start(), calls=%async_computation.2 | async-start | bytes 7077888 | tf_op jit(solution)/shard_map/all_gather | solution.py:95
  62.2 174.7 %all-gather.5.cloned.1.call-start = ((), (), s32[]{:S(2)}) async-start(), calls=%async_computation.3 | async-start | bytes 7077888 | tf_op jit(solution)/shard_map/all_gather | solution.py:96
  67.2 43.7 %all-to-all-start = ((bf16[512,8,384]{2,0,1:T(8,128)(2,1)}), bf16[512,8,384]{2,0,1:T(8,128)(2,1)}, u32[]{:S(2)}, u32[]{:S(2)}) async-start(bf16[512,8,384]{2,0,1:T(8,128)(2,1)} %bitcast.133), calls=%async_computation | async-start | bytes 6291456 | tf_op jit(solution)/shard_map/all_to_all | solution.py:92
  111.0 85.4 %all-to-all-start.1 = ((bf16[512,8,384]{2,0,1:T(8,128)(2,1)}), bf16[512,8,384]{2,0,1:T(8,128)(2,1)}, u32[]{:S(2)}, u32[]{:S(2)}) async-start(bf16[512,8,384]{2,0,1:T(8,128)(2,1)} %bitcast.132), calls=%async_computation.1 | async-start | bytes 6291456 | tf_op jit(solution)/shard_map/all_to_all | solution.py:93
  125.1 51.2 %collective-permute-start = (bf16[8,64,768]{2,1,0:T(8,128)(2,1)S(1)}, bf16[8,64,768]{2,1,0:T(8,128)(2,1)S(1)}, u32[]{:S(2)}, u32[]{:S(2)}) collective-permute-start(bf16[8,64,768]{2,1,0:T(8,128)(2,1)S(1)} %fusion.107), channel_id=1, source_target_pairs={{8,0},{16,8},{24,16},{9,1},{17,9},{25,17},{10,2},{18,10},{26,18},{... | collective-permute-start | bytes 2359304 | tf_op jit(solution)/shard_map/ppermute | solution.py:13
Sparse Core Ops, SparseCore 0:
  61.6 76.0 all-reduce.3
  140.2 48.7 all-gather.2
  191.4 45.5 all-gather.4
where the time goes:
time: 253 us
  waiting for transfers between devices  88.7 us (35%)
  blocking collectives  47.5 us (19%)
  other arithmetic  39.6 us (16%)
  matrix products  34.1 us (13%)
  local copies, waits for them, and re-layouts  17.2 us (7%)
  between operations  14.4 us (6%)
  starting transfers between devices  11.1 us (4%)
    psum x1, blocking collectives, shards(): small_sum, b1_sum = lax.psum((small, b1_term), 'dp')  47.5 us
    all_gather x1, waiting for transfers between devices, shards(): lax.all_gather(gproj, 'dp', axis=0, tiled=True)  40.6 us
    all_to_all x1, waiting for transfers between devices, shards(): lax.all_to_all(gpre, 'dp', split_axis=1, concat_axis=0, tiled=True)  34.6 us
    dot_general x2, matrix products, contract_first(): lax.dot_general(left, right, (((0,), (0,)), ((), ())), preferred_element_...  15.5 us
    all_gather x1, waiting for transfers between devices, shards(): lax.all_gather(ynorm, 'dp', axis=0, tiled=True)  12.7 us
    reduce_sum x3, other arithmetic, tap_grads(): pieces.append(jnp.sum(grad * padded[i:i + rows, j:j + cols], axis=(0, 1)))  12.5 us
    dot_general x2, matrix products, contract_last(): lax.dot_general(left, right, (((1,), (1,)), ((), ())), preferred_element_...  10.8 us
    reduce_sum x1, other arithmetic, shards(): centered = depthwise - jnp.mean(depthwise, axis=-1, keepdims=True)  10.3 us
  transfers between devices with their start and end apart: 6, of which 3 were waited for; matrix products, arithmetic and copies ran while one was open for 11% of the time, Pallas kernels for 0%

commit v1 on v0

v1 whole, which is shorter than its diff:
```python
import jax
import jax.numpy as jnp
from jax import lax
from jax.experimental import pallas as pl
from jax.experimental.pallas import tpu as pltpu
from jax.sharding import PartitionSpec as P

root_half = 0.7071067811865476
inv_root_two_pi = 0.3989422804014327
f32 = jnp.float32
bf16 = jnp.bfloat16
LANES = 128
EDGE = 8
VMEM_LIMIT = 48 * 1024 * 1024


def struct(shape, dtype):
    return jax.ShapeDtypeStruct(shape, dtype)


def call(body, out_shape, *args, name, aliases=None, scratch=(), scalars=0, in_specs=None, cost=None):
    vmem = pl.BlockSpec(memory_space=pltpu.VMEM)
    smem = pl.BlockSpec(memory_space=pltpu.SMEM)
    specs = [smem] * scalars + [vmem] * (len(args) - scalars) if in_specs is None else in_specs
    return pl.pallas_call(
        body,
        out_shape=out_shape,
        in_specs=specs,
        out_specs=jax.tree.map(lambda _: vmem, out_shape),
        scratch_shapes=list(scratch),
        input_output_aliases=aliases or {},
        compiler_params=pltpu.CompilerParams(vmem_limit_bytes=VMEM_LIMIT),
        cost_estimate=cost,
        name=name,
    )(*args)


def estimate(flops, nbytes):
    return pl.CostEstimate(flops=int(flops), transcendentals=0, bytes_accessed=int(nbytes))


def dot(a, b):
    return jnp.dot(a, b, preferred_element_type=f32)


def dot_last(a, b):
    return lax.dot_general(a, b, (((1,), (1,)), ((), ())), preferred_element_type=f32)


def expand_taps(w_ref, wexp, blocks):
    for c in range(blocks):
        for k in range(w_ref.shape[0]):
            row = w_ref[k : k + 1, c * LANES : (c + 1) * LANES].astype(f32)
            wexp[c, k] = jnp.broadcast_to(row, (8, LANES))


def zero_edges(buf, blocks, rows, cols):
    zero = jnp.zeros((rows, EDGE, LANES), f32)
    for c in range(blocks):
        buf[c, :, 0:EDGE, :] = zero
        buf[c, :, EDGE + cols : EDGE + cols + EDGE, :] = zero


def conv_block(src, c, wexp, rows, start, width, flip):
    groups = width // 8
    acc = [None] * rows
    for j in range(7):
        at = start + EDGE + (3 - j if flip else j - 3)
        for hp in range(rows):
            piece = src[c, hp, at : at + width, :].reshape(groups, 8, LANES)
            for h in range(max(0, hp - 3), min(rows, hp + 4)):
                i = h - hp + 3 if flip else hp - h + 3
                term = piece * wexp[c, 7 * i + j]
                acc[h] = term if acc[h] is None else acc[h] + term
    return acc


def front_kernel(x_ref, g_ref, w_ref, db_ref, gain_ref, shift_ref, scale_ref,
                 yn_ref, gp_ref, gpt_ref, normed_ref, rstd_ref, xp_ref, sums_ref, wexp):
    rows, cols, chans = x_ref.shape
    blocks = chans // LANES
    half = cols // 2
    zero_edges(xp_ref, blocks, rows, cols)
    for c in range(blocks):
        xp_ref[c, :, EDGE : EDGE + cols, :] = x_ref[:, :, c * LANES : (c + 1) * LANES].astype(f32)
    expand_taps(w_ref, wexp, blocks)

    def conv_step(c, carry):
        lanes = pl.ds(pl.multiple_of(c * LANES, LANES), LANES)
        for part in range(2):
            acc = conv_block(xp_ref, c, wexp, rows, part * half, half, False)
            for h in range(rows):
                normed_ref[h * cols + part * half : h * cols + part * half + half, lanes] = acc[h].reshape(half, LANES)
        return carry

    lax.fori_loop(0, blocks, conv_step, 0)
    bias, gain, shift, scale = db_ref[...], gain_ref[...], shift_ref[...], scale_ref[...]

    def norm_step(r, carry):
        at = pl.ds(pl.multiple_of(r * cols, cols), cols)
        d = normed_ref[at, :] + bias
        d = d - jnp.mean(d, axis=-1, keepdims=True)
        rs = lax.rsqrt(jnp.mean(d * d, axis=-1, keepdims=True) + 1e-06)
        normed = d * rs
        normed_ref[at, :] = normed
        rstd_ref[at, :] = jnp.broadcast_to(rs, (cols, LANES))
        yn_ref[at, :] = (normed * gain + shift).astype(bf16)
        g = g_ref[r].astype(f32)
        gp = (g * scale).astype(bf16)
        gp_ref[at, :] = gp
        b2 = jnp.sum(gp.astype(f32).reshape(cols // 8, 8, chans), axis=0)
        gs = jnp.sum(g.reshape(cols // 8, 8, chans), axis=0)
        return carry[0] + b2, carry[1] + gs

    zero = jnp.zeros((8, chans), f32)
    b2, gs = lax.fori_loop(0, rows, norm_step, (zero, zero))
    sums_ref[0:1, :] = jnp.sum(b2, axis=0, keepdims=True)
    sums_ref[1:2, :] = jnp.sum(gs, axis=0, keepdims=True)
    sums_ref[2:8, :] = jnp.zeros((6, chans), f32)
    gpt_ref[...] = gp_ref[...].T


def wide_kernel(pos_ref, yn_ref, gp_ref, w1_ref, b1_ref, w2_ref, *rest, first):
    if first:
        gn_ref, bsum_ref, kh_ref, kg_ref, sh_ref, sg_ref = rest
        gin_ref = None
    else:
        gin_ref, gn_ref, bsum_ref, kh_ref, kg_ref, sh_ref, sg_ref = rest
    cells = yn_ref.shape[0]
    wide = bsum_ref.shape[1]
    part = wide // 2
    at = pl.multiple_of(pos_ref[0] * wide, wide)
    core = pos_ref[1]
    w1 = w1_ref[pl.ds(at, wide), :]
    w2 = w2_ref[:, pl.ds(at, wide)]
    b1 = b1_ref[:, pl.ds(at, wide)]
    step = 128
    total = jnp.zeros((8, wide), f32)
    for r in range(0, cells, step):
        pre = dot_last(yn_ref[r : r + step, :], w1) + b1
        cdf = 0.5 * (1.0 + lax.erf(pre * root_half))
        hidden = (pre * cdf).astype(bf16)
        ghid = dot(gp_ref[r : r + step, :], w2)
        density = jnp.exp(-0.5 * pre * pre) * inv_root_two_pi
        gpre = (ghid * (cdf + pre * density)).astype(bf16)
        total = total + jnp.sum(gpre.astype(f32).reshape(step // 8, 8, wide), axis=0)
        gn = dot(gpre, w1)
        gn_ref[r : r + step, :] = gn if first else gin_ref[r : r + step, :] + gn
        gt = gpre.T
        for side in range(2):
            @pl.when(core == side)
            def _(side=side):
                k, s = side * part, (1 - side) * part
                kh_ref[r : r + step, :] = hidden[:, k : k + part]
                sh_ref[r : r + step, :] = hidden[:, s : s + part]
                kg_ref[:, r : r + step] = gt[k : k + part, :]
                sg_ref[:, r : r + step] = gt[s : s + part, :]
    bsum_ref[...] = jnp.broadcast_to(jnp.sum(total, axis=0, keepdims=True), (8, wide))


def share_kernel(pos_ref, w2_ref, yo_ref, ys_ref, go_ref, gs_ref, kh_ref, rh_ref, kg_ref, rg_ref,
                 d1_ref, d2_ref, scale_ref):
    part = kh_ref.shape[1]
    at = pl.multiple_of((2 * pos_ref[0] + pos_ref[1]) * part, part)
    d1 = dot(kg_ref[...], yo_ref[...]) + dot(rg_ref[...], ys_ref[...])
    d1_ref[...] = d1.astype(d1_ref.dtype)
    d2 = dot(go_ref[...], kh_ref[...]) + dot(gs_ref[...], rh_ref[...])
    d2_ref[...] = d2.astype(d2_ref.dtype)
    prod = d2 * w2_ref[:, pl.ds(at, part)].astype(f32)
    lanes = prod[:, 0:LANES]
    for k in range(LANES, part, LANES):
        lanes = lanes + prod[:, k : k + LANES]
    scale_ref[...] = lanes


def back_kernel(gn_ref, normed_ref, rstd_ref, gain_ref, g_ref, w_ref, gi_ref, gd_ref, sums_ref, wexp):
    rows, cols, chans = g_ref.shape
    blocks = chans // LANES
    half = cols // 2
    zero_edges(gd_ref, blocks, rows, cols)
    expand_taps(w_ref, wexp, blocks)
    gain = gain_ref[...]

    def norm_step(r, carry):
        at = pl.ds(pl.multiple_of(r * cols, cols), cols)
        gn = gn_ref[at, :]
        normed = normed_ref[at, :]
        prod = gn * normed
        scaled = gn * gain
        mean_a = jnp.mean(scaled, axis=-1, keepdims=True)
        mean_b = jnp.mean(prod * gain, axis=-1, keepdims=True)
        rs = rstd_ref[at, 0:1]
        gd = rs * (scaled - mean_a - normed * mean_b)
        for c in range(blocks):
            gd_ref[c, r, EDGE : EDGE + cols, :] = gd[:, c * LANES : (c + 1) * LANES]
        fold = lambda v: jnp.sum(v.reshape(cols // 8, 8, chans), axis=0)
        return carry[0] + fold(gd), carry[1] + fold(prod), carry[2] + fold(gn)

    zero = jnp.zeros((8, chans), f32)
    sums = lax.fori_loop(0, rows, norm_step, (zero, zero, zero))
    for k in range(3):
        sums_ref[k : k + 1, :] = jnp.sum(sums[k], axis=0, keepdims=True)
    sums_ref[3:8, :] = jnp.zeros((5, chans), f32)

    def conv_step(c, carry):
        lanes = pl.ds(pl.multiple_of(c * LANES, LANES), LANES)
        for part in range(2):
            acc = conv_block(gd_ref, c, wexp, rows, part * half, half, True)
            for h in range(rows):
                span = slice(part * half, part * half + half)
                gi_ref[h, span, lanes] = (g_ref[h, span, lanes].astype(f32) + acc[h].reshape(half, LANES)).astype(bf16)
        return carry

    lax.fori_loop(0, blocks, conv_step, 0)


def tap_kernel(xp_ref, gd_ref, taps_ref):
    blocks, rows, padded, _ = xp_ref.shape
    cols = padded - 2 * EDGE

    def step(c, carry):
        lanes = pl.ds(pl.multiple_of(c * LANES, LANES), LANES)
        for j in range(7):
            acc = [None] * 7
            for b in range(0, cols, 16):
                grads = [gd_ref[c, h, EDGE + b : EDGE + b + 16, :].reshape(2, 8, LANES) for h in range(rows)]
                for hp in range(rows):
                    at = EDGE + b + j - 3
                    piece = xp_ref[c, hp, at : at + 16, :].reshape(2, 8, LANES)
                    for h in range(max(0, hp - 3), min(rows, hp + 4)):
                        i = hp - h + 3
                        term = grads[h] * piece
                        term = term[0] + term[1]
                        acc[i] = term if acc[i] is None else acc[i] + term
            for i in range(7):
                taps_ref[7 * i + j : 7 * i + j + 1, lanes] = jnp.sum(acc[i], axis=0, keepdims=True)
        return carry

    lax.fori_loop(0, blocks, step, 0)


def shifted(block, axis, distance):
    devices = range(lax.axis_size(axis))
    route = [(i - distance, i) for i in devices if i - distance in devices]
    return lax.ppermute(block, axis, route)


def swap(value, bit, count):
    return lax.ppermute(value, "dp", [(i, i ^ bit) for i in range(count)])


def shards(
    block_input,
    grad_output,
    depth_weight,
    depth_bias,
    norm_gain,
    norm_shift,
    pw1_weight,
    pw1_bias,
    pw2_weight,
    pw2_bias,
    layer_scale,
):
    x, g = block_input[0, 0], grad_output[0, 0]
    rows, cols, chans = x.shape
    cells = rows * cols
    blocks = chans // LANES
    taps = depth_weight.shape[1]
    w1, w2 = pw1_weight[0], pw2_weight[0]
    units = w1.shape[0]
    replicas = lax.axis_size("dp")
    factor = 1.0 / replicas
    wide = 768
    part = wide // 2
    me = lax.axis_index("dp")
    chip, core = me // 2, me % 2

    wexp = pltpu.VMEM((blocks, taps, 8, LANES), f32)
    padded = struct((blocks, rows, cols + 2 * EDGE, LANES), f32)
    yn, gp, gpt, normed, rstd, xp, sums_a = call(
        front_kernel,
        (struct((cells, chans), bf16), struct((cells, chans), bf16), struct((chans, cells), bf16),
         struct((cells, chans), f32), struct((cells, LANES), f32), padded, struct((8, chans), f32)),
        x, g, depth_weight[0], depth_bias, norm_gain, norm_shift, layer_scale,
        name="front", scratch=[wexp], cost=estimate(1e10, 5e6),
    )

    def wide_step(p, gn):
        pos = jnp.stack([p, core]).astype(jnp.int32)
        outs = (struct((cells, chans), f32), struct((8, wide), f32), struct((cells, part), bf16),
                struct((part, cells), bf16), struct((cells, part), bf16), struct((part, cells), bf16))
        first = gn is None
        args = (pos, yn, gp, w1, pw1_bias, w2) + (() if first else (gn,))
        return call(
            lambda *refs: wide_kernel(*refs, first=first), outs, *args,
            name="wide", aliases={} if first else {6: 0}, scalars=1, cost=estimate(4e9, 8e6),
        )

    if replicas == 8 and units == 4 * wide:
        yn_s, gpt_s = swap(yn, 1, replicas), swap(gpt, 1, replicas)

        def share(p, kh, kg, rh, rg, types):
            pos = jnp.stack([p, core]).astype(jnp.int32)
            outs = (struct((part, chans), types[0]), struct((chans, part), types[1]), struct((chans, LANES), f32))
            return call(share_kernel, outs, pos, w2, yn, yn_s, gpt, gpt_s, kh, rh, kg, rg,
                        name="share", scalars=1, cost=estimate(2e9, 5e6))

        pd, px, py = chip ^ 3, chip ^ 1, chip ^ 2
        gn, bd, khd, kgd, shd, sgd = wide_step(pd, None)
        rhd, rgd = swap(shd, 1, replicas), swap(sgd, 1, replicas)
        gn, bx, khx, kgx, shx, sgx = wide_step(px, gn)
        rhx, rgx = swap(shx, 1, replicas), swap(sgx, 1, replicas)
        d1, d2, sc_d = share(pd, khd, kgd, rhd, rgd, (bf16, bf16))
        gn, d1, d2 = lax.optimization_barrier((gn, d1, d2))
        d1_in, d2_in = swap(d1, 2, replicas), swap(d2, 4, replicas)
        gn, by, khy, kgy, shy, sgy = wide_step(py, gn)
        rhy, rgy = swap(shy, 1, replicas), swap(sgy, 1, replicas)
        x1, x2, sc_x = share(px, khx, kgx, rhx, rgx, (bf16, f32))
        gn, x1, x2 = lax.optimization_barrier((gn, x1, x2))
        x1_in = swap(x1, 2, replicas)
        gn, bo, kho, kgo, sho, sgo = wide_step(chip, gn)
        rho, rgo = swap(sho, 1, replicas), swap(sgo, 1, replicas)
        y1, y2, sc_y = share(py, khy, kgy, rhy, rgy, (f32, bf16))
        gn, y1, y2 = lax.optimization_barrier((gn, y1, y2))
        y2_in = swap(y2, 4, replicas)
    else:
        gn, bsums, scales, g1, g2 = None, [], [], [], []
        for p in range(units // wide):
            gn, bsum, kh, kg, sh, sg = wide_step(jnp.int32(p), gn)
            lo = lambda k, s: jnp.where(core == 0, k, s)
            hidden = jnp.concatenate([lo(kh, sh), lo(sh, kh)], axis=1)
            gpre_t = jnp.concatenate([lo(kg, sg), lo(sg, kg)], axis=0)
            bsums.append(bsum[0])
            g1.append(dot(gpre_t, yn))
            g2.append(dot(gpt, hidden))
        g1, g2 = jnp.concatenate(g1, axis=0), jnp.concatenate(g2, axis=1)
        scale_sum = jnp.sum(g2 * w2.astype(f32), axis=1)
        b1_sum = jnp.concatenate(bsums)

    gi, gd, sums_b = call(
        back_kernel,
        (struct((rows, cols, chans), bf16), padded, struct((8, chans), f32)),
        gn, normed, rstd, norm_gain, g, depth_weight[0],
        name="back", scratch=[wexp], cost=estimate(1e10, 6e6),
    )
    received = shifted(gi, "section", -1)

    if replicas == 8 and units == 4 * wide:
        o1, o2, sc_o = share(chip, kho, kgo, rho, rgo, (f32, f32))
        scale_sum = jnp.sum(sc_d + sc_x + sc_y + sc_o, axis=1)
        pieces = jnp.stack([bo[0], bx[0], by[0], bd[0]])
        b1_sum = jnp.concatenate([lax.dynamic_slice(pieces, (chip ^ k, 0), (1, wide))[0] for k in range(4)])

    tap_term = call(tap_kernel, struct((taps, chans), f32), xp, gd, name="taps", cost=estimate(1e10, 4e6))
    gscale = scale_sum / layer_scale[0] + pw2_bias[0] * sums_a[1]
    small = jnp.concatenate([tap_term, sums_b[0:3], sums_a[0:1], gscale[None], b1_sum.reshape(-1, chans)], axis=0)

    if replicas == 8 and units == 4 * wide:
        m2 = (x2 + d2_in.astype(f32)).astype(bf16)
        m1 = (y1 + d1_in.astype(f32)).astype(bf16)
        m2_in, m1_in = swap(m2, 2, replicas), swap(m1, 4, replicas)
        for bit in (1, 2, 4):
            small = small + swap(small, bit, replicas)
        out1 = o1 + x1_in.astype(f32) + m1_in.astype(f32)
        out2 = o2 + y2_in.astype(f32) + m2_in.astype(f32)
    else:
        small = lax.psum(small, "dp")
        out1 = lax.psum_scatter(g1, "dp", scatter_dimension=0, tiled=True)
        out2 = lax.psum_scatter(g2, "dp", scatter_dimension=1, tiled=True)
    small = small * factor
    return (
        (out1 * factor)[None],
        (out2 * factor)[None],
        small[taps + 5 :].reshape(1, -1),
        small[None, : taps + 5],
        received[None, None],
    )


def solution(mesh):
    in_specs = (
        P("section", "dp", None, None, None),
        P("section", "dp", None, None, None),
        P("section", None, None),
        P("section", None),
        P("section", None),
        P("section", None),
        P("section", None, None),
        P("section", None),
        P("section", None, None),
        P("section", None),
        P("section", None),
    )
    out_specs = (
        P("section", "dp", None),
        P("section", None, "dp"),
        P("section", None),
        P("section", None, None),
        P("section", "dp", None, None, None),
    )
    return jax.shard_map(shards, mesh=mesh, in_specs=in_specs, out_specs=out_specs, check_vma=False)
```

time: 253 us -> 164 us (0.65)
  Pallas kernels: 0 us -> 76.8 us
  waiting for transfers between devices: 88.7 us -> 31.7 us
  blocking collectives: 47.5 us -> 0 us
  matrix products: 34.1 us -> 0 us
  other arithmetic: 39.6 us -> 7.02 us
  local copies, waits for them, and re-layouts: 17.2 us -> 35.3 us
  between operations: 14.4 us -> 1.08 us
    pallas_call x0 -> x11, Pallas kernels: none -> 76.8 us  [call(): pl.pallas_call(body, out_shape=out_shape, in_specs=specs, out_specs=jax.t...]
    all_gather x2 -> x0, waiting for transfers between devices: 53.3 us -> none  [the longest x1 40.6 us: shards(): lax.all_gather(gproj, 'dp', axis=0, tiled=True)]
    psum x1 -> x0, blocking collectives: 47.5 us -> none  [shards(): small_sum, b1_sum = lax.psum((small, b1_term), 'dp')]
    all_to_all x2 -> x0, waiting for transfers between devices: 34.6 us -> none  [the longest x1 34.6 us: shards(): lax.all_to_all(gpre, 'dp', split_axis=1, concat_axis=0, tiled=True)]
    dot_general x6 -> x0, matrix products: 34.1 us -> none  [the longest x2 15.5 us: contract_first(): lax.dot_general(left, right, (((0,), (0,)), ((), ())), preferred_element_...]
    ppermute x0 -> x19, waiting for transfers between devices: none -> 31.7 us  [swap(): return lax.ppermute(value, 'dp', [(i, i ^ bit) for i in range(count)])]
    unnamed x27 -> x136, local copies, waits for them, and re-layouts: 3.29 us -> 31.1 us
    reduce_sum x7 -> x1, other arithmetic: 24.8 us -> 0.2 us  [shards(): scale_sum = jnp.sum(sc_d + sc_x + sc_y + sc_o, axis=1)]
  transfers between devices with their start and end apart: 6 -> 20, of which waited for: 3 -> 4; matrix products, arithmetic and copies ran while one was open for 11% -> 7% of each run, Pallas kernels for 0% -> 42%
where the time goes in v1:
time: 164 us; the launch traced here: 163 us
  Pallas kernels  76.8 us (47%)
  local copies, waits for them, and re-layouts  35.3 us (22%)
  waiting for transfers between devices  31.7 us (19%)
  starting transfers between devices  11.6 us (7%)
  other arithmetic  7.02 us (4%)
    pallas_call x11, Pallas kernels, call(): pl.pallas_call(body, out_shape=out_shape, in_specs=specs, out_specs=jax.t...  76.8 us
    ppermute x19, waiting for transfers between devices, swap(): return lax.ppermute(value, 'dp', [(i, i ^ bit) for i in range(count)])  31.7 us
    unnamed x136, local copies, waits for them, and re-layouts  31.1 us
    ppermute x19, starting transfers between devices, swap(): return lax.ppermute(value, 'dp', [(i, i ^ bit) for i in range(count)])  10.3 us
  transfers between devices with their start and end apart: 20, of which 4 were waited for; matrix products, arithmetic and copies ran while one was open for 7% of the time, Pallas kernels for 42%

profile of v1, /device:TPU:0, one launch (start us, length us, event | category | flops | bytes accessed | tf_op | source)
XLA Modules:
  0.0 163.4 jit_solution(18083116071189451636)
XLA Ops:
  1.3 1.1 copy-done.25
  2.5 1.1 copy-done.26
  6.5 8.7 %front.1 = (bf16[512,768]{1,0:T(8,128)(2,1)S(1)}, bf16[512,768]{1,0:T(8,128)(2,1)S(1)}, bf16[768,512]{1,0:T(8,128)(2,1)S(1)}, f32[512,768]{1,0:T(8,128)S(1)}, f3...) custom-call(bf16[8,64,768]{2,1,0:T(8,128)(2,1)S(1)} %bitcast.21, ...), custom_call_target="tpu_custom_call" | custom-call | flops 10000000000 | bytes 5000000 | tf_op jit(solution)/shard_map/front/pallas_call | solution.py:25
  16.7 1.2 copy-done.55
  19.8 1.1 copy-done.51
  21.0 8.7 %wide.4 = (f32[512,768]{1,0:T(8,128)S(1)}, f32[8,768]{1,0:T(8,128)S(1)}, bf16[512,384]{1,0:T(8,128)(2,1)S(1)}, bf16[384,512]{1,0:T(8,128)(2,1)S(1)}, bf16[512,384]{1,0:T(8,128)(2,1)}, /*index=5*/bf16[384,512]{1,0:T(8,128)(2,1)}) custom-call(s32[2]{0:T(128)S(1)} %get-tuple-element.129.refs_0_.pos_ref, bf16[512,768]{1,0:T(8,128)(2,1)S(1)} %get-tuple-element.60.refs_1_.yo_ref, ...), custom_call_target="tpu_custom_call" | custom-call | flops 4000000000 | bytes 8000000 | tf_op jit(solution)/shard_map/wide/pallas_call | solution.py:25
  30.8 8.6 %wide.5 = (f32[512,768]{1,0:T(8,128)S(1)}, f32[8,768]{1,0:T(8,128)S(1)}, bf16[512,384]{1,0:T(8,128)(2,1)S(1)}, bf16[384,512]{1,0:T(8,128)(2,1)S(1)}, bf16[512,38...) custom-call(s32[2]{0:T(128)S(1)} %get-tuple-element.128.refs_0_.pos_ref, ...), custom_call_target="tpu_custom_call", output_to_operand_aliasing={{0}: (6, {})} | custom-call | flops 4000000000 | bytes 8000000 | tf_op jit(solution)/shard_map/wide/pallas_call | solution.py:25
  41.5 1.2 copy-done.46
  43.2 1.3 slice.33
  44.5 1.3 slice.31
  48.9 5.4 %share.4 = (bf16[384,768]{1,0:T(8,128)(2,1)}, bf16[768,384]{1,0:T(8,128)(2,1)}, f32[768,128]{1,0:T(8,128)S(1)}) custom-call(s32[2]{0:T(128)S(1)} %get-tuple-element.129.refs_0_.pos_ref, bf16[768,3072]{1,0:T(8,128)(2,1)} %bitcast.28, bf16[512,768]{1,0:T(8,128)(2,1)S(1)} %get-tuple-element.60.refs_1_.yo_ref, bf16[512,768]{1,0:T(8,128)(2,1)S(1)} %collective-permute-done.ys_ref, ...), custom_call_target="tpu_custom_call" | custom-call | flops 2000000000 | bytes 5000000 | tf_op jit(solution)/shard_map/share/pallas_call | solution.py:25
  54.3 2.9 %collective-permute-start.11 = (bf16[384,768]{1,0:T(8,128)(2,1)}, bf16[384,768]{1,0:T(8,128)(2,1)}, u32[]{:S(2)}, u32[]{:S(2)}) collective-permute-start(bf16[384,768]{1,0:T(8,128)(2,1)} %get-tuple-element.94), channel_id=1, source_target_pairs={{0,2},{1,3},{2,0},{3,1},{4,6},{5,7},{6,4},{7,5},{8,10},{9,11},{10,... | collective-permute-start | bytes 1769480 | tf_op jit(solution)/shard_map/ppermute | solution.py:249
  57.2 1.5 collective-permute-start.14
  58.7 9.0 %wide.6 = (f32[512,768]{1,0:T(8,128)S(1)}, f32[8,768]{1,0:T(8,128)S(1)}, bf16[512,384]{1,0:T(8,128)(2,1)S(1)}, bf16[384,512]{1,0:T(8,128)(2,1)S(1)}, bf16[512,384]{1,0:T(8,128)(2,1)}, /*index=5*/bf16[384,512]{1,0:T(8,128)(2,1)}) custom-call(s32[2]{0:T(128)S(1)} %get-tuple-element.127.refs_0_.pos_ref, ...), custom_call_target="tpu_custom_call", output_to_operand_aliasing={{0}: (6, {})} | custom-call | flops 4000000000 | bytes 8000000 | tf_op jit(solution)/shard_map/wide/pallas_call | solution.py:25
  67.8 5.4 %share.5 = (bf16[384,768]{1,0:T(8,128)(2,1)S(1)}, f32[768,384]{1,0:T(8,128)}, f32[768,128]{1,0:T(8,128)S(1)}) custom-call(s32[2]{0:T(128)S(1)} %get-tuple-element.128.refs_0_.pos_ref, bf16[768,3072]{1,0:T(8,128)(2,1)} %bitcast.30, bf16[512,768]{1,0:T(8,128)(2,1)S(1)} %get-tuple-element.60.refs_1_.yo_ref, bf16[512,768]{1,0:T(8,128)(2,1)S(1)} %collective-permute-done.ys_ref, ...), custom_call_target="tpu_custom_call" | custom-call | flops 2000000000 | bytes 5000000 | tf_op jit(solution)/shard_map/share/pallas_call | solution.py:25
  75.3 7.9 %wide.7 = (f32[512,768]{1,0:T(8,128)S(1)}, f32[8,768]{1,0:T(8,128)S(1)}, bf16[512,384]{1,0:T(8,128)(2,1)S(1)}, bf16[384,512]{1,0:T(8,128)(2,1)S(1)}, bf16[512,38...) custom-call(s32[2]{0:T(128)S(1)} %get-tuple-element.126.refs_0_.pos_ref, ...), custom_call_target="tpu_custom_call", output_to_operand_aliasing={{0}: (6, {})} | custom-call | flops 4000000000 | bytes 8000000 | tf_op jit(solution)/shard_map/wide/pallas_call | solution.py:25
  86.2 1.2 copy-done.48
  88.1 1.3 reshape.17
  91.0 4.7 %share.7 = (f32[384,768]{1,0:T(8,128)}, bf16[768,384]{1,0:T(8,128)(2,1)S(1)}, f32[768,128]{1,0:T(8,128)S(1)}) custom-call(s32[2]{0:T(128)S(1)} %get-tuple-element.127.refs_0_.pos_ref, bf16[768,3072]{1,0:T(8,128)(2,1)} %bitcast.32, bf16[512,768]{1,0:T(8,128)(2,1)S(1)} %get-tuple-element.60.refs_1_.yo_ref, bf16[512,768]{1,0:T(8,128)(2,1)S(1)} %collective-permute-done.ys_ref, ...), custom_call_target="tpu_custom_call" | custom-call | flops 2000000000 | bytes 5000000 | tf_op jit(solution)/shard_map/share/pallas_call | solution.py:25
  96.5 7.6 %back.1 = (bf16[8,64,768]{2,1,0:T(8,128)(2,1)S(1)}, f32[6,8,80,128]{3,2,1,0:T(8,128)}, f32[8,768]{1,0:T(8,128)S(1)}) custom-call(f32[512,768]{1,0:T(8,128)S(1)} %copy-done.49, f32[512,768]{1,0:T(8,128)S(1)} %copy-done.56, f32[512,128]{1,0:T(8,128)S(1)} %copy-done.58, f32[1,768]{1,0:T(1,128)S(1)} %copy-done.45, bf16[8,64,768]{2,1,0:T(8,128)(2,1)S(1)} %bitcast.23, ...), custom_call_target="tpu_custom_call" | custom-call | flops 10000000000 | bytes 6000000 | tf_op jit(solution)/shard_map/back/pallas_call | solution.py:25
  105.0 1.5 copy-done.53
  106.6 5.8 %taps.1 = f32[49,768]{1,0:T(8,128)S(1)} custom-call(f32[6,8,80,128]{3,2,1,0:T(8,128)S(1)} %copy-done.54, f32[6,8,80,128]{3,2,1,0:T(8,128)S(1)} %copy-done.53), custom_call_target="tpu_custom_call" | custom-call | flops 10000000000 | bytes 4000000 | tf_op jit(solution)/shard_map/taps/pallas_call | solution.py:25
  112.4 5.0 %share.6 = (f32[384,768]{1,0:T(8,128)}, f32[768,384]{1,0:T(8,128)}, f32[768,128]{1,0:T(8,128)S(1)}) custom-call(s32[2]{0:T(128)S(1)} %get-tuple-element.126.refs_0_.pos_ref, bf16[768,3072]{1,0:T(8,128)(2,1)} %bitcast.33, bf16[512,768]{1,0:T(8,128)(2,1)S(1)} %get-tuple-element.60.refs_1_.yo_ref, bf16[512,768]{1,0:T(8,128)(2,1)S(1)} %collective-permute-done.ys_ref, ...), custom_call_target="tpu_custom_call" | custom-call | flops 2000000000 | bytes 5000000 | tf_op jit(solution)/shard_map/share/pallas_call | solution.py:25
  120.6 1.3 collective-permute-start.19
  122.0 1.3 collective-permute-start.17
  123.3 1.5 add_convert_fusion
  124.8 14.4 %collective-permute-done.17 = f32[58,768]{1,0:T(8,128)S(1)} collective-permute-done((f32[58,768]{1,0:T(8,128)S(1)}, f32[58,768]{1,0:T(8,128)S(1)}, u32[]{:S(2)}, u32[]{:S(2)}) %collective-permute-start.17) | collective-permute-done | bytes 178208 | tf_op jit(solution)/shard_map/ppermute | solution.py:249
  140.1 1.2 add_convert_fusion.1
  141.3 4.7 %collective-permute-done.18 = f32[58,768]{1,0:T(8,128)S(1)} collective-permute-done((f32[58,768]{1,0:T(8,128)S(1)}, f32[58,768]{1,0:T(8,128)S(1)}, u32[]{:S(2)}, u32[]{:S(2)}) %collective-permute-start.18) | collective-permute-done | bytes 178208 | tf_op jit(solution)/shard_map/ppermute | solution.py:249
  147.9 11.8 %collective-permute-done.12 = bf16[384,768]{1,0:T(8,128)(2,1)S(1)} collective-permute-done((bf16[384,768]{1,0:T(8,128)(2,1)S(1)}, bf16[384,768]{1,0:T(8,128)(2,1)S(1)}, u32[]{:S(2)}, u32[]{:S(2)}) %collective-permute-start.12) | collective-permute-done | bytes 589856 | tf_op jit(solution)/shard_map/ppermute | solution.py:249
  159.7 1.2 multiply_bitcast_fusion.1
  161.3 1.2 multiply_bitcast_fusion
  (177 shorter events, 30.2 us)
Async XLA Ops:
  18.5 27.4 %collective-permute-start.1 = (bf16[768,512]{1,0:T(8,128)(2,1)S(1)}, bf16[768,512]{1,0:T(8,128)(2,1)S(1)}, u32[]{:S(2)}, u32[]{:S(2)}) collective-permute-start(bf16[768,512]{1,0:T(8,128)(2,1)S(1)} %get-tuple-element.61.go_ref), channel_id=1, source_target_pairs={{0,1},{1,0},{2,3},{3,2},{4,5},{5,4},{6,7},{7,6},{8,9},{9,8},{10,11... | collective-permute-start | bytes 2359304 | tf_op jit(solution)/shard_map/ppermute | solution.py:249
  19.0 27.0 %collective-permute-start = (bf16[512,768]{1,0:T(8,128)(2,1)S(1)}, bf16[512,768]{1,0:T(8,128)(2,1)S(1)}, u32[]{:S(2)}, u32[]{:S(2)}) collective-permute-start(bf16[512,768]{1,0:T(8,128)(2,1)S(1)} %get-tuple-element.60.refs_1_.yo_ref), channel_id=1, source_target_pairs={{0,1},{1,0},{2,3},{3,2},{4,5},{5,4},{6,7},{7,6},{8,9},{9,8},{10,11... | collective-permute-start | bytes 2359304 | tf_op jit(solution)/shard_map/ppermute | solution.py:249
  21.0 9.8 %copy-start.40 = (f32[1,3072]{1,0:T(1,128)S(1)}, f32[1,3072]{1,0:T(1,128)}, u32[]{:S(2)}) copy-start(f32[1,3072]{1,0:T(1,128)} %refs_4_.7) | copy-start | bytes 36868
  30.3 9.1 %copy-start.12 = (bf16[512,384]{1,0:T(8,128)(2,1)}, bf16[512,384]{1,0:T(8,128)(2,1)S(1)}, u32[]{:S(2)}) copy-start(bf16[512,384]{1,0:T(8,128)(2,1)S(1)} %get-tuple-element.65.kh_ref) | copy-start | bytes 1179652
  30.3 9.1 %copy-start.14 = (bf16[384,512]{1,0:T(8,128)(2,1)}, bf16[384,512]{1,0:T(8,128)(2,1)S(1)}, u32[]{:S(2)}) copy-start(bf16[384,512]{1,0:T(8,128)(2,1)S(1)} %get-tuple-element.67.kg_ref) | copy-start | bytes 1179652
  30.3 15.7 %collective-permute-start.2 = (bf16[512,384]{1,0:T(8,128)(2,1)}, bf16[512,384]{1,0:T(8,128)(2,1)}, u32[]{:S(2)}, u32[]{:S(2)}) collective-permute-start(bf16[512,384]{1,0:T(8,128)(2,1)} %get-tuple-element.66), channel_id=1, source_target_pairs={{0,1},{1,0},{2,3},{3,2},{4,5},{5,4},{6,7},{7,6},{8,9},{9,8},{10,11... | collective-permute-start | bytes 1179656 | tf_op jit(solution)/shard_map/ppermute | solution.py:249
  30.8 15.2 %collective-permute-start.3 = (bf16[384,512]{1,0:T(8,128)(2,1)}, bf16[384,512]{1,0:T(8,128)(2,1)}, u32[]{:S(2)}, u32[]{:S(2)}) collective-permute-start(bf16[384,512]{1,0:T(8,128)(2,1)} %get-tuple-element.68), channel_id=1, source_target_pairs={{0,1},{1,0},{2,3},{3,2},{4,5},{5,4},{6,7},{7,6},{8,9},{9,8},{10,11... | collective-permute-start | bytes 1179656 | tf_op jit(solution)/shard_map/ppermute | solution.py:249
  42.7 25.0 %collective-permute-start.4 = (bf16[512,384]{1,0:T(8,128)(2,1)}, bf16[512,384]{1,0:T(8,128)(2,1)}, u32[]{:S(2)}, u32[]{:S(2)}) collective-permute-start(bf16[512,384]{1,0:T(8,128)(2,1)} %get-tuple-element.74), channel_id=1, source_target_pairs={{0,1},{1,0},{2,3},{3,2},{4,5},{5,4},{6,7},{7,6},{8,9},{9,8},{10,11... | collective-permute-start | bytes 1179656 | tf_op jit(solution)/shard_map/ppermute | solution.py:249
  45.9 21.8 %collective-permute-start.5 = (bf16[384,512]{1,0:T(8,128)(2,1)}, bf16[384,512]{1,0:T(8,128)(2,1)S(1)}, u32[]{:S(2)}, u32[]{:S(2)}) collective-permute-start(bf16[384,512]{1,0:T(8,128)(2,1)} %copy-done.34), channel_id=1, source_target_pairs={{0,1},{1,0},{2,3},{3,2},{4,5},{5,4},{6,7},{7,6},{8,9},{9,8},{10,11... | collective-permute-start | bytes 1179656 | tf_op jit(solution)/shard_map/ppermute | solution.py:249
  48.8 9.9 %copy-start.41 = (f32[1,3072]{1,0:T(1,128)S(1)}, f32[1,3072]{1,0:T(1,128)}, u32[]{:S(2)}) copy-start(f32[1,3072]{1,0:T(1,128)} %refs_4_.7) | copy-start | bytes 36868
  48.8 9.9 %copy-start.47 = (f32[512,768]{1,0:T(8,128)S(1)}, f32[512,768]{1,0:T(8,128)}, u32[]{:S(2)}) copy-start(f32[512,768]{1,0:T(8,128)} %copy-done.46) | copy-start | bytes 4718596
  48.9 9.9 %copy-start.52 = (bf16[512,768]{1,0:T(8,128)(2,1)S(1)}, bf16[512,768]{1,0:T(8,128)(2,1)}, u32[]{:S(2)}) copy-start(bf16[512,768]{1,0:T(8,128)(2,1)} %copy-done.50) | copy-start | bytes 2359300
  54.3 13.5 %copy-start.16 = (f32[768,128]{1,0:T(8,128)}, f32[768,128]{1,0:T(8,128)S(1)}, u32[]{:S(2)}) copy-start(f32[768,128]{1,0:T(8,128)S(1)} %get-tuple-element.106) | copy-start | bytes 1179652
  54.3 85.5 %collective-permute-start.11 = (bf16[384,768]{1,0:T(8,128)(2,1)}, bf16[384,768]{1,0:T(8,128)(2,1)}, u32[]{:S(2)}, u32[]{:S(2)}) collective-permute-start(bf16[384,768]{1,0:T(8,128)(2,1)} %get-tuple-element.94), channel_id=1, source_target_pairs={{0,2},{1,3},{2,0},{3,1},{4,6},{5,7},{6,4},{7,5},{8,10},{9,11},{10,... | collective-permute-start | bytes 1769480 | tf_op jit(solution)/shard_map/ppermute | solution.py:249
  57.2 64.8 %collective-permute-start.14 = (bf16[768,384]{1,0:T(8,128)(2,1)}, bf16[768,384]{1,0:T(8,128)(2,1)}, u32[]{:S(2)}, u32[]{:S(2)}) collective-permute-start(bf16[768,384]{1,0:T(8,128)(2,1)} %get-tuple-element.98), channel_id=1, source_target_pairs={{0,4},{1,5},{2,6},{3,7},{4,0},{5,1},{6,2},{7,3},{8,12},{9,13},{10,... | collective-permute-start | bytes 1769480 | tf_op jit(solution)/shard_map/ppermute | solution.py:249
  74.8 14.6 %collective-permute-start.9 = (bf16[512,384]{1,0:T(8,128)(2,1)}, bf16[512,384]{1,0:T(8,128)(2,1)}, u32[]{:S(2)}, u32[]{:S(2)}) collective-permute-start(bf16[512,384]{1,0:T(8,128)(2,1)} %get-tuple-element.88), channel_id=1, source_target_pairs={{0,1},{1,0},{2,3},{3,2},{4,5},{5,4},{6,7},{7,6},{8,9},{9,8},{10,11... | collective-permute-start | bytes 1179656 | tf_op jit(solution)/shard_map/ppermute | solution.py:249
  74.8 15.1 %collective-permute-start.10 = (bf16[384,512]{1,0:T(8,128)(2,1)}, bf16[384,512]{1,0:T(8,128)(2,1)}, u32[]{:S(2)}, u32[]{:S(2)}) collective-permute-start(bf16[384,512]{1,0:T(8,128)(2,1)} %get-tuple-element.90), channel_id=1, source_target_pairs={{0,1},{1,0},{2,3},{3,2},{4,5},{5,4},{6,7},{7,6},{8,9},{9,8},{10,11... | collective-permute-start | bytes 1179656 | tf_op jit(solution)/shard_map/ppermute | solution.py:249
  75.3 12.1 %copy-start.63 = (f32[1,768]{1,0:T(1,128)S(1)}, f32[1,768]{1,0:T(1,128)}, u32[]{:S(2)}) copy-start(f32[1,768]{1,0:T(1,128)} %slice.33) | copy-start | bytes 9220
  75.3 12.1 %copy-start.64 = (f32[1,768]{1,0:T(1,128)S(1)}, f32[1,768]{1,0:T(1,128)}, u32[]{:S(2)}) copy-start(f32[1,768]{1,0:T(1,128)} %slice.31) | copy-start | bytes 9220
  75.3 14.6 %copy-start.5 = (bf16[512,384]{1,0:T(8,128)(2,1)S(1)}, bf16[512,384]{1,0:T(8,128)(2,1)}, u32[]{:S(2)}) copy-start(bf16[512,384]{1,0:T(8,128)(2,1)} %copy-done.4) | copy-start | bytes 1179652
  89.4 22.9 %collective-permute-start.6 = (bf16[512,384]{1,0:T(8,128)(2,1)}, bf16[512,384]{1,0:T(8,128)(2,1)S(1)}, u32[]{:S(2)}, u32[]{:S(2)}) collective-permute-start(bf16[512,384]{1,0:T(8,128)(2,1)} %copy-done.36), channel_id=1, source_target_pairs={{0,1},{1,0},{2,3},{3,2},{4,5},{5,4},{6,7},{7,6},{8,9},{9,8},{10,11... | collective-permute-start | bytes 1179656 | tf_op jit(solution)/shard_map/ppermute | solution.py:249
  89.4 22.9 %collective-permute-start.7 = (bf16[384,512]{1,0:T(8,128)(2,1)}, bf16[384,512]{1,0:T(8,128)(2,1)S(1)}, u32[]{:S(2)}, u32[]{:S(2)}) collective-permute-start(bf16[384,512]{1,0:T(8,128)(2,1)} %copy-done.35), channel_id=1, source_target_pairs={{0,1},{1,0},{2,3},{3,2},{4,5},{5,4},{6,7},{7,6},{8,9},{9,8},{10,11... | collective-permute-start | bytes 1179656 | tf_op jit(solution)/shard_map/ppermute | solution.py:249
  119.1 1.5 collective-permute-start.16
  119.2 28.7 %collective-permute-start.8 = (bf16[384,768]{1,0:T(8,128)(2,1)S(1)}, bf16[384,768]{1,0:T(8,128)(2,1)S(1)}, u32[]{:S(2)}, u32[]{:S(2)}) collective-permute-start(bf16[384,768]{1,0:T(8,128)(2,1)S(1)} %copy-done.31), channel_id=1, source_target_pairs={{0,2},{1,3},{2,0},{3,1},{4,6},{5,7},{6,4},{7,5},{8,10},{9,11},{10,... | collective-permute-start | bytes 1769480 | tf_op jit(solution)/shard_map/ppermute | solution.py:249
  119.8 41.1 %collective-permute-start.13 = (bf16[768,384]{1,0:T(8,128)(2,1)S(1)}, bf16[768,384]{1,0:T(8,128)(2,1)S(1)}, u32[]{:S(2)}, u32[]{:S(2)}) collective-permute-start(bf16[768,384]{1,0:T(8,128)(2,1)S(1)} %copy-done.33), channel_id=1, source_target_pairs={{0,4},{1,5},{2,6},{3,7},{4,0},{5,1},{6,2},{7,3},{8,12},{9,13},{10,... | collective-permute-start | bytes 1769480 | tf_op jit(solution)/shard_map/ppermute | solution.py:249
  120.6 27.3 %collective-permute-start.19 = (bf16[8,64,768]{2,1,0:T(8,128)(2,1)S(1)}, bf16[8,64,768]{2,1,0:T(8,128)(2,1)S(1)}, u32[]{:S(2)}, u32[]{:S(2)}) collective-permute-start(bf16[8,64,768]{2,1,0:T(8,128)(2,1)S(1)} %copy-done.29), channel_id=1, source_target_pairs={{8,0},{16,8},{24,16},{9,1},{17,9},{25,17},{10,2},{18,10},{26,18},{... | collective-permute-start | bytes 2359304 | tf_op jit(solution)/shard_map/ppermute | solution.py:245
  122.0 18.1 %copy-start.61 = (f32[384,768]{1,0:T(8,128)S(1)}, f32[384,768]{1,0:T(8,128)}, u32[]{:S(2)}) copy-start(f32[384,768]{1,0:T(8,128)} %get-tuple-element.93) | copy-start | bytes 3538948
  122.0 17.2 %collective-permute-start.17 = (f32[58,768]{1,0:T(8,128)S(1)}, f32[58,768]{1,0:T(8,128)S(1)}, u32[]{:S(2)}, u32[]{:S(2)}) collective-permute-start(f32[58,768]{1,0:T(8,128)S(1)} %add.72), channel_id=1, source_target_pairs={{0,2},{1,3},{2,0},{3,1},{4,6},{5,7},{6,4},{7,5},{8,10},{9,11},{10,... | collective-permute-start | bytes 534536 | tf_op jit(solution)/shard_map/ppermute | solution.py:249
  139.2 21.7 %collective-permute-start.15 = (bf16[768,384]{1,0:T(8,128)(2,1)S(1)}, bf16[768,384]{1,0:T(8,128)(2,1)S(1)}, u32[]{:S(2)}, u32[]{:S(2)}) collective-permute-start(bf16[768,384]{1,0:T(8,128)(2,1)S(1)} %add_convert_fusion), channel_id=1, source_target_pairs={{0,2},{1,3},{2,0},{3,1},{4,6},{5,7},{6,4},{7,5},{8,10},{9,11},{10,... | collective-permute-start | bytes 1769480 | tf_op jit(solution)/shard_map/ppermute | solution.py:249
  139.7 6.2 %collective-permute-start.18 = (f32[58,768]{1,0:T(8,128)S(1)}, f32[58,768]{1,0:T(8,128)S(1)}, u32[]{:S(2)}, u32[]{:S(2)}) collective-permute-start(f32[58,768]{1,0:T(8,128)S(1)} %add.73), channel_id=1, source_target_pairs={{0,4},{1,5},{2,6},{3,7},{4,0},{5,1},{6,2},{7,3},{8,12},{9,13},{10,... | collective-permute-start | bytes 534536 | tf_op jit(solution)/shard_map/ppermute | solution.py:249
  141.3 18.4 %copy-start.60 = (f32[384,768]{1,0:T(8,128)S(1)}, f32[384,768]{1,0:T(8,128)}, u32[]{:S(2)}) copy-start(f32[384,768]{1,0:T(8,128)} %get-tuple-element.84) | copy-start | bytes 3538948
  146.0 13.7 %collective-permute-start.12 = (bf16[384,768]{1,0:T(8,128)(2,1)S(1)}, bf16[384,768]{1,0:T(8,128)(2,1)S(1)}, u32[]{:S(2)}, u32[]{:S(2)}) collective-permute-start(bf16[384,768]{1,0:T(8,128)(2,1)S(1)} %add_convert_fusion.1), channel_id=1, source_target_pairs={{0,4},{1,5},{2,6},{3,7},{4,0},{5,1},{6,2},{7,3},{8,12},{9,13},{10,... | collective-permute-start | bytes 1769480 | tf_op jit(solution)/shard_map/ppermute | solution.py:249
  (54 other events, 142.0 us)

commit v2 on v1

v2 whole, which is shorter than its diff:
```python
import jax
import jax.numpy as jnp
from jax import lax
from jax.experimental import pallas as pl
from jax.experimental.pallas import tpu as pltpu
from jax.sharding import PartitionSpec as P

root_half = 0.7071067811865476
inv_root_two_pi = 0.3989422804014327
f32 = jnp.float32
bf16 = jnp.bfloat16
LANES = 128
EDGE = 8
VMEM_LIMIT = 12 * 1024 * 1024


def struct(shape, dtype):
    return jax.ShapeDtypeStruct(shape, dtype)


def call(body, out_shape, *args, name, aliases=None, scratch=(), scalars=0, in_specs=None, cost=None):
    vmem = pl.BlockSpec(memory_space=pltpu.VMEM)
    smem = pl.BlockSpec(memory_space=pltpu.SMEM)
    specs = [smem] * scalars + [vmem] * (len(args) - scalars) if in_specs is None else in_specs
    return pl.pallas_call(
        body,
        out_shape=out_shape,
        in_specs=specs,
        out_specs=jax.tree.map(lambda _: vmem, out_shape),
        scratch_shapes=list(scratch),
        input_output_aliases=aliases or {},
        compiler_params=pltpu.CompilerParams(vmem_limit_bytes=VMEM_LIMIT),
        cost_estimate=cost,
        name=name,
    )(*args)


def estimate(flops, nbytes):
    return pl.CostEstimate(flops=int(flops), transcendentals=0, bytes_accessed=int(nbytes))


def dot(a, b):
    return jnp.dot(a, b, preferred_element_type=f32)


def dot_last(a, b):
    return lax.dot_general(a, b, (((1,), (1,)), ((), ())), preferred_element_type=f32)


def place():
    me = lax.axis_index("dp")
    return lax.shift_right_logical(me, 1), lax.bitwise_and(me, 1)


def expand_taps(w_ref, wexp, blocks):
    for c in range(blocks):
        for k in range(w_ref.shape[0]):
            row = w_ref[k : k + 1, c * LANES : (c + 1) * LANES].astype(f32)
            wexp[c, k] = jnp.broadcast_to(row, (8, LANES))


def zero_edges(buf, blocks, rows, cols):
    zero = jnp.zeros((rows, EDGE, LANES), f32)
    for c in range(blocks):
        buf[c, :, 0:EDGE, :] = zero
        buf[c, :, EDGE + cols : EDGE + cols + EDGE, :] = zero


def conv_block(src, c, wexp, rows, start, width, flip):
    groups = width // 8
    acc = [None] * rows
    for j in range(7):
        at = start + EDGE + (3 - j if flip else j - 3)
        for hp in range(rows):
            piece = src[c, hp, at : at + width, :].reshape(groups, 8, LANES)
            for h in range(max(0, hp - 3), min(rows, hp + 4)):
                i = h - hp + 3 if flip else hp - h + 3
                term = piece * wexp[c, 7 * i + j]
                acc[h] = term if acc[h] is None else acc[h] + term
    return acc


def front_kernel(x_hbm, g_hbm, w_hbm, db_hbm, gain_hbm, shift_hbm, scale_hbm, bb_hbm, w1_hbm, b1_hbm, w2_hbm,
                 acts_ref, normed_ref, rstd_ref, xp_ref, vecs_ref, wexp, g_ref, w1_ref, b1_ref, w2_ref,
                 x_ref, w_ref, tmp_ref, sems):
    rows, cols, chans = x_ref.shape
    blocks = chans // LANES
    half = cols // 2
    moves = [(x_hbm, x_ref), (w_hbm, w_ref), (g_hbm, g_ref), (db_hbm, tmp_ref.at[0:1]), (gain_hbm, tmp_ref.at[1:2]),
             (shift_hbm, tmp_ref.at[2:3]), (scale_hbm, tmp_ref.at[3:4]), (bb_hbm, tmp_ref.at[4:5]),
             (w1_hbm, w1_ref), (b1_hbm, b1_ref), (w2_hbm, w2_ref)]
    copies = [pltpu.make_async_copy(src, dst, sems.at[k]) for k, (src, dst) in enumerate(moves)]
    for copy in copies:
        copy.start()
    zero_edges(xp_ref, blocks, rows, cols)
    copies[0].wait()
    for c in range(blocks):
        xp_ref[c, :, EDGE : EDGE + cols, :] = x_ref[:, :, c * LANES : (c + 1) * LANES].astype(f32)
    copies[1].wait()
    expand_taps(w_ref, wexp, blocks)

    def conv_step(c, carry):
        lanes = pl.ds(pl.multiple_of(c * LANES, LANES), LANES)
        for part in range(2):
            acc = conv_block(xp_ref, c, wexp, rows, part * half, half, False)
            for h in range(rows):
                normed_ref[h * cols + part * half : h * cols + part * half + half, lanes] = acc[h].reshape(half, LANES)
        return carry

    lax.fori_loop(0, blocks, conv_step, 0)
    for copy in copies[2:8]:
        copy.wait()
    bias, gain, shift, scale = (tmp_ref[k : k + 1, :] for k in range(4))

    def norm_step(r, carry):
        at = pl.ds(pl.multiple_of(r * cols, cols), cols)
        d = normed_ref[at, :] + bias
        d = d - jnp.mean(d, axis=-1, keepdims=True)
        rs = lax.rsqrt(jnp.mean(d * d, axis=-1, keepdims=True) + 1e-06)
        normed = d * rs
        normed_ref[at, :] = normed
        rstd_ref[at, :] = jnp.broadcast_to(rs, (cols, LANES))
        acts_ref[at, :] = (normed * gain + shift).astype(bf16)
        g = g_ref[r].astype(f32)
        gp = (g * scale).astype(bf16)
        acts_ref[pl.ds(pl.multiple_of((rows + r) * cols, cols), cols), :] = gp
        b2 = jnp.sum(gp.astype(f32).reshape(cols // 8, 8, chans), axis=0)
        gs = jnp.sum(g.reshape(cols // 8, 8, chans), axis=0)
        return carry[0] + b2, carry[1] + gs

    zero = jnp.zeros((8, chans), f32)
    b2, gs = lax.fori_loop(0, rows, norm_step, (zero, zero))
    vecs_ref[0:1, :] = gain
    vecs_ref[1:2, :] = scale
    vecs_ref[2:3, :] = tmp_ref[4:5, :]
    vecs_ref[3:4, :] = jnp.sum(b2, axis=0, keepdims=True)
    vecs_ref[4:5, :] = jnp.sum(gs, axis=0, keepdims=True)
    vecs_ref[5:8, :] = jnp.zeros((3, chans), f32)
    for copy in copies[8:]:
        copy.wait()


def wide_kernel(acts_ref, w1_ref, b1_ref, w2_ref, *rest, first, slot):
    *gin, gn_ref, bsum_ref, keep_ref, send_ref = rest
    cells = acts_ref.shape[0] // 2
    wide = bsum_ref.shape[1]
    part = wide // 2
    chip, core = place()
    at = pl.multiple_of(slot(chip) * wide, wide)
    w1 = w1_ref[pl.ds(at, wide), :]
    w2 = w2_ref[:, pl.ds(at, wide)]
    b1 = b1_ref[:, pl.ds(at, wide)]
    step = 128
    total = jnp.zeros((8, wide), f32)
    for r in range(0, cells, step):
        pre = dot_last(acts_ref[r : r + step, :], w1) + b1
        cdf = 0.5 * (1.0 + lax.erf(pre * root_half))
        hidden = (pre * cdf).astype(bf16)
        ghid = dot(acts_ref[cells + r : cells + r + step, :], w2)
        density = jnp.exp(-0.5 * pre * pre) * inv_root_two_pi
        gpre = (ghid * (cdf + pre * density)).astype(bf16)
        total = total + jnp.sum(gpre.astype(f32).reshape(step // 8, 8, wide), axis=0)
        gn = dot(gpre, w1)
        gn_ref[r : r + step, :] = gn if first else gin[0][r : r + step, :] + gn
        gt, ht = gpre.T, hidden.T
        for side in range(2):
            @pl.when(core == side)
            def _(side=side):
                k, s = side * part, (1 - side) * part
                keep_ref[0:part, r : r + step] = gt[k : k + part, :]
                send_ref[0:part, r : r + step] = gt[s : s + part, :]
                keep_ref[part:, r : r + step] = ht[k : k + part, :]
                send_ref[part:, r : r + step] = ht[s : s + part, :]
    bsum_ref[...] = jnp.broadcast_to(jnp.sum(total, axis=0, keepdims=True), (8, wide))


def share_kernel(w2_ref, own_ref, sib_ref, keep_ref, got_ref, *rest, slot, mode):
    part = keep_ref.shape[0] // 2
    cells = own_ref.shape[0] // 2
    chip, core = place()
    at = pl.multiple_of((2 * slot(chip) + core) * part, part)
    d1 = dot(keep_ref[0:part, :], own_ref[0:cells, :]) + dot(got_ref[0:part, :], sib_ref[0:cells, :])
    d2 = dot(keep_ref[part:, :], own_ref[cells:, :]) + dot(got_ref[part:, :], sib_ref[cells:, :])
    prod = d2 * w2_ref[:, pl.ds(at, part)].T.astype(f32)
    if mode == "split":
        d1_ref, d2_ref, scale_ref = rest
        d1_ref[...] = d1.astype(d1_ref.dtype)
        d2_ref[...] = d2.astype(d2_ref.dtype)
    else:
        in_ref, pack_ref, scale_ref = rest
        more = in_ref[...].astype(f32)
        if mode == "first":
            d1 = d1 + more
        else:
            d2 = d2 + more
        pack_ref[0:part, :] = d1.astype(bf16)
        pack_ref[part:, :] = d2.astype(bf16)
    scale_ref[...] = jnp.sum(prod.reshape(part // 8, 8, prod.shape[1]), axis=0)


def back_kernel(gn_ref, normed_ref, rstd_ref, vecs_ref, g_ref, wexp, gi_ref, gd_ref, sums_ref):
    rows, cols, chans = g_ref.shape
    blocks = chans // LANES
    half = cols // 2
    zero_edges(gd_ref, blocks, rows, cols)
    gain = vecs_ref[0:1, :]

    def norm_step(r, carry):
        at = pl.ds(pl.multiple_of(r * cols, cols), cols)
        gn = gn_ref[at, :]
        normed = normed_ref[at, :]
        prod = gn * normed
        scaled = gn * gain
        mean_a = jnp.mean(scaled, axis=-1, keepdims=True)
        mean_b = jnp.mean(prod * gain, axis=-1, keepdims=True)
        rs = rstd_ref[at, 0:1]
        gd = rs * (scaled - mean_a - normed * mean_b)
        for c in range(blocks):
            gd_ref[c, r, EDGE : EDGE + cols, :] = gd[:, c * LANES : (c + 1) * LANES]
        fold = lambda v: jnp.sum(v.reshape(cols // 8, 8, chans), axis=0)
        return carry[0] + fold(gd), carry[1] + fold(prod), carry[2] + fold(gn)

    zero = jnp.zeros((8, chans), f32)
    sums = lax.fori_loop(0, rows, norm_step, (zero, zero, zero))
    for k in range(3):
        sums_ref[k : k + 1, :] = jnp.sum(sums[k], axis=0, keepdims=True)
    sums_ref[3:8, :] = jnp.zeros((5, chans), f32)

    def conv_step(c, carry):
        lanes = pl.ds(pl.multiple_of(c * LANES, LANES), LANES)
        for part in range(2):
            acc = conv_block(gd_ref, c, wexp, rows, part * half, half, True)
            for h in range(rows):
                span = slice(part * half, part * half + half)
                gi_ref[h, span, lanes] = (g_ref[h, span, lanes].astype(f32) + acc[h].reshape(half, LANES)).astype(bf16)
        return carry

    lax.fori_loop(0, blocks, conv_step, 0)


def tap_kernel(xp_ref, gd_ref, vecs_ref, sums_ref, *rest, taps, fast):
    *more, small_ref = rest
    blocks, rows, padded, _ = xp_ref.shape
    cols = padded - 2 * EDGE
    chans = blocks * LANES

    def step(c, carry):
        lanes = pl.ds(pl.multiple_of(c * LANES, LANES), LANES)
        for j in range(7):
            acc = [None] * 7
            for b in range(0, cols, 16):
                grads = [gd_ref[c, h, EDGE + b : EDGE + b + 16, :].reshape(2, 8, LANES) for h in range(rows)]
                for hp in range(rows):
                    at = EDGE + b + j - 3
                    piece = xp_ref[c, hp, at : at + 16, :].reshape(2, 8, LANES)
                    for h in range(max(0, hp - 3), min(rows, hp + 4)):
                        i = hp - h + 3
                        term = grads[h] * piece
                        term = term[0] + term[1]
                        acc[i] = term if acc[i] is None else acc[i] + term
            for i in range(7):
                small_ref[7 * i + j : 7 * i + j + 1, lanes] = jnp.sum(acc[i], axis=0, keepdims=True)
        return carry

    small_ref[taps:, :] = jnp.zeros((small_ref.shape[0] - taps, chans), f32)
    lax.fori_loop(0, blocks, step, 0)
    small_ref[taps : taps + 3, :] = sums_ref[0:3, :]
    small_ref[taps + 3 : taps + 4, :] = vecs_ref[3:4, :]
    if fast:
        scales, bsums = more[:4], more[4:]
        total = scales[0][...] + scales[1][...] + scales[2][...] + scales[3][...]
        row = jnp.sum(total, axis=0, keepdims=True) / vecs_ref[1:2, :] + vecs_ref[2:3, :] * vecs_ref[4:5, :]
        small_ref[taps + 4 : taps + 5, :] = row
        chip, _ = place()
        for k in range(4):
            small_ref[pl.ds(taps + 5 + lax.bitwise_xor(chip, k), 1), :] = bsums[k][0:1, :]


def merge_kernel(o1_ref, o2_ref, x_ref, y_ref, out1_ref, out2_ref, *, factor):
    part = o1_ref.shape[0]
    out1_ref[...] = (o1_ref[...] + x_ref[0:part, :].astype(f32) + y_ref[0:part, :].astype(f32)) * factor
    out2_ref[...] = ((o2_ref[...] + x_ref[part:, :].astype(f32) + y_ref[part:, :].astype(f32)) * factor).T


def shifted(block, axis, distance):
    devices = range(lax.axis_size(axis))
    route = [(i - distance, i) for i in devices if i - distance in devices]
    return lax.ppermute(block, axis, route)


def swap(value, bit, count):
    return lax.ppermute(value, "dp", [(i, i ^ bit) for i in range(count)])


def shards(
    block_input,
    grad_output,
    depth_weight,
    depth_bias,
    norm_gain,
    norm_shift,
    pw1_weight,
    pw1_bias,
    pw2_weight,
    pw2_bias,
    layer_scale,
):
    x, g = block_input[0, 0], grad_output[0, 0]
    rows, cols, chans = x.shape
    cells = rows * cols
    blocks = chans // LANES
    taps = depth_weight.shape[1]
    w1, w2 = pw1_weight[0], pw2_weight[0]
    units = w1.shape[0]
    replicas = lax.axis_size("dp")
    factor = 1.0 / replicas
    wide = 768
    part = wide // 2
    fast = replicas == 8 and units == 4 * wide

    wexp = struct((blocks, taps, 8, LANES), f32)
    padded = struct((blocks, rows, cols + 2 * EDGE, LANES), f32)
    like = lambda v: struct(v.shape, v.dtype)
    hbm = pl.BlockSpec(memory_space=pltpu.HBM)
    front_args = (x, g, depth_weight[0], depth_bias, norm_gain, norm_shift, layer_scale, pw2_bias, w1, pw1_bias, w2)
    acts, normed, rstd, xp, vecs, wexp, gv, w1, b1, w2 = call(
        front_kernel,
        (struct((2 * cells, chans), bf16), struct((cells, chans), f32), struct((cells, LANES), f32), padded, struct((8, chans), f32), wexp,
         like(g), like(w1), like(pw1_bias), like(w2)),
        *(pltpu.with_memory_space_constraint(v, pltpu.HBM) for v in front_args),
        name="front", in_specs=[hbm] * 11, cost=estimate(1e10, 1e6),
        scratch=[pltpu.VMEM(x.shape, bf16), pltpu.VMEM((taps, chans), bf16), pltpu.VMEM((8, chans), f32),
                 pltpu.SemaphoreType.DMA((11,))],
    )

    def wide_step(slot, gn):
        outs = (struct((cells, chans), f32), struct((8, wide), f32), struct((wide, cells), bf16),
                struct((wide, cells), bf16))
        first = gn is None
        args = (acts, w1, b1, w2) + (() if first else (gn,))
        return call(
            lambda *refs: wide_kernel(*refs, first=first, slot=slot), outs, *args,
            name="wide", aliases={} if first else {4: 0}, cost=estimate(1e10, 1e6),
        )

    def flip(k):
        return lambda chip: lax.bitwise_xor(chip, k)

    if fast:
        acts_s = swap(acts, 1, replicas)

        def share(k, keep, got, types):
            outs = (struct((part, chans), types), struct((part, chans), types), struct((8, chans), f32))
            return call(lambda *refs: share_kernel(*refs, slot=flip(k), mode="split"), outs,
                        w2, acts, acts_s, keep, got, name="share", cost=estimate(1e6, 1e3))

        def share_pack(k, keep, got, more, mode):
            outs = (struct((wide, chans), bf16), struct((8, chans), f32))
            return call(lambda *refs: share_kernel(*refs, slot=flip(k), mode=mode), outs,
                        w2, acts, acts_s, keep, got, more, name="pack", cost=estimate(1e10, 1e6))

        gn, bd, keep_d, send_d = wide_step(flip(3), None)
        got_d = swap(send_d, 1, replicas)
        gn, bx, keep_x, send_x = wide_step(flip(1), gn)
        got_x = swap(send_x, 1, replicas)
        d1, d2, sc_d = share(3, keep_d, got_d, bf16)
        gn, d1, d2 = lax.optimization_barrier((gn, d1, d2))
        d1_in, d2_in = swap(d1, 2, replicas), swap(d2, 4, replicas)
        gn, by, keep_y, send_y = wide_step(flip(2), gn)
        got_y = swap(send_y, 1, replicas)
        gn, bo, keep_o, send_o = wide_step(flip(0), gn)
        got_o = swap(send_o, 1, replicas)
        pack_x, sc_x = share_pack(1, keep_x, got_x, d2_in, "second")
        gn, pack_x, d1_in = lax.optimization_barrier((gn, pack_x, d1_in))
        pack_y, sc_y = share_pack(2, keep_y, got_y, d1_in, "first")
        gn, pack_y = lax.optimization_barrier((gn, pack_y))
        x_in, y_in = swap(pack_x, 2, replicas), swap(pack_y, 4, replicas)
    else:
        core = lax.axis_index("dp") % 2
        gn, bsums, g1, g2 = None, [], [], []
        for p in range(units // wide):
            gn, bsum, keep, send = wide_step(lambda chip, p=p: jnp.int32(p), gn)
            lo, hi = jnp.where(core == 0, keep, send), jnp.where(core == 0, send, keep)
            bsums.append(bsum[0:1])
            g1 += [dot(v[:part], acts[:cells]) for v in (lo, hi)]
            g2 += [dot(v[part:], acts[cells:]) for v in (lo, hi)]
        g1, g2 = jnp.concatenate(g1, axis=0), jnp.concatenate(g2, axis=0).T

    gi, gd, sums = call(
        back_kernel,
        (struct((rows, cols, chans), bf16), padded, struct((8, chans), f32)),
        gn, normed, rstd, vecs, gv, wexp,
        name="back", cost=estimate(1e6, 1e3),
    )
    received = shifted(gi, "section", -1)

    if fast:
        o1, o2, sc_o = share(0, keep_o, got_o, f32)
        more = (sc_d, sc_x, sc_y, sc_o, bo, bx, by, bd)
    else:
        more = ()
    total_rows = -(-(taps + 5 + units // chans) // 8) * 8
    small = call(lambda *refs: tap_kernel(*refs, taps=taps, fast=fast), struct((total_rows, chans), f32),
                 xp, gd, vecs, sums, *more, name="taps", cost=estimate(1e6, 1e3))

    if fast:
        for bit in (1, 2, 4):
            small = small + swap(small, bit, replicas)
        out1, out2 = call(
            lambda *refs: merge_kernel(*refs, factor=factor),
            (struct((part, chans), f32), struct((chans, part), f32)),
            o1, o2, x_in, y_in, name="merge", cost=estimate(1e10, 1e6),
        )
    else:
        scale_sum = jnp.sum(g2 * w2.astype(f32), axis=1)
        gscale = scale_sum / layer_scale[0] + pw2_bias[0] * vecs[4]
        small = jnp.concatenate([small[: taps + 4], gscale[None], *bsums], axis=0)
        small = lax.psum(small, "dp")
        out1 = lax.psum_scatter(g1, "dp", scatter_dimension=0, tiled=True) * factor
        out2 = lax.psum_scatter(g2, "dp", scatter_dimension=1, tiled=True) * factor
    small = small * factor
    return (
        out1[None],
        out2[None],
        small[taps + 5 : taps + 5 + units // chans].reshape(1, -1),
        small[None, : taps + 5],
        received[None, None],
    )


def solution(mesh):
    in_specs = (
        P("section", "dp", None, None, None),
        P("section", "dp", None, None, None),
        P("section", None, None),
        P("section", None),
        P("section", None),
        P("section", None),
        P("section", None, None),
        P("section", None),
        P("section", None, None),
        P("section", None),
        P("section", None),
    )
    out_specs = (
        P("section", "dp", None),
        P("section", None, "dp"),
        P("section", None),
        P("section", None, None),
        P("section", "dp", None, None, None),
    )
    return jax.shard_map(shards, mesh=mesh, in_specs=in_specs, out_specs=out_specs, check_vma=False)
```

time: 164 us -> 112 us (0.68)
  local copies, waits for them, and re-layouts: 35.3 us -> 2.35 us
  Pallas kernels: 76.8 us -> 45.5 us
  waiting for transfers between devices: 31.7 us -> 50 us
  other arithmetic: 7.02 us -> 0.08 us
    pallas_call x11 -> x12, Pallas kernels: 76.8 us -> 45.5 us  [call(): pl.pallas_call(body, out_shape=out_shape, in_specs=specs, out_specs=jax.t...]
    unnamed x136 -> x4, local copies, waits for them, and re-layouts: 31.1 us -> 2.34 us
    ppermute x1, waiting for transfers between devices: 0.01 us -> 14.5 us  [shifted(): return lax.ppermute(block, axis, route)]
    ppermute x19 -> x12, waiting for transfers between devices: 31.7 us -> 35.6 us  [swap(): return lax.ppermute(value, 'dp', [(i, i ^ bit) for i in range(count)])]
    convert_element_type x2 -> x0, other arithmetic: 2.71 us -> none  [the longest x1 1.53 us: shards(): m2 = (x2 + d2_in.astype(f32)).astype(bf16)]
    slice x5 -> x0, local copies, waits for them, and re-layouts: 2.66 us -> none  [the longest x4 2.65 us: shards(): pieces = jnp.stack([bo[0], bx[0], by[0], bd[0]])]
    broadcast_in_dim x2 -> x0, other arithmetic: 2.43 us -> none  [the longest x1 1.22 us: shards(): (out2 * factor)[None]]
    ppermute x19 -> x12, starting transfers between devices: 10.3 us -> 11.6 us  [swap(): return lax.ppermute(value, 'dp', [(i, i ^ bit) for i in range(count)])]
  transfers between devices with their start and end apart: 20 -> 13, of which waited for: 4 -> 4; matrix products, arithmetic and copies ran while one was open for 7% -> 1% of each run, Pallas kernels for 42% -> 25%
where the time goes in v2:
time: 112 us
  waiting for transfers between devices  50 us (45%)
  Pallas kernels  45.5 us (41%)
  starting transfers between devices  12.9 us (12%)
  local copies, waits for them, and re-layouts  2.35 us (2%)
    pallas_call x12, Pallas kernels, call(): pl.pallas_call(body, out_shape=out_shape, in_specs=specs, out_specs=jax.t...  45.5 us
    ppermute x12, waiting for transfers between devices, swap(): return lax.ppermute(value, 'dp', [(i, i ^ bit) for i in range(count)])  35.6 us
    ppermute x1, waiting for transfers between devices, shifted(): return lax.ppermute(block, axis, route)  14.5 us
    ppermute x12, starting transfers between devices, swap(): return lax.ppermute(value, 'dp', [(i, i ^ bit) for i in range(count)])  11.6 us
    unnamed x4, local copies, waits for them, and re-layouts  2.34 us
  transfers between devices with their start and end apart: 13, of which 4 were waited for; matrix products, arithmetic and copies ran while one was open for 1% of the time, Pallas kernels for 25%

profile of v2, /device:TPU:0, one launch (start us, length us, event | category | flops | bytes accessed | tf_op | source)
XLA Modules:
  0.0 111.7 jit_solution(17495450586108165794)
XLA Ops:
  0.6 8.4 %front.1 = (bf16[1024,768]{1,0:T(8,128)(2,1)S(1)}, f32[512,768]{1,0:T(8,128)S(1)}, f32[512,128]{1,0:T(8,128)S(1)}, f32[6,8,80,128]{3,2,1,0:T(8,128)S(1)}, f32[8,...) custom-call(bf16[8,64,768]{2,1,0:T(8,128)(2,1)} %bitcast.18, ...), custom_call_target="tpu_custom_call" | custom-call | flops 10000000000 | bytes 1000000 | tf_op jit(solution)/shard_map/front/pallas_call | solution.py:25
  9.1 0.5 collective-permute-start
  9.6 4.1 %wide.4 = (f32[512,768]{1,0:T(8,128)S(1)}, f32[8,768]{1,0:T(8,128)S(1)}, bf16[768,512]{1,0:T(8,128)(2,1)S(1)}, bf16[768,512]{1,0:T(8,128)(2,1)S(1)}) custom-call(bf16[1024,768]{1,0:T(8,128)(2,1)S(1)} %get-tuple-element.55.refs_0_.refs_1_, bf16[3072,768]{1,0:T(8,128)(2,1)S(1)} %get-tuple-element.56.refs_1_, f32[1,3072]{1,0:T(1,128)S(1)} %get-tuple-element.57.refs_2_, ...), custom_call_target="tpu_custom_call" | custom-call | flops 10000000000 | bytes 1000000 | tf_op jit(solution)/shard_map/wide/pallas_call | solution.py:25
  13.7 0.2 collective-permute-start.1
  13.9 4.1 %wide.5 = (f32[512,768]{1,0:T(8,128)S(1)}, f32[8,768]{1,0:T(8,128)S(1)}, bf16[768,512]{1,0:T(8,128)(2,1)S(1)}, bf16[768,512]{1,0:T(8,128)(2,1)S(1)}) custom-call(bf16[1024,768]{1,0:T(8,128)(2,1)S(1)} %get-tuple-element.55.refs_0_.refs_1_, bf16[3072,768]{1,0:T(8,128)(2,1)S(1)} %get-tuple-element.56.refs_1_, ...), custom_call_target="tpu_custom_call", output_to_operand_aliasing={{0}: (4, {})} | custom-call | flops 10000000000 | bytes 1000000 | tf_op jit(solution)/shard_map/wide/pallas_call | solution.py:25
  18.0 0.5 collective-permute-start.3
  18.5 1.4 %share.2 = (bf16[384,768]{1,0:T(8,128)(2,1)S(1)}, bf16[384,768]{1,0:T(8,128)(2,1)S(1)}, f32[8,768]{1,0:T(8,128)S(1)}) custom-call(bf16[768,3072]{1,0:T(8,128)(2,1)S(1)} %get-tuple-element.54.refs_3_.refs_0_, bf16[1024,768]{1,0:T(8,128)(2,1)S(1)} %get-tuple-element.55.refs_0_.refs_1_, bf16[1024,768]{1,0:T(8,128)(2,1)S(1)} %collective-permute-done.refs_2_, ...), custom_call_target="tpu_custom_call" | custom-call | flops 1000000 | bytes 1000 | tf_op jit(solution)/shard_map/share/pallas_call | solution.py:25
  19.9 2.6 %collective-permute-start.4 = (bf16[384,768]{1,0:T(8,128)(2,1)S(1)}, bf16[384,768]{1,0:T(8,128)(2,1)S(1)}, u32[]{:S(2)}, u32[]{:S(2)}) collective-permute-start(bf16[384,768]{1,0:T(8,128)(2,1)S(1)} %get-tuple-element.73), channel_id=1, source_target_pairs={{0,4},{1,5},{2,6},{3,7},{4,0},{5,1},{6,2},{7,3},{8,12},{9,13},{10,... | collective-permute-start | bytes 1769480 | tf_op jit(solution)/shard_map/ppermute | solution.py:292
  22.5 1.5 %collective-permute-start.5 = (bf16[384,768]{1,0:T(8,128)(2,1)S(1)}, bf16[384,768]{1,0:T(8,128)(2,1)S(1)}, u32[]{:S(2)}, u32[]{:S(2)}) collective-permute-start(bf16[384,768]{1,0:T(8,128)(2,1)S(1)} %get-tuple-element.75), channel_id=1, source_target_pairs={{0,2},{1,3},{2,0},{3,1},{4,6},{5,7},{6,4},{7,5},{8,10},{9,11},{10,... | collective-permute-start | bytes 1769480 | tf_op jit(solution)/shard_map/ppermute | solution.py:292
  24.0 4.3 %wide.6 = (f32[512,768]{1,0:T(8,128)S(1)}, f32[8,768]{1,0:T(8,128)S(1)}, bf16[768,512]{1,0:T(8,128)(2,1)S(1)}, bf16[768,512]{1,0:T(8,128)(2,1)S(1)}) custom-call(bf16[1024,768]{1,0:T(8,128)(2,1)S(1)} %get-tuple-element.55.refs_0_.refs_1_, bf16[3072,768]{1,0:T(8,128)(2,1)S(1)} %get-tuple-element.56.refs_1_, ...), custom_call_target="tpu_custom_call", output_to_operand_aliasing={{0}: (4, {})} | custom-call | flops 10000000000 | bytes 1000000 | tf_op jit(solution)/shard_map/wide/pallas_call | solution.py:25
  28.4 4.1 %wide.7 = (f32[512,768]{1,0:T(8,128)S(1)}, f32[8,768]{1,0:T(8,128)S(1)}, bf16[768,512]{1,0:T(8,128)(2,1)S(1)}, bf16[768,512]{1,0:T(8,128)(2,1)S(1)}) custom-call(bf16[1024,768]{1,0:T(8,128)(2,1)S(1)} %get-tuple-element.55.refs_0_.refs_1_, bf16[3072,768]{1,0:T(8,128)(2,1)S(1)} %get-tuple-element.56.refs_1_, ...), custom_call_target="tpu_custom_call", output_to_operand_aliasing={{0}: (4, {})} | custom-call | flops 10000000000 | bytes 1000000 | tf_op jit(solution)/shard_map/wide/pallas_call | solution.py:25
  32.5 0.1 collective-permute-start.2
  32.6 0.5 collective-permute-start.7
  33.1 3.4 %collective-permute-done.4.refs_5_ = bf16[384,768]{1,0:T(8,128)(2,1)S(1)} collective-permute-done((bf16[384,768]{1,0:T(8,128)(2,1)S(1)}, bf16[384,768]{1,0:T(8,128)(2,1)S(1)}, u32[]{:S(2)}, u32[]{:S(2)}) %collective-permute-start.4) | collective-permute-done | bytes 589856 | tf_op jit(solution)/shard_map/ppermute | solution.py:292
  36.5 1.4 %pack.2 = (bf16[768,768]{1,0:T(8,128)(2,1)S(1)}, f32[8,768]{1,0:T(8,128)S(1)}) custom-call(bf16[768,3072]{1,0:T(8,128)(2,1)S(1)} %get-tuple-element.54.refs_3_.refs_0_, bf16[1024,768]{1,0:T(8,128)(2,1)S(1)} %get-tuple-element.55.refs_0_.refs_1_, bf16[1024,768]{1,0:T(8,128)(2,1)S(1)} %collective-permute-done.refs_2_, ...), custom_call_target="tpu_custom_call" | custom-call | flops 10000000000 | bytes 1000000 | tf_op jit(solution)/shard_map/pack/pallas_call | solution.py:25
  38.0 1.4 %pack.3 = (bf16[768,768]{1,0:T(8,128)(2,1)S(1)}, f32[8,768]{1,0:T(8,128)S(1)}) custom-call(bf16[768,3072]{1,0:T(8,128)(2,1)S(1)} %get-tuple-element.54.refs_3_.refs_0_, bf16[1024,768]{1,0:T(8,128)(2,1)S(1)} %get-tuple-element.55.refs_0_.refs_1_, bf16[1024,768]{1,0:T(8,128)(2,1)S(1)} %collective-permute-done.refs_2_, ...), custom_call_target="tpu_custom_call" | custom-call | flops 10000000000 | bytes 1000000 | tf_op jit(solution)/shard_map/pack/pallas_call | solution.py:25
  39.4 7.1 %back.1 = (bf16[8,64,768]{2,1,0:T(8,128)(2,1)S(1)}, f32[6,8,80,128]{3,2,1,0:T(8,128)S(1)}, f32[8,768]{1,0:T(8,128)S(1)}) custom-call(f32[512,768]{1,0:T(8,128)S(1)} %get-tuple-element.86.gn_ref, f32[512,768]{1,0:T(8,128)S(1)} %get-tuple-element.87.normed_ref, f32[512,128]{1,0:T(8,128)S(1)} %get-tuple-element.88.rstd_ref, ...), custom_call_target="tpu_custom_call" | custom-call | flops 1000000 | bytes 1000 | tf_op jit(solution)/shard_map/back/pallas_call | solution.py:25
  46.4 1.4 %share.3 = (f32[384,768]{1,0:T(8,128)S(1)}, f32[384,768]{1,0:T(8,128)S(1)}, f32[8,768]{1,0:T(8,128)S(1)}) custom-call(bf16[768,3072]{1,0:T(8,128)(2,1)S(1)} %get-tuple-element.54.refs_3_.refs_0_, bf16[1024,768]{1,0:T(8,128)(2,1)S(1)} %get-tuple-element.55.refs_0_.refs_1_, bf16[1024,768]{1,0:T(8,128)(2,1)S(1)} %collective-permute-done.refs_2_, ...), custom_call_target="tpu_custom_call" | custom-call | flops 1000000 | bytes 1000 | tf_op jit(solution)/shard_map/share/pallas_call | solution.py:25
  47.8 5.8 %taps.1 = f32[64,768]{1,0:T(8,128)S(1)} custom-call(f32[6,8,80,128]{3,2,1,0:T(8,128)S(1)} %get-tuple-element.85.refs_0_, f32[6,8,80,128]{3,2,1,0:T(8,128)S(1)} %get-tuple-element.92.refs_1_, f32[8,768]{1,0:T(8,128)S(1)} %get-tuple-element.89.vecs_ref.refs_2_, f32[8,768]{1,0:T(8,128)S(1)} %get-tuple-element.93.refs_3_, ...), custom_call_target="tpu_custom_call" | custom-call | flops 1000000 | bytes 1000 | tf_op jit(solution)/shard_map/taps/pallas_call | solution.py:25
  53.6 0.1 collective-permute-start.9
  53.7 1.8 %collective-permute-start.6 = (bf16[768,768]{1,0:T(8,128)(2,1)S(1)}, bf16[768,768]{1,0:T(8,128)(2,1)S(1)}, u32[]{:S(2)}, u32[]{:S(2)}) collective-permute-start(bf16[768,768]{1,0:T(8,128)(2,1)S(1)} %get-tuple-element.76), channel_id=1, source_target_pairs={{0,2},{1,3},{2,0},{3,1},{4,6},{5,7},{6,4},{7,5},{8,10},{9,11},{10,... | collective-permute-start | bytes 3538952 | tf_op jit(solution)/shard_map/ppermute | solution.py:292
  55.5 1.5 %collective-permute-start.8 = (bf16[768,768]{1,0:T(8,128)(2,1)S(1)}, bf16[768,768]{1,0:T(8,128)(2,1)S(1)}, u32[]{:S(2)}, u32[]{:S(2)}) collective-permute-start(bf16[768,768]{1,0:T(8,128)(2,1)S(1)} %get-tuple-element.82), channel_id=1, source_target_pairs={{0,4},{1,5},{2,6},{3,7},{4,0},{5,1},{6,2},{7,3},{8,12},{9,13},{10,... | collective-permute-start | bytes 3538952 | tf_op jit(solution)/shard_map/ppermute | solution.py:292
  57.1 0.6 collective-permute-start.10
  57.6 28.7 %collective-permute-done.10 = f32[64,768]{1,0:T(8,128)S(1)} collective-permute-done((f32[64,768]{1,0:T(8,128)S(1)}, f32[64,768]{1,0:T(8,128)S(1)}, u32[]{:S(2)}, u32[]{:S(2)}) %collective-permute-start.10) | collective-permute-done | bytes 196640 | tf_op jit(solution)/shard_map/ppermute | solution.py:292
  86.3 1.8 %collective-permute-start.11 = (f32[64,768]{1,0:T(8,128)S(1)}, f32[64,768]{1,0:T(8,128)S(1)}, u32[]{:S(2)}, u32[]{:S(2)}) collective-permute-start(f32[64,768]{1,0:T(8,128)S(1)} %add.10), channel_id=1, source_target_pairs={{0,4},{1,5},{2,6},{3,7},{4,0},{5,1},{6,2},{7,3},{8,12},{9,13},{10,... | collective-permute-start | bytes 589832 | tf_op jit(solution)/shard_map/ppermute | solution.py:292
  88.1 1.3 %collective-permute-start.12 = (bf16[8,64,768]{2,1,0:T(8,128)(2,1)S(1)}, bf16[8,64,768]{2,1,0:T(8,128)(2,1)S(1)}, u32[]{:S(2)}, u32[]{:S(2)}) collective-permute-start(bf16[8,64,768]{2,1,0:T(8,128)(2,1)S(1)} %get-tuple-element.102), channel_id=1, source_target_pairs={{8,0},{16,8},{24,16},{9,1},{17,9},{25,17},{10,2},{18,10},{26,18},{... | collective-permute-start | bytes 2359304 | tf_op jit(solution)/shard_map/ppermute | solution.py:288
  89.4 3.4 %collective-permute-done.11 = f32[64,768]{1,0:T(8,128)S(1)} collective-permute-done((f32[64,768]{1,0:T(8,128)S(1)}, f32[64,768]{1,0:T(8,128)S(1)}, u32[]{:S(2)}, u32[]{:S(2)}) %collective-permute-start.11) | collective-permute-done | bytes 196640 | tf_op jit(solution)/shard_map/ppermute | solution.py:292
  92.9 0.8 copy.19
  93.8 0.6 copy.20
  94.4 14.5 %collective-permute-done.12 = bf16[8,64,768]{2,1,0:T(8,128)(2,1)S(1)} collective-permute-done((bf16[8,64,768]{2,1,0:T(8,128)(2,1)S(1)}, bf16[8,64,768]{2,1,0:T(8,128)(2,1)S(1)}, u32[]{:S(2)}, u32[]{:S(2)}) %collective-permute-start.12) | collective-permute-done | bytes 786464 | tf_op jit(solution)/shard_map/ppermute | solution.py:288
  108.9 1.9 %merge.1 = (f32[384,768]{1,0:T(8,128)}, f32[768,384]{1,0:T(8,128)}) custom-call(f32[384,768]{1,0:T(8,128)S(1)} %get-tuple-element.68.refs_0_, f32[384,768]{1,0:T(8,128)S(1)} %get-tuple-element.69.refs_1_, bf16[768,768]{1,0:T(8,128)(2,1)S(1)} %collective-permute-done.6.refs_2_, bf16[768,768]{1,0:T(8,128)(2,1)S(1)} %collective-permute-done.8.refs_3_), custom_call_target="tpu_custom_call" | custom-call | flops 10000000000 | bytes 1000000 | tf_op jit(solution)/shard_map/merge/pallas_call | solution.py:25
  110.8 0.9 copy.25
  (14 shorter events, 0.1 us)
Async XLA Ops:
  9.1 9.4 %collective-permute-start = (bf16[1024,768]{1,0:T(8,128)(2,1)S(1)}, bf16[1024,768]{1,0:T(8,128)(2,1)S(1)}, u32[]{:S(2)}, u32[]{:S(2)}) collective-permute-start(bf16[1024,768]{1,0:T(8,128)(2,1)S(1)} %get-tuple-element.55.refs_0_.refs_1_), channel_id=1, source_target_pairs={{0,1},{1,0},{2,3},{3,2},{4,5},{5,4},{6,7},{7,6},{8,9},{9,8},{10,11... | collective-permute-start | bytes 4718600 | tf_op jit(solution)/shard_map/ppermute | solution.py:292
  13.7 4.8 %collective-permute-start.1 = (bf16[768,512]{1,0:T(8,128)(2,1)S(1)}, bf16[768,512]{1,0:T(8,128)(2,1)S(1)}, u32[]{:S(2)}, u32[]{:S(2)}) collective-permute-start(bf16[768,512]{1,0:T(8,128)(2,1)S(1)} %get-tuple-element.61), channel_id=1, source_target_pairs={{0,1},{1,0},{2,3},{3,2},{4,5},{5,4},{6,7},{7,6},{8,9},{9,8},{10,11... | collective-permute-start | bytes 2359304 | tf_op jit(solution)/shard_map/ppermute | solution.py:292
  18.0 15.1 %collective-permute-start.3 = (bf16[768,512]{1,0:T(8,128)(2,1)S(1)}, bf16[768,512]{1,0:T(8,128)(2,1)S(1)}, u32[]{:S(2)}, u32[]{:S(2)}) collective-permute-start(bf16[768,512]{1,0:T(8,128)(2,1)S(1)} %get-tuple-element.72), channel_id=1, source_target_pairs={{0,1},{1,0},{2,3},{3,2},{4,5},{5,4},{6,7},{7,6},{8,9},{9,8},{10,11... | collective-permute-start | bytes 2359304 | tf_op jit(solution)/shard_map/ppermute | solution.py:292
  19.9 16.6 %collective-permute-start.4 = (bf16[384,768]{1,0:T(8,128)(2,1)S(1)}, bf16[384,768]{1,0:T(8,128)(2,1)S(1)}, u32[]{:S(2)}, u32[]{:S(2)}) collective-permute-start(bf16[384,768]{1,0:T(8,128)(2,1)S(1)} %get-tuple-element.73), channel_id=1, source_target_pairs={{0,4},{1,5},{2,6},{3,7},{4,0},{5,1},{6,2},{7,3},{8,12},{9,13},{10,... | collective-permute-start | bytes 1769480 | tf_op jit(solution)/shard_map/ppermute | solution.py:292
  22.5 15.4 %collective-permute-start.5 = (bf16[384,768]{1,0:T(8,128)(2,1)S(1)}, bf16[384,768]{1,0:T(8,128)(2,1)S(1)}, u32[]{:S(2)}, u32[]{:S(2)}) collective-permute-start(bf16[384,768]{1,0:T(8,128)(2,1)S(1)} %get-tuple-element.75), channel_id=1, source_target_pairs={{0,2},{1,3},{2,0},{3,1},{4,6},{5,7},{6,4},{7,5},{8,10},{9,11},{10,... | collective-permute-start | bytes 1769480 | tf_op jit(solution)/shard_map/ppermute | solution.py:292
  32.5 13.9 %collective-permute-start.2 = (bf16[768,512]{1,0:T(8,128)(2,1)S(1)}, bf16[768,512]{1,0:T(8,128)(2,1)S(1)}, u32[]{:S(2)}, u32[]{:S(2)}) collective-permute-start(bf16[768,512]{1,0:T(8,128)(2,1)S(1)} %get-tuple-element.67), channel_id=1, source_target_pairs={{0,1},{1,0},{2,3},{3,2},{4,5},{5,4},{6,7},{7,6},{8,9},{9,8},{10,11... | collective-permute-start | bytes 2359304 | tf_op jit(solution)/shard_map/ppermute | solution.py:292
  32.6 5.4 %collective-permute-start.7 = (bf16[768,512]{1,0:T(8,128)(2,1)S(1)}, bf16[768,512]{1,0:T(8,128)(2,1)S(1)}, u32[]{:S(2)}, u32[]{:S(2)}) collective-permute-start(bf16[768,512]{1,0:T(8,128)(2,1)S(1)} %get-tuple-element.79), channel_id=1, source_target_pairs={{0,1},{1,0},{2,3},{3,2},{4,5},{5,4},{6,7},{7,6},{8,9},{9,8},{10,11... | collective-permute-start | bytes 2359304 | tf_op jit(solution)/shard_map/ppermute | solution.py:292
  53.6 3.4 %collective-permute-start.9 = (f32[64,768]{1,0:T(8,128)S(1)}, f32[64,768]{1,0:T(8,128)S(1)}, u32[]{:S(2)}, u32[]{:S(2)}) collective-permute-start(f32[64,768]{1,0:T(8,128)S(1)} %taps.1), channel_id=1, source_target_pairs={{0,1},{1,0},{2,3},{3,2},{4,5},{5,4},{6,7},{7,6},{8,9},{9,8},{10,11... | collective-permute-start | bytes 589832 | tf_op jit(solution)/shard_map/ppermute | solution.py:292
  53.7 55.1 %collective-permute-start.6 = (bf16[768,768]{1,0:T(8,128)(2,1)S(1)}, bf16[768,768]{1,0:T(8,128)(2,1)S(1)}, u32[]{:S(2)}, u32[]{:S(2)}) collective-permute-start(bf16[768,768]{1,0:T(8,128)(2,1)S(1)} %get-tuple-element.76), channel_id=1, source_target_pairs={{0,2},{1,3},{2,0},{3,1},{4,6},{5,7},{6,4},{7,5},{8,10},{9,11},{10,... | collective-permute-start | bytes 3538952 | tf_op jit(solution)/shard_map/ppermute | solution.py:292
  55.5 53.3 %collective-permute-start.8 = (bf16[768,768]{1,0:T(8,128)(2,1)S(1)}, bf16[768,768]{1,0:T(8,128)(2,1)S(1)}, u32[]{:S(2)}, u32[]{:S(2)}) collective-permute-start(bf16[768,768]{1,0:T(8,128)(2,1)S(1)} %get-tuple-element.82), channel_id=1, source_target_pairs={{0,4},{1,5},{2,6},{3,7},{4,0},{5,1},{6,2},{7,3},{8,12},{9,13},{10,... | collective-permute-start | bytes 3538952 | tf_op jit(solution)/shard_map/ppermute | solution.py:292
  57.1 29.2 %collective-permute-start.10 = (f32[64,768]{1,0:T(8,128)S(1)}, f32[64,768]{1,0:T(8,128)S(1)}, u32[]{:S(2)}, u32[]{:S(2)}) collective-permute-start(f32[64,768]{1,0:T(8,128)S(1)} %add.9), channel_id=1, source_target_pairs={{0,2},{1,3},{2,0},{3,1},{4,6},{5,7},{6,4},{7,5},{8,10},{9,11},{10,... | collective-permute-start | bytes 589832 | tf_op jit(solution)/shard_map/ppermute | solution.py:292
  86.3 6.5 %collective-permute-start.11 = (f32[64,768]{1,0:T(8,128)S(1)}, f32[64,768]{1,0:T(8,128)S(1)}, u32[]{:S(2)}, u32[]{:S(2)}) collective-permute-start(f32[64,768]{1,0:T(8,128)S(1)} %add.10), channel_id=1, source_target_pairs={{0,4},{1,5},{2,6},{3,7},{4,0},{5,1},{6,2},{7,3},{8,12},{9,13},{10,... | collective-permute-start | bytes 589832 | tf_op jit(solution)/shard_map/ppermute | solution.py:292
  88.1 20.7 %collective-permute-start.12 = (bf16[8,64,768]{2,1,0:T(8,128)(2,1)S(1)}, bf16[8,64,768]{2,1,0:T(8,128)(2,1)S(1)}, u32[]{:S(2)}, u32[]{:S(2)}) collective-permute-start(bf16[8,64,768]{2,1,0:T(8,128)(2,1)S(1)} %get-tuple-element.102), channel_id=1, source_target_pairs={{8,0},{16,8},{24,16},{9,1},{17,9},{25,17},{10,2},{18,10},{26,18},{... | collective-permute-start | bytes 2359304 | tf_op jit(solution)/shard_map/ppermute | solution.py:288

commit v3 on v2

--- a/solution.py
+++ b/solution.py
@@ -404,8 +404,7 @@
                  xp, gd, vecs, sums, *more, name="taps", cost=estimate(1e6, 1e3))
 
     if fast:
-        for bit in (1, 2, 4):
-            small = small + swap(small, bit, replicas)
+        small = jnp.sum(lax.all_gather(small.astype(bf16), "dp").astype(f32), axis=0)
         out1, out2 = call(
             lambda *refs: merge_kernel(*refs, factor=factor),
             (struct((part, chans), f32), struct((chans, part), f32)),

time: 112 us -> 79.2 us (0.71)
  waiting for transfers between devices: 50 us -> 3.46 us
  blocking collectives: 0 us -> 16.3 us
  starting transfers between devices: 12.9 us -> 10.5 us
    ppermute x12 -> x9, waiting for transfers between devices: 35.6 us -> 3.46 us  [swap(): return lax.ppermute(value, 'dp', [(i, i ^ bit) for i in range(count)])]
    all_gather x0 -> x1, blocking collectives: none -> 16.3 us  [shards(): lax.all_gather(small.astype(bf16), 'dp').astype(f32)]
    ppermute x1, waiting for transfers between devices: 14.5 us -> 0.01 us  [shifted(): return lax.ppermute(block, axis, route)]
    ppermute x12 -> x9, starting transfers between devices: 11.6 us -> 9.25 us  [swap(): return lax.ppermute(value, 'dp', [(i, i ^ bit) for i in range(count)])]
    unnamed x4 -> x3, local copies, waits for them, and re-layouts: 2.34 us -> 1.5 us
  transfers between devices with their start and end apart: 13 -> 10, of which waited for: 4 -> 1; matrix products, arithmetic and copies ran while one was open for 1% -> 2% of each run, Pallas kernels for 25% -> 44%
where the time goes in v3:
time: 79.2 us; the launch traced here: 79 us
  Pallas kernels  45.5 us (57%)
  blocking collectives  16.3 us (21%)
  starting transfers between devices  10.5 us (13%)
  waiting for transfers between devices  3.46 us (4%)
  local copies, waits for them, and re-layouts  2.29 us (3%)
    pallas_call x12, Pallas kernels, call(): pl.pallas_call(body, out_shape=out_shape, in_specs=specs, out_specs=jax.t...  45.5 us
    all_gather x1, blocking collectives, shards(): lax.all_gather(small.astype(bf16), 'dp').astype(f32)  16.3 us
    ppermute x9, starting transfers between devices, swap(): return lax.ppermute(value, 'dp', [(i, i ^ bit) for i in range(count)])  9.25 us
    ppermute x9, waiting for transfers between devices, swap(): return lax.ppermute(value, 'dp', [(i, i ^ bit) for i in range(count)])  3.46 us
  transfers between devices with their start and end apart: 10, of which 1 were waited for; matrix products, arithmetic and copies ran while one was open for 2% of the time, Pallas kernels for 44%

profile of v3, /device:TPU:0, one launch (start us, length us, event | category | flops | bytes accessed | tf_op | source)
XLA Modules:
  0.0 79.0 jit_solution(7569012688003315430)
XLA Ops:
  0.6 8.4 %front.1 = (bf16[1024,768]{1,0:T(8,128)(2,1)S(1)}, f32[512,768]{1,0:T(8,128)S(1)}, f32[512,128]{1,0:T(8,128)S(1)}, f32[6,8,80,128]{3,2,1,0:T(8,128)S(1)}, f32[8,...) custom-call(bf16[8,64,768]{2,1,0:T(8,128)(2,1)} %bitcast.19, ...), custom_call_target="tpu_custom_call" | custom-call | flops 10000000000 | bytes 1000000 | tf_op jit(solution)/shard_map/front/pallas_call | solution.py:25
  9.1 0.5 collective-permute-start
  9.6 4.1 %wide.4 = (f32[512,768]{1,0:T(8,128)S(1)}, f32[8,768]{1,0:T(8,128)S(1)}, bf16[768,512]{1,0:T(8,128)(2,1)S(1)}, bf16[768,512]{1,0:T(8,128)(2,1)S(1)}) custom-call(bf16[1024,768]{1,0:T(8,128)(2,1)S(1)} %get-tuple-element.55.refs_0_.refs_1_, bf16[3072,768]{1,0:T(8,128)(2,1)S(1)} %get-tuple-element.56.refs_1_, f32[1,3072]{1,0:T(1,128)S(1)} %get-tuple-element.57.refs_2_, ...), custom_call_target="tpu_custom_call" | custom-call | flops 10000000000 | bytes 1000000 | tf_op jit(solution)/shard_map/wide/pallas_call | solution.py:25
  13.7 0.2 collective-permute-start.1
  13.9 4.1 %wide.5 = (f32[512,768]{1,0:T(8,128)S(1)}, f32[8,768]{1,0:T(8,128)S(1)}, bf16[768,512]{1,0:T(8,128)(2,1)S(1)}, bf16[768,512]{1,0:T(8,128)(2,1)S(1)}) custom-call(bf16[1024,768]{1,0:T(8,128)(2,1)S(1)} %get-tuple-element.55.refs_0_.refs_1_, bf16[3072,768]{1,0:T(8,128)(2,1)S(1)} %get-tuple-element.56.refs_1_, ...), custom_call_target="tpu_custom_call", output_to_operand_aliasing={{0}: (4, {})} | custom-call | flops 10000000000 | bytes 1000000 | tf_op jit(solution)/shard_map/wide/pallas_call | solution.py:25
  18.0 0.5 collective-permute-start.3
  18.5 1.4 %share.2 = (bf16[384,768]{1,0:T(8,128)(2,1)S(1)}, bf16[384,768]{1,0:T(8,128)(2,1)S(1)}, f32[8,768]{1,0:T(8,128)S(1)}) custom-call(bf16[768,3072]{1,0:T(8,128)(2,1)S(1)} %get-tuple-element.54.refs_3_.refs_0_, bf16[1024,768]{1,0:T(8,128)(2,1)S(1)} %get-tuple-element.55.refs_0_.refs_1_, bf16[1024,768]{1,0:T(8,128)(2,1)S(1)} %collective-permute-done.refs_2_, ...), custom_call_target="tpu_custom_call" | custom-call | flops 1000000 | bytes 1000 | tf_op jit(solution)/shard_map/share/pallas_call | solution.py:25
  19.9 2.6 %collective-permute-start.4 = (bf16[384,768]{1,0:T(8,128)(2,1)S(1)}, bf16[384,768]{1,0:T(8,128)(2,1)S(1)}, u32[]{:S(2)}, u32[]{:S(2)}) collective-permute-start(bf16[384,768]{1,0:T(8,128)(2,1)S(1)} %get-tuple-element.73), channel_id=1, source_target_pairs={{0,4},{1,5},{2,6},{3,7},{4,0},{5,1},{6,2},{7,3},{8,12},{9,13},{10,... | collective-permute-start | bytes 1769480 | tf_op jit(solution)/shard_map/ppermute | solution.py:292
  22.5 1.5 %collective-permute-start.5 = (bf16[384,768]{1,0:T(8,128)(2,1)S(1)}, bf16[384,768]{1,0:T(8,128)(2,1)S(1)}, u32[]{:S(2)}, u32[]{:S(2)}) collective-permute-start(bf16[384,768]{1,0:T(8,128)(2,1)S(1)} %get-tuple-element.75), channel_id=1, source_target_pairs={{0,2},{1,3},{2,0},{3,1},{4,6},{5,7},{6,4},{7,5},{8,10},{9,11},{10,... | collective-permute-start | bytes 1769480 | tf_op jit(solution)/shard_map/ppermute | solution.py:292
  24.0 4.3 %wide.6 = (f32[512,768]{1,0:T(8,128)S(1)}, f32[8,768]{1,0:T(8,128)S(1)}, bf16[768,512]{1,0:T(8,128)(2,1)S(1)}, bf16[768,512]{1,0:T(8,128)(2,1)S(1)}) custom-call(bf16[1024,768]{1,0:T(8,128)(2,1)S(1)} %get-tuple-element.55.refs_0_.refs_1_, bf16[3072,768]{1,0:T(8,128)(2,1)S(1)} %get-tuple-element.56.refs_1_, ...), custom_call_target="tpu_custom_call", output_to_operand_aliasing={{0}: (4, {})} | custom-call | flops 10000000000 | bytes 1000000 | tf_op jit(solution)/shard_map/wide/pallas_call | solution.py:25
  28.4 4.1 %wide.7 = (f32[512,768]{1,0:T(8,128)S(1)}, f32[8,768]{1,0:T(8,128)S(1)}, bf16[768,512]{1,0:T(8,128)(2,1)S(1)}, bf16[768,512]{1,0:T(8,128)(2,1)S(1)}) custom-call(bf16[1024,768]{1,0:T(8,128)(2,1)S(1)} %get-tuple-element.55.refs_0_.refs_1_, bf16[3072,768]{1,0:T(8,128)(2,1)S(1)} %get-tuple-element.56.refs_1_, ...), custom_call_target="tpu_custom_call", output_to_operand_aliasing={{0}: (4, {})} | custom-call | flops 10000000000 | bytes 1000000 | tf_op jit(solution)/shard_map/wide/pallas_call | solution.py:25
  32.5 0.1 collective-permute-start.2
  32.6 0.5 collective-permute-start.7
  33.1 0.0 collective-permute-done.3.refs_4_
  33.1 3.4 %collective-permute-done.4.refs_5_ = bf16[384,768]{1,0:T(8,128)(2,1)S(1)} collective-permute-done((bf16[384,768]{1,0:T(8,128)(2,1)S(1)}, bf16[384,768]{1,0:T(8,128)(2,1)S(1)}, u32[]{:S(2)}, u32[]{:S(2)}) %collective-permute-start.4) | collective-permute-done | bytes 589856 | tf_op jit(solution)/shard_map/ppermute | solution.py:292
  36.5 1.4 %pack.2 = (bf16[768,768]{1,0:T(8,128)(2,1)S(1)}, f32[8,768]{1,0:T(8,128)S(1)}) custom-call(bf16[768,3072]{1,0:T(8,128)(2,1)S(1)} %get-tuple-element.54.refs_3_.refs_0_, bf16[1024,768]{1,0:T(8,128)(2,1)S(1)} %get-tuple-element.55.refs_0_.refs_1_, bf16[1024,768]{1,0:T(8,128)(2,1)S(1)} %collective-permute-done.refs_2_, ...), custom_call_target="tpu_custom_call" | custom-call | flops 10000000000 | bytes 1000000 | tf_op jit(solution)/shard_map/pack/pallas_call | solution.py:25
  37.9 0.0 collective-permute-done.5.refs_5_
  37.9 1.8 %collective-permute-start.6 = (bf16[768,768]{1,0:T(8,128)(2,1)S(1)}, bf16[768,768]{1,0:T(8,128)(2,1)S(1)}, u32[]{:S(2)}, u32[]{:S(2)}) collective-permute-start(bf16[768,768]{1,0:T(8,128)(2,1)S(1)} %get-tuple-element.76), channel_id=1, source_target_pairs={{0,2},{1,3},{2,0},{3,1},{4,6},{5,7},{6,4},{7,5},{8,10},{9,11},{10,... | collective-permute-start | bytes 3538952 | tf_op jit(solution)/shard_map/ppermute | solution.py:292
  39.7 0.0 collective-permute-done.7.refs_4_
  39.7 1.4 %pack.3 = (bf16[768,768]{1,0:T(8,128)(2,1)S(1)}, f32[8,768]{1,0:T(8,128)S(1)}) custom-call(bf16[768,3072]{1,0:T(8,128)(2,1)S(1)} %get-tuple-element.54.refs_3_.refs_0_, bf16[1024,768]{1,0:T(8,128)(2,1)S(1)} %get-tuple-element.55.refs_0_.refs_1_, bf16[1024,768]{1,0:T(8,128)(2,1)S(1)} %collective-permute-done.refs_2_, ...), custom_call_target="tpu_custom_call" | custom-call | flops 10000000000 | bytes 1000000 | tf_op jit(solution)/shard_map/pack/pallas_call | solution.py:25
  41.2 1.6 %collective-permute-start.8 = (bf16[768,768]{1,0:T(8,128)(2,1)S(1)}, bf16[768,768]{1,0:T(8,128)(2,1)S(1)}, u32[]{:S(2)}, u32[]{:S(2)}) collective-permute-start(bf16[768,768]{1,0:T(8,128)(2,1)S(1)} %get-tuple-element.82), channel_id=1, source_target_pairs={{0,4},{1,5},{2,6},{3,7},{4,0},{5,1},{6,2},{7,3},{8,12},{9,13},{10,... | collective-permute-start | bytes 3538952 | tf_op jit(solution)/shard_map/ppermute | solution.py:292
  42.7 7.1 %back.1 = (bf16[8,64,768]{2,1,0:T(8,128)(2,1)S(1)}, f32[6,8,80,128]{3,2,1,0:T(8,128)S(1)}, f32[8,768]{1,0:T(8,128)S(1)}) custom-call(f32[512,768]{1,0:T(8,128)S(1)} %get-tuple-element.86.gn_ref, f32[512,768]{1,0:T(8,128)S(1)} %get-tuple-element.87.normed_ref, f32[512,128]{1,0:T(8,128)S(1)} %get-tuple-element.88.rstd_ref, ...), custom_call_target="tpu_custom_call" | custom-call | flops 1000000 | bytes 1000 | tf_op jit(solution)/shard_map/back/pallas_call | solution.py:25
  49.8 1.3 %collective-permute-start.9 = (bf16[8,64,768]{2,1,0:T(8,128)(2,1)S(1)}, bf16[8,64,768]{2,1,0:T(8,128)(2,1)S(1)}, u32[]{:S(2)}, u32[]{:S(2)}) collective-permute-start(bf16[8,64,768]{2,1,0:T(8,128)(2,1)S(1)} %get-tuple-element.102), channel_id=1, source_target_pairs={{8,0},{16,8},{24,16},{9,1},{17,9},{25,17},{10,2},{18,10},{26,18},{... | collective-permute-start | bytes 2359304 | tf_op jit(solution)/shard_map/ppermute | solution.py:288
  51.1 0.0 collective-permute-done.2.refs_4_
  51.1 1.4 %share.3 = (f32[384,768]{1,0:T(8,128)S(1)}, f32[384,768]{1,0:T(8,128)S(1)}, f32[8,768]{1,0:T(8,128)S(1)}) custom-call(bf16[768,3072]{1,0:T(8,128)(2,1)S(1)} %get-tuple-element.54.refs_3_.refs_0_, bf16[1024,768]{1,0:T(8,128)(2,1)S(1)} %get-tuple-element.55.refs_0_.refs_1_, bf16[1024,768]{1,0:T(8,128)(2,1)S(1)} %collective-permute-done.refs_2_, ...), custom_call_target="tpu_custom_call" | custom-call | flops 1000000 | bytes 1000 | tf_op jit(solution)/shard_map/share/pallas_call | solution.py:25
  52.5 5.8 %taps.1 = f32[64,768]{1,0:T(8,128)S(1)} custom-call(f32[6,8,80,128]{3,2,1,0:T(8,128)S(1)} %get-tuple-element.85.refs_0_, f32[6,8,80,128]{3,2,1,0:T(8,128)S(1)} %get-tuple-element.92.refs_1_, f32[8,768]{1,0:T(8,128)S(1)} %get-tuple-element.89.vecs_ref.refs_2_, f32[8,768]{1,0:T(8,128)S(1)} %get-tuple-element.93.refs_3_, ...), custom_call_target="tpu_custom_call" | custom-call | flops 1000000 | bytes 1000 | tf_op jit(solution)/shard_map/taps/pallas_call | solution.py:25
  58.3 16.3 %all-gather = bf16[512,768]{1,0:T(8,128)(2,1)S(1)} all-gather(bf16[64,768]{1,0:T(8,128)(2,1)S(1)} %convert_element_type.6), channel_id=2, replica_groups=mesh['section'=4,'dp'=8] {'dp'}, dimensions={0}, use_global_device_ids=true | all-gather | bytes 884736 | tf_op jit(solution)/shard_map/all_gather | solution.py:407
  74.6 0.1 convert_reduce_fusion
  74.8 0.8 broadcast_in_dim.14
  75.6 0.6 copy.19
  76.2 1.9 %merge.1 = (f32[384,768]{1,0:T(8,128)}, f32[768,384]{1,0:T(8,128)}) custom-call(f32[384,768]{1,0:T(8,128)S(1)} %get-tuple-element.68.refs_0_, f32[384,768]{1,0:T(8,128)S(1)} %get-tuple-element.69.refs_1_, bf16[768,768]{1,0:T(8,128)(2,1)S(1)} %collective-permute-done.6.refs_2_, bf16[768,768]{1,0:T(8,128)(2,1)S(1)} %collective-permute-done.8.refs_3_), custom_call_target="tpu_custom_call" | custom-call | flops 10000000000 | bytes 1000000 | tf_op jit(solution)/shard_map/merge/pallas_call | solution.py:25
  78.1 0.9 %copy.24 = bf16[1,1,8,64,768]{4,3,2,1,0:T(8,128)(2,1)} copy(bf16[1,1,8,64,768]{4,3,2,1,0:T(8,128)(2,1)S(1)} %bitcast.15) | data formatting | bytes 1572864
  (9 shorter events, 0.1 us)
Async XLA Ops:
  9.1 9.4 %collective-permute-start = (bf16[1024,768]{1,0:T(8,128)(2,1)S(1)}, bf16[1024,768]{1,0:T(8,128)(2,1)S(1)}, u32[]{:S(2)}, u32[]{:S(2)}) collective-permute-start(bf16[1024,768]{1,0:T(8,128)(2,1)S(1)} %get-tuple-element.55.refs_0_.refs_1_), channel_id=1, source_target_pairs={{0,1},{1,0},{2,3},{3,2},{4,5},{5,4},{6,7},{7,6},{8,9},{9,8},{10,11... | collective-permute-start | bytes 4718600 | tf_op jit(solution)/shard_map/ppermute | solution.py:292
  13.7 4.8 %collective-permute-start.1 = (bf16[768,512]{1,0:T(8,128)(2,1)S(1)}, bf16[768,512]{1,0:T(8,128)(2,1)S(1)}, u32[]{:S(2)}, u32[]{:S(2)}) collective-permute-start(bf16[768,512]{1,0:T(8,128)(2,1)S(1)} %get-tuple-element.61), channel_id=1, source_target_pairs={{0,1},{1,0},{2,3},{3,2},{4,5},{5,4},{6,7},{7,6},{8,9},{9,8},{10,11... | collective-permute-start | bytes 2359304 | tf_op jit(solution)/shard_map/ppermute | solution.py:292
  18.0 15.1 %collective-permute-start.3 = (bf16[768,512]{1,0:T(8,128)(2,1)S(1)}, bf16[768,512]{1,0:T(8,128)(2,1)S(1)}, u32[]{:S(2)}, u32[]{:S(2)}) collective-permute-start(bf16[768,512]{1,0:T(8,128)(2,1)S(1)} %get-tuple-element.72), channel_id=1, source_target_pairs={{0,1},{1,0},{2,3},{3,2},{4,5},{5,4},{6,7},{7,6},{8,9},{9,8},{10,11... | collective-permute-start | bytes 2359304 | tf_op jit(solution)/shard_map/ppermute | solution.py:292
  19.9 16.6 %collective-permute-start.4 = (bf16[384,768]{1,0:T(8,128)(2,1)S(1)}, bf16[384,768]{1,0:T(8,128)(2,1)S(1)}, u32[]{:S(2)}, u32[]{:S(2)}) collective-permute-start(bf16[384,768]{1,0:T(8,128)(2,1)S(1)} %get-tuple-element.73), channel_id=1, source_target_pairs={{0,4},{1,5},{2,6},{3,7},{4,0},{5,1},{6,2},{7,3},{8,12},{9,13},{10,... | collective-permute-start | bytes 1769480 | tf_op jit(solution)/shard_map/ppermute | solution.py:292
  22.5 15.4 %collective-permute-start.5 = (bf16[384,768]{1,0:T(8,128)(2,1)S(1)}, bf16[384,768]{1,0:T(8,128)(2,1)S(1)}, u32[]{:S(2)}, u32[]{:S(2)}) collective-permute-start(bf16[384,768]{1,0:T(8,128)(2,1)S(1)} %get-tuple-element.75), channel_id=1, source_target_pairs={{0,2},{1,3},{2,0},{3,1},{4,6},{5,7},{6,4},{7,5},{8,10},{9,11},{10,... | collective-permute-start | bytes 1769480 | tf_op jit(solution)/shard_map/ppermute | solution.py:292
  32.5 18.6 %collective-permute-start.2 = (bf16[768,512]{1,0:T(8,128)(2,1)S(1)}, bf16[768,512]{1,0:T(8,128)(2,1)S(1)}, u32[]{:S(2)}, u32[]{:S(2)}) collective-permute-start(bf16[768,512]{1,0:T(8,128)(2,1)S(1)} %get-tuple-element.67), channel_id=1, source_target_pairs={{0,1},{1,0},{2,3},{3,2},{4,5},{5,4},{6,7},{7,6},{8,9},{9,8},{10,11... | collective-permute-start | bytes 2359304 | tf_op jit(solution)/shard_map/ppermute | solution.py:292
  32.6 7.2 %collective-permute-start.7 = (bf16[768,512]{1,0:T(8,128)(2,1)S(1)}, bf16[768,512]{1,0:T(8,128)(2,1)S(1)}, u32[]{:S(2)}, u32[]{:S(2)}) collective-permute-start(bf16[768,512]{1,0:T(8,128)(2,1)S(1)} %get-tuple-element.79), channel_id=1, source_target_pairs={{0,1},{1,0},{2,3},{3,2},{4,5},{5,4},{6,7},{7,6},{8,9},{9,8},{10,11... | collective-permute-start | bytes 2359304 | tf_op jit(solution)/shard_map/ppermute | solution.py:292
  37.9 38.2 %collective-permute-start.6 = (bf16[768,768]{1,0:T(8,128)(2,1)S(1)}, bf16[768,768]{1,0:T(8,128)(2,1)S(1)}, u32[]{:S(2)}, u32[]{:S(2)}) collective-permute-start(bf16[768,768]{1,0:T(8,128)(2,1)S(1)} %get-tuple-element.76), channel_id=1, source_target_pairs={{0,2},{1,3},{2,0},{3,1},{4,6},{5,7},{6,4},{7,5},{8,10},{9,11},{10,... | collective-permute-start | bytes 3538952 | tf_op jit(solution)/shard_map/ppermute | solution.py:292
  41.2 35.0 %collective-permute-start.8 = (bf16[768,768]{1,0:T(8,128)(2,1)S(1)}, bf16[768,768]{1,0:T(8,128)(2,1)S(1)}, u32[]{:S(2)}, u32[]{:S(2)}) collective-permute-start(bf16[768,768]{1,0:T(8,128)(2,1)S(1)} %get-tuple-element.82), channel_id=1, source_target_pairs={{0,4},{1,5},{2,6},{3,7},{4,0},{5,1},{6,2},{7,3},{8,12},{9,13},{10,... | collective-permute-start | bytes 3538952 | tf_op jit(solution)/shard_map/ppermute | solution.py:292
  49.8 26.4 %collective-permute-start.9 = (bf16[8,64,768]{2,1,0:T(8,128)(2,1)S(1)}, bf16[8,64,768]{2,1,0:T(8,128)(2,1)S(1)}, u32[]{:S(2)}, u32[]{:S(2)}) collective-permute-start(bf16[8,64,768]{2,1,0:T(8,128)(2,1)S(1)} %get-tuple-element.102), channel_id=1, source_target_pairs={{8,0},{16,8},{24,16},{9,1},{17,9},{25,17},{10,2},{18,10},{26,18},{... | collective-permute-start | bytes 2359304 | tf_op jit(solution)/shard_map/ppermute | solution.py:288

commit v4 on v3

--- a/solution.py
+++ b/solution.py
@@ -150,52 +150,44 @@
     w1 = w1_ref[pl.ds(at, wide), :]
     w2 = w2_ref[:, pl.ds(at, wide)]
     b1 = b1_ref[:, pl.ds(at, wide)]
-    step = 128
-    total = jnp.zeros((8, wide), f32)
-    for r in range(0, cells, step):
-        pre = dot_last(acts_ref[r : r + step, :], w1) + b1
-        cdf = 0.5 * (1.0 + lax.erf(pre * root_half))
-        hidden = (pre * cdf).astype(bf16)
-        ghid = dot(acts_ref[cells + r : cells + r + step, :], w2)
-        density = jnp.exp(-0.5 * pre * pre) * inv_root_two_pi
-        gpre = (ghid * (cdf + pre * density)).astype(bf16)
-        total = total + jnp.sum(gpre.astype(f32).reshape(step // 8, 8, wide), axis=0)
-        gn = dot(gpre, w1)
-        gn_ref[r : r + step, :] = gn if first else gin[0][r : r + step, :] + gn
-        gt, ht = gpre.T, hidden.T
-        for side in range(2):
-            @pl.when(core == side)
-            def _(side=side):
-                k, s = side * part, (1 - side) * part
-                keep_ref[0:part, r : r + step] = gt[k : k + part, :]
-                send_ref[0:part, r : r + step] = gt[s : s + part, :]
-                keep_ref[part:, r : r + step] = ht[k : k + part, :]
-                send_ref[part:, r : r + step] = ht[s : s + part, :]
-    bsum_ref[...] = jnp.broadcast_to(jnp.sum(total, axis=0, keepdims=True), (8, wide))
-
-
-def share_kernel(w2_ref, own_ref, sib_ref, keep_ref, got_ref, *rest, slot, mode):
+    pre = dot_last(acts_ref[0:cells, :], w1) + b1
+    cdf = 0.5 * (1.0 + lax.erf(pre * root_half))
+    hidden = (pre * cdf).astype(bf16)
+    ghid = dot(acts_ref[cells:, :], w2)
+    density = jnp.exp(-0.5 * pre * pre) * inv_root_two_pi
+    gpre = (ghid * (cdf + pre * density)).astype(bf16)
+    total = jnp.sum(gpre.astype(f32), axis=0, keepdims=True)
+    bsum_ref[...] = jnp.broadcast_to(total, (8, wide))
+    gn = dot(gpre, w1)
+    gn_ref[...] = gn if first else gin[0][...] + gn
+    gt, ht = gpre.T, hidden.T
+    for side in range(2):
+        @pl.when(core == side)
+        def _(side=side):
+            k, s = side * part, (1 - side) * part
+            keep_ref[0:part, :] = gt[k : k + part, :]
+            send_ref[0:part, :] = gt[s : s + part, :]
+            keep_ref[part:, :] = ht[k : k + part, :]
+            send_ref[part:, :] = ht[s : s + part, :]
+
+
+def share_kernel(w2_ref, own_ref, sib_ref, keep_ref, got_ref, d1_ref, d2_ref, scale_ref, *, slot):
     part = keep_ref.shape[0] // 2
     cells = own_ref.shape[0] // 2
     chip, core = place()
     at = pl.multiple_of((2 * slot(chip) + core) * part, part)
     d1 = dot(keep_ref[0:part, :], own_ref[0:cells, :]) + dot(got_ref[0:part, :], sib_ref[0:cells, :])
+    d1_ref[...] = d1.astype(d1_ref.dtype)
     d2 = dot(keep_ref[part:, :], own_ref[cells:, :]) + dot(got_ref[part:, :], sib_ref[cells:, :])
+    d2_ref[...] = d2.astype(d2_ref.dtype)
     prod = d2 * w2_ref[:, pl.ds(at, part)].T.astype(f32)
-    if mode == "split":
-        d1_ref, d2_ref, scale_ref = rest
-        d1_ref[...] = d1.astype(d1_ref.dtype)
-        d2_ref[...] = d2.astype(d2_ref.dtype)
-    else:
-        in_ref, pack_ref, scale_ref = rest
-        more = in_ref[...].astype(f32)
-        if mode == "first":
-            d1 = d1 + more
-        else:
-            d2 = d2 + more
-        pack_ref[0:part, :] = d1.astype(bf16)
-        pack_ref[part:, :] = d2.astype(bf16)
     scale_ref[...] = jnp.sum(prod.reshape(part // 8, 8, prod.shape[1]), axis=0)
+
+
+def relay_kernel(direct_ref, base_ref, more_ref, pack_ref):
+    part = direct_ref.shape[0]
+    pack_ref[0:part, :] = direct_ref[...]
+    pack_ref[part:, :] = (base_ref[...] + more_ref[...].astype(f32)).astype(bf16)
 
 
 def back_kernel(gn_ref, normed_ref, rstd_ref, vecs_ref, g_ref, wexp, gi_ref, gd_ref, sums_ref):
@@ -276,10 +268,24 @@
             small_ref[pl.ds(taps + 5 + lax.bitwise_xor(chip, k), 1), :] = bsums[k][0:1, :]
 
 
-def merge_kernel(o1_ref, o2_ref, x_ref, y_ref, out1_ref, out2_ref, *, factor):
-    part = o1_ref.shape[0]
-    out1_ref[...] = (o1_ref[...] + x_ref[0:part, :].astype(f32) + y_ref[0:part, :].astype(f32)) * factor
-    out2_ref[...] = ((o2_ref[...] + x_ref[part:, :].astype(f32) + y_ref[part:, :].astype(f32)) * factor).T
+def merge_kernel(o1_ref, o2_ref, x_ref, y_ref, all_ref, gi_ref,
+                 out1_ref, out2_ref, bias_ref, small_ref, recv_hbm, stage_ref, sem, *, factor):
+    part, chans = o1_ref.shape
+    move = pltpu.make_async_copy(gi_ref, recv_hbm, sem)
+    move.start()
+    out1_ref[...] = (o1_ref[...] + x_ref[0:part, :].astype(f32) + y_ref[part:, :].astype(f32)) * factor
+    out2_ref[...] = ((o2_ref[...] + x_ref[part:, :].astype(f32) + y_ref[0:part, :].astype(f32)) * factor).T
+    total = all_ref[0].astype(f32)
+    for k in range(1, all_ref.shape[0]):
+        total = total + all_ref[k].astype(f32)
+    total = total * factor
+    rows = small_ref.shape[0]
+    stage_ref[...] = total
+    for k in range(rows):
+        small_ref[k] = stage_ref[k : k + 1, :]
+    for k in range(bias_ref.shape[1] // chans):
+        bias_ref[:, k * chans : (k + 1) * chans] = stage_ref[rows + k : rows + k + 1, :]
+    move.wait()
 
 
 def shifted(block, axis, distance):
@@ -350,29 +356,34 @@
         acts_s = swap(acts, 1, replicas)
 
         def share(k, keep, got, types):
-            outs = (struct((part, chans), types), struct((part, chans), types), struct((8, chans), f32))
-            return call(lambda *refs: share_kernel(*refs, slot=flip(k), mode="split"), outs,
+            outs = (struct((part, chans), types[0]), struct((part, chans), types[1]), struct((8, chans), f32))
+            return call(lambda *refs: share_kernel(*refs, slot=flip(k)), outs,
                         w2, acts, acts_s, keep, got, name="share", cost=estimate(1e6, 1e3))
-
-        def share_pack(k, keep, got, more, mode):
-            outs = (struct((wide, chans), bf16), struct((8, chans), f32))
-            return call(lambda *refs: share_kernel(*refs, slot=flip(k), mode=mode), outs,
-                        w2, acts, acts_s, keep, got, more, name="pack", cost=estimate(1e10, 1e6))
 
         gn, bd, keep_d, send_d = wide_step(flip(3), None)
         got_d = swap(send_d, 1, replicas)
+        d1, d2, sc_d = share(3, keep_d, got_d, (bf16, bf16))
+        gn, d1, d2 = lax.optimization_barrier((gn, d1, d2))
+        d1_in, d2_in = swap(d1, 2, replicas), swap(d2, 4, replicas)
         gn, bx, keep_x, send_x = wide_step(flip(1), gn)
         got_x = swap(send_x, 1, replicas)
-        d1, d2, sc_d = share(3, keep_d, got_d, bf16)
-        gn, d1, d2 = lax.optimization_barrier((gn, d1, d2))
-        d1_in, d2_in = swap(d1, 2, replicas), swap(d2, 4, replicas)
         gn, by, keep_y, send_y = wide_step(flip(2), gn)
         got_y = swap(send_y, 1, replicas)
         gn, bo, keep_o, send_o = wide_step(flip(0), gn)
         got_o = swap(send_o, 1, replicas)
-        pack_x, sc_x = share_pack(1, keep_x, got_x, d2_in, "second")
-        gn, pack_x, d1_in = lax.optimization_barrier((gn, pack_x, d1_in))
-        pack_y, sc_y = share_pack(2, keep_y, got_y, d1_in, "first")
+        gn, got_x = lax.optimization_barrier((gn, got_x))
+        x1, x2, sc_x = share(1, keep_x, got_x, (bf16, f32))
+        x1, got_y = lax.optimization_barrier((x1, got_y))
+        y1, y2, sc_y = share(2, keep_y, got_y, (f32, bf16))
+        x1, x2, y1, y2, d1_in, d2_in = lax.optimization_barrier((x1, x2, y1, y2, d1_in, d2_in))
+
+        def relay(direct, base, more):
+            return call(relay_kernel, struct((wide, chans), bf16), direct, base, more,
+                        name="relay", cost=estimate(1e6, 1e3))
+
+        pack_x = relay(x1, x2, d2_in)
+        y2, pack_x = lax.optimization_barrier((y2, pack_x))
+        pack_y = relay(y2, y1, d1_in)
         gn, pack_y = lax.optimization_barrier((gn, pack_y))
         x_in, y_in = swap(pack_x, 2, replicas), swap(pack_y, 4, replicas)
     else:
@@ -392,10 +403,12 @@
         gn, normed, rstd, vecs, gv, wexp,
         name="back", cost=estimate(1e6, 1e3),
     )
+    if fast:
+        gi, got_o = lax.optimization_barrier((gi, got_o))
     received = shifted(gi, "section", -1)
 
     if fast:
-        o1, o2, sc_o = share(0, keep_o, got_o, f32)
+        o1, o2, sc_o = share(0, keep_o, got_o, (f32, f32))
         more = (sc_d, sc_x, sc_y, sc_o, bo, bx, by, bd)
     else:
         more = ()
@@ -404,12 +417,19 @@
                  xp, gd, vecs, sums, *more, name="taps", cost=estimate(1e6, 1e3))
 
     if fast:
-        small = jnp.sum(lax.all_gather(small.astype(bf16), "dp").astype(f32), axis=0)
-        out1, out2 = call(
+        every = lax.all_gather(small.astype(bf16), "dp")
+        vmem = pl.BlockSpec(memory_space=pltpu.VMEM)
+        out1, out2, bias, small, received = pl.pallas_call(
             lambda *refs: merge_kernel(*refs, factor=factor),
-            (struct((part, chans), f32), struct((chans, part), f32)),
-            o1, o2, x_in, y_in, name="merge", cost=estimate(1e10, 1e6),
-        )
+            out_shape=(struct((part, chans), f32), struct((chans, part), f32), struct((1, units), f32),
+                       struct((taps + 5, 1, chans), f32), like(gi)),
+            in_specs=[vmem] * 6,
+            out_specs=(vmem,) * 4 + (pl.BlockSpec(memory_space=pltpu.HBM),),
+            scratch_shapes=[pltpu.VMEM((total_rows, chans), f32), pltpu.SemaphoreType.DMA],
+            compiler_params=pltpu.CompilerParams(vmem_limit_bytes=VMEM_LIMIT),
+            name="merge",
+        )(o1, o2, x_in, y_in, every, received)
+        small = jnp.transpose(small, (1, 0, 2))
     else:
         scale_sum = jnp.sum(g2 * w2.astype(f32), axis=1)
         gscale = scale_sum / layer_scale[0] + pw2_bias[0] * vecs[4]
@@ -417,14 +437,9 @@
         small = lax.psum(small, "dp")
         out1 = lax.psum_scatter(g1, "dp", scatter_dimension=0, tiled=True) * factor
         out2 = lax.psum_scatter(g2, "dp", scatter_dimension=1, tiled=True) * factor
-    small = small * factor
-    return (
-        out1[None],
-        out2[None],
-        small[taps + 5 : taps + 5 + units // chans].reshape(1, -1),
-        small[None, : taps + 5],
-        received[None, None],
-    )
+        small = small * factor
+        bias, small = small[taps + 5 :].reshape(1, -1), small[None, : taps + 5]
+    return (out1[None], out2[None], bias, small, received[None, None])
 
 
 def solution(mesh):

time: 79.2 us -> 70.5 us (0.89)
  Pallas kernels: 45.5 us -> 40.2 us
  local copies, waits for them, and re-layouts: 2.29 us -> 0 us
  starting transfers between devices: 10.5 us -> 8.97 us
  waiting for transfers between devices: 3.46 us -> 4.44 us
    pallas_call x12 -> x13, Pallas kernels: 45.5 us -> 37.8 us  [call(): pl.pallas_call(body, out_shape=out_shape, in_specs=specs, out_specs=jax.t...]
    pallas_call x0 -> x1, Pallas kernels: none -> 2.37 us  [shards(): pl.pallas_call(lambda *refs: merge_kernel(*refs, factor=factor), out_shap...]
    ppermute x9, starting transfers between devices: 9.25 us -> 7.68 us  [swap(): return lax.ppermute(value, 'dp', [(i, i ^ bit) for i in range(count)])]
    unnamed x3 -> x0, local copies, waits for them, and re-layouts: 1.5 us -> none
    ppermute x9, waiting for transfers between devices: 3.46 us -> 4.43 us  [swap(): return lax.ppermute(value, 'dp', [(i, i ^ bit) for i in range(count)])]
  transfers between devices with their start and end apart: 10 -> 10, of which waited for: 1 -> 3; matrix products, arithmetic and copies ran while one was open for 2% -> 0% of each run, Pallas kernels for 44% -> 40%
where the time goes in v4:
time: 70.5 us; the launch traced here: 70.3 us
  Pallas kernels  40.2 us (57%)
  blocking collectives  15.8 us (22%)
  starting transfers between devices  8.97 us (13%)
  waiting for transfers between devices  4.44 us (6%)
  between operations  0.94 us (1%)
    pallas_call x13, Pallas kernels, call(): pl.pallas_call(body, out_shape=out_shape, in_specs=specs, out_specs=jax.t...  37.8 us
    all_gather x1, blocking collectives, shards(): every = lax.all_gather(small.astype(bf16), 'dp')  15.8 us
    ppermute x9, starting transfers between devices, swap(): return lax.ppermute(value, 'dp', [(i, i ^ bit) for i in range(count)])  7.68 us
    ppermute x9, waiting for transfers between devices, swap(): return lax.ppermute(value, 'dp', [(i, i ^ bit) for i in range(count)])  4.43 us
    pallas_call x1, Pallas kernels, shards(): pl.pallas_call(lambda *refs: merge_kernel(*refs, factor=factor), out_shap...  2.37 us
  transfers between devices with their start and end apart: 10, of which 3 were waited for; matrix products, arithmetic and copies ran while one was open for 0% of the time, Pallas kernels for 40%

profile of v4, /device:TPU:0, one launch (start us, length us, event | category | flops | bytes accessed | tf_op | source)
XLA Modules:
  0.0 70.3 jit_solution(10896907618101987343)
XLA Ops:
  0.6 8.4 %front.1 = (bf16[1024,768]{1,0:T(8,128)(2,1)S(1)}, f32[512,768]{1,0:T(8,128)S(1)}, f32[512,128]{1,0:T(8,128)S(1)}, f32[6,8,80,128]{3,2,1,0:T(8,128)S(1)}, f32[8,...) custom-call(bf16[8,64,768]{2,1,0:T(8,128)(2,1)} %bitcast.15, ...), custom_call_target="tpu_custom_call" | custom-call | flops 10000000000 | bytes 1000000 | tf_op jit(solution)/shard_map/front/pallas_call | solution.py:25
  9.1 0.5 collective-permute-start
  9.6 2.6 %wide.4 = (f32[512,768]{1,0:T(8,128)S(1)}, f32[8,768]{1,0:T(8,128)S(1)}, bf16[768,512]{1,0:T(8,128)(2,1)S(1)}, bf16[768,512]{1,0:T(8,128)(2,1)S(1)}) custom-call(bf16[1024,768]{1,0:T(8,128)(2,1)S(1)} %get-tuple-element.71.refs_0_.refs_1_, bf16[3072,768]{1,0:T(8,128)(2,1)S(1)} %get-tuple-element.72.refs_1_, f32[1,3072]{1,0:T(1,128)S(1)} %get-tuple-element.73.refs_2_, ...), custom_call_target="tpu_custom_call" | custom-call | flops 10000000000 | bytes 1000000 | tf_op jit(solution)/shard_map/wide/pallas_call | solution.py:25
  12.1 0.1 collective-permute-start.1
  12.3 2.2 %collective-permute-done.1.refs_4_ = bf16[768,512]{1,0:T(8,128)(2,1)S(1)} collective-permute-done((bf16[768,512]{1,0:T(8,128)(2,1)S(1)}, bf16[768,512]{1,0:T(8,128)(2,1)S(1)}, u32[]{:S(2)}, u32[]{:S(2)}) %collective-permute-start.1) | collective-permute-done | bytes 786464 | tf_op jit(solution)/shard_map/ppermute | solution.py:298
  14.5 0.0 collective-permute-done.refs_2_
  14.5 1.4 %share.4 = (bf16[384,768]{1,0:T(8,128)(2,1)S(1)}, bf16[384,768]{1,0:T(8,128)(2,1)S(1)}, f32[8,768]{1,0:T(8,128)S(1)}) custom-call(bf16[768,3072]{1,0:T(8,128)(2,1)S(1)} %get-tuple-element.70.refs_3_.refs_0_, bf16[1024,768]{1,0:T(8,128)(2,1)S(1)} %get-tuple-element.71.refs_0_.refs_1_, bf16[1024,768]{1,0:T(8,128)(2,1)S(1)} %collective-permute-done.refs_2_, ...), custom_call_target="tpu_custom_call" | custom-call | flops 1000000 | bytes 1000 | tf_op jit(solution)/shard_map/share/pallas_call | solution.py:25
  15.9 2.7 %collective-permute-start.4 = (bf16[384,768]{1,0:T(8,128)(2,1)S(1)}, bf16[384,768]{1,0:T(8,128)(2,1)S(1)}, u32[]{:S(2)}, u32[]{:S(2)}) collective-permute-start(bf16[384,768]{1,0:T(8,128)(2,1)S(1)} %get-tuple-element.96), channel_id=1, source_target_pairs={{0,2},{1,3},{2,0},{3,1},{4,6},{5,7},{6,4},{7,5},{8,10},{9,11},{10,... | collective-permute-start | bytes 1769480 | tf_op jit(solution)/shard_map/ppermute | solution.py:298
  18.6 1.5 %collective-permute-start.5 = (bf16[384,768]{1,0:T(8,128)(2,1)S(1)}, bf16[384,768]{1,0:T(8,128)(2,1)S(1)}, u32[]{:S(2)}, u32[]{:S(2)}) collective-permute-start(bf16[384,768]{1,0:T(8,128)(2,1)S(1)} %get-tuple-element.97), channel_id=1, source_target_pairs={{0,4},{1,5},{2,6},{3,7},{4,0},{5,1},{6,2},{7,3},{8,12},{9,13},{10,... | collective-permute-start | bytes 1769480 | tf_op jit(solution)/shard_map/ppermute | solution.py:298
  20.1 2.6 %wide.5 = (f32[512,768]{1,0:T(8,128)S(1)}, f32[8,768]{1,0:T(8,128)S(1)}, bf16[768,512]{1,0:T(8,128)(2,1)S(1)}, bf16[768,512]{1,0:T(8,128)(2,1)S(1)}) custom-call(bf16[1024,768]{1,0:T(8,128)(2,1)S(1)} %get-tuple-element.71.refs_0_.refs_1_, bf16[3072,768]{1,0:T(8,128)(2,1)S(1)} %get-tuple-element.72.refs_1_, ...), custom_call_target="tpu_custom_call", output_to_operand_aliasing={{0}: (4, {})} | custom-call | flops 10000000000 | bytes 1000000 | tf_op jit(solution)/shard_map/wide/pallas_call | solution.py:25
  22.7 0.1 collective-permute-start.2
  22.8 2.6 %wide.6 = (f32[512,768]{1,0:T(8,128)S(1)}, f32[8,768]{1,0:T(8,128)S(1)}, bf16[768,512]{1,0:T(8,128)(2,1)S(1)}, bf16[768,512]{1,0:T(8,128)(2,1)S(1)}) custom-call(bf16[1024,768]{1,0:T(8,128)(2,1)S(1)} %get-tuple-element.71.refs_0_.refs_1_, bf16[3072,768]{1,0:T(8,128)(2,1)S(1)} %get-tuple-element.72.refs_1_, ...), custom_call_target="tpu_custom_call", output_to_operand_aliasing={{0}: (4, {})} | custom-call | flops 10000000000 | bytes 1000000 | tf_op jit(solution)/shard_map/wide/pallas_call | solution.py:25
  25.5 0.5 collective-permute-start.3
  26.0 2.8 %wide.7 = (f32[512,768]{1,0:T(8,128)S(1)}, f32[8,768]{1,0:T(8,128)S(1)}, bf16[768,512]{1,0:T(8,128)(2,1)S(1)}, bf16[768,512]{1,0:T(8,128)(2,1)S(1)}) custom-call(bf16[1024,768]{1,0:T(8,128)(2,1)S(1)} %get-tuple-element.71.refs_0_.refs_1_, bf16[3072,768]{1,0:T(8,128)(2,1)S(1)} %get-tuple-element.72.refs_1_, ...), custom_call_target="tpu_custom_call", output_to_operand_aliasing={{0}: (4, {})} | custom-call | flops 10000000000 | bytes 1000000 | tf_op jit(solution)/shard_map/wide/pallas_call | solution.py:25
  28.8 0.1 collective-permute-start.6
  28.9 0.0 collective-permute-done.2.refs_4_
  28.9 1.4 %share.5 = (bf16[384,768]{1,0:T(8,128)(2,1)S(1)}, f32[384,768]{1,0:T(8,128)S(1)}, f32[8,768]{1,0:T(8,128)S(1)}) custom-call(bf16[768,3072]{1,0:T(8,128)(2,1)S(1)} %get-tuple-element.70.refs_3_.refs_0_, bf16[1024,768]{1,0:T(8,128)(2,1)S(1)} %get-tuple-element.71.refs_0_.refs_1_, bf16[1024,768]{1,0:T(8,128)(2,1)S(1)} %collective-permute-done.refs_2_, ...), custom_call_target="tpu_custom_call" | custom-call | flops 1000000 | bytes 1000 | tf_op jit(solution)/shard_map/share/pallas_call | solution.py:25
  30.3 1.4 %share.6 = (f32[384,768]{1,0:T(8,128)S(1)}, bf16[384,768]{1,0:T(8,128)(2,1)S(1)}, f32[8,768]{1,0:T(8,128)S(1)}) custom-call(bf16[768,3072]{1,0:T(8,128)(2,1)S(1)} %get-tuple-element.70.refs_3_.refs_0_, bf16[1024,768]{1,0:T(8,128)(2,1)S(1)} %get-tuple-element.71.refs_0_.refs_1_, bf16[1024,768]{1,0:T(8,128)(2,1)S(1)} %collective-permute-done.refs_2_, ...), custom_call_target="tpu_custom_call" | custom-call | flops 1000000 | bytes 1000 | tf_op jit(solution)/shard_map/share/pallas_call | solution.py:25
  31.7 0.7 %collective-permute-done.4.more_ref = bf16[384,768]{1,0:T(8,128)(2,1)S(1)} collective-permute-done((bf16[384,768]{1,0:T(8,128)(2,1)S(1)}, bf16[384,768]{1,0:T(8,128)(2,1)S(1)}, u32[]{:S(2)}, u32[]{:S(2)}) %collective-permute-start.4) | collective-permute-done | bytes 589856 | tf_op jit(solution)/shard_map/ppermute | solution.py:298
  32.5 1.5 %collective-permute-done.5.more_ref = bf16[384,768]{1,0:T(8,128)(2,1)S(1)} collective-permute-done((bf16[384,768]{1,0:T(8,128)(2,1)S(1)}, bf16[384,768]{1,0:T(8,128)(2,1)S(1)}, u32[]{:S(2)}, u32[]{:S(2)}) %collective-permute-start.5) | collective-permute-done | bytes 589856 | tf_op jit(solution)/shard_map/ppermute | solution.py:298
  33.9 0.2 relay.2
  34.1 0.2 relay.3
  34.3 1.6 %collective-permute-start.8 = (bf16[768,768]{1,0:T(8,128)(2,1)S(1)}, bf16[768,768]{1,0:T(8,128)(2,1)S(1)}, u32[]{:S(2)}, u32[]{:S(2)}) collective-permute-start(bf16[768,768]{1,0:T(8,128)(2,1)S(1)} %relay.3), channel_id=1, source_target_pairs={{0,4},{1,5},{2,6},{3,7},{4,0},{5,1},{6,2},{7,3},{8,12},{9,13},{10,... | collective-permute-start | bytes 3538952 | tf_op jit(solution)/shard_map/ppermute | solution.py:298
  35.8 0.5 collective-permute-start.7
  36.4 7.1 %back.1 = (bf16[8,64,768]{2,1,0:T(8,128)(2,1)S(1)}, f32[6,8,80,128]{3,2,1,0:T(8,128)S(1)}, f32[8,768]{1,0:T(8,128)S(1)}) custom-call(f32[512,768]{1,0:T(8,128)S(1)} %get-tuple-element.105.gn_ref, f32[512,768]{1,0:T(8,128)S(1)} %get-tuple-element.106.normed_ref, f32[512,128]{1,0:T(8,128)S(1)} %get-tuple-element.107.rstd_ref, ...), custom_call_target="tpu_custom_call" | custom-call | flops 1000000 | bytes 1000 | tf_op jit(solution)/shard_map/back/pallas_call | solution.py:25
  43.5 1.3 %collective-permute-start.9 = (bf16[8,64,768]{2,1,0:T(8,128)(2,1)S(1)}, bf16[8,64,768]{2,1,0:T(8,128)(2,1)S(1)}, u32[]{:S(2)}, u32[]{:S(2)}) collective-permute-start(bf16[8,64,768]{2,1,0:T(8,128)(2,1)S(1)} %get-tuple-element.129), channel_id=1, source_target_pairs={{8,0},{16,8},{24,16},{9,1},{17,9},{25,17},{10,2},{18,10},{26,18},{... | collective-permute-start | bytes 2359304 | tf_op jit(solution)/shard_map/ppermute | solution.py:294
  44.8 1.4 %share.7 = (f32[384,768]{1,0:T(8,128)S(1)}, f32[384,768]{1,0:T(8,128)S(1)}, f32[8,768]{1,0:T(8,128)S(1)}) custom-call(bf16[768,3072]{1,0:T(8,128)(2,1)S(1)} %get-tuple-element.70.refs_3_.refs_0_, bf16[1024,768]{1,0:T(8,128)(2,1)S(1)} %get-tuple-element.71.refs_0_.refs_1_, bf16[1024,768]{1,0:T(8,128)(2,1)S(1)} %collective-permute-done.refs_2_, ...), custom_call_target="tpu_custom_call" | custom-call | flops 1000000 | bytes 1000 | tf_op jit(solution)/shard_map/share/pallas_call | solution.py:25
  46.2 5.8 %taps.1 = f32[64,768]{1,0:T(8,128)S(1)} custom-call(f32[6,8,80,128]{3,2,1,0:T(8,128)S(1)} %get-tuple-element.118.refs_0_, f32[6,8,80,128]{3,2,1,0:T(8,128)S(1)} %get-tuple-element.119.refs_1_, f32[8,768]{1,0:T(8,128)S(1)} %get-tuple-element.108.vecs_ref.refs_2_, f32[8,768]{1,0:T(8,128)S(1)} %get-tuple-element.120.refs_3_, ...), custom_call_target="tpu_custom_call" | custom-call | flops 1000000 | bytes 1000 | tf_op jit(solution)/shard_map/taps/pallas_call | solution.py:25
  52.0 15.8 %all-gather = bf16[512,768]{1,0:T(8,128)(2,1)S(1)} all-gather(bf16[64,768]{1,0:T(8,128)(2,1)S(1)} %convert_element_type.3), channel_id=2, replica_groups=mesh['section'=4,'dp'=8] {'dp'}, dimensions={0}, use_global_device_ids=true | all-gather | bytes 884736 | tf_op jit(solution)/shard_map/all_gather | solution.py:420
  67.8 0.0 collective-permute-done.9.refs_5_
  67.8 0.0 collective-permute-done.8.refs_3_
  67.8 2.4 %merge.1 = (f32[384,768]{1,0:T(8,128)}, f32[768,384]{1,0:T(8,128)}, f32[1,3072]{1,0:T(1,128)}, f32[54,1,768]{2,1,0:T(1,128)}, bf16[8,64,768]{2,1,0:T(8,128)(2,1)}) custom-call(f32[384,768]{1,0:T(8,128)S(1)} %get-tuple-element.114.refs_0_, f32[384,768]{1,0:T(8,128)S(1)} %get-tuple-element.115.refs_1_, bf16[768,768]{1,0:T(8,128)(2,1)S(1)} %collective-permute-done.7.refs_2_, ...), custom_call_target="tpu_custom_call" | custom-call | tf_op jit(solution)/shard_map/merge/pallas_call | solution.py:422
  (4 shorter events, 0.0 us)
Async XLA Ops:
  9.1 5.4 %collective-permute-start = (bf16[1024,768]{1,0:T(8,128)(2,1)S(1)}, bf16[1024,768]{1,0:T(8,128)(2,1)S(1)}, u32[]{:S(2)}, u32[]{:S(2)}) collective-permute-start(bf16[1024,768]{1,0:T(8,128)(2,1)S(1)} %get-tuple-element.71.refs_0_.refs_1_), channel_id=1, source_target_pairs={{0,1},{1,0},{2,3},{3,2},{4,5},{5,4},{6,7},{7,6},{8,9},{9,8},{10,11... | collective-permute-start | bytes 4718600 | tf_op jit(solution)/shard_map/ppermute | solution.py:298
  12.1 2.4 %collective-permute-start.1 = (bf16[768,512]{1,0:T(8,128)(2,1)S(1)}, bf16[768,512]{1,0:T(8,128)(2,1)S(1)}, u32[]{:S(2)}, u32[]{:S(2)}) collective-permute-start(bf16[768,512]{1,0:T(8,128)(2,1)S(1)} %get-tuple-element.76), channel_id=1, source_target_pairs={{0,1},{1,0},{2,3},{3,2},{4,5},{5,4},{6,7},{7,6},{8,9},{9,8},{10,11... | collective-permute-start | bytes 2359304 | tf_op jit(solution)/shard_map/ppermute | solution.py:298
  15.9 16.6 %collective-permute-start.4 = (bf16[384,768]{1,0:T(8,128)(2,1)S(1)}, bf16[384,768]{1,0:T(8,128)(2,1)S(1)}, u32[]{:S(2)}, u32[]{:S(2)}) collective-permute-start(bf16[384,768]{1,0:T(8,128)(2,1)S(1)} %get-tuple-element.96), channel_id=1, source_target_pairs={{0,2},{1,3},{2,0},{3,1},{4,6},{5,7},{6,4},{7,5},{8,10},{9,11},{10,... | collective-permute-start | bytes 1769480 | tf_op jit(solution)/shard_map/ppermute | solution.py:298
  18.6 15.3 %collective-permute-start.5 = (bf16[384,768]{1,0:T(8,128)(2,1)S(1)}, bf16[384,768]{1,0:T(8,128)(2,1)S(1)}, u32[]{:S(2)}, u32[]{:S(2)}) collective-permute-start(bf16[384,768]{1,0:T(8,128)(2,1)S(1)} %get-tuple-element.97), channel_id=1, source_target_pairs={{0,4},{1,5},{2,6},{3,7},{4,0},{5,1},{6,2},{7,3},{8,12},{9,13},{10,... | collective-permute-start | bytes 1769480 | tf_op jit(solution)/shard_map/ppermute | solution.py:298
  22.7 6.2 %collective-permute-start.2 = (bf16[768,512]{1,0:T(8,128)(2,1)S(1)}, bf16[768,512]{1,0:T(8,128)(2,1)S(1)}, u32[]{:S(2)}, u32[]{:S(2)}) collective-permute-start(bf16[768,512]{1,0:T(8,128)(2,1)S(1)} %get-tuple-element.84), channel_id=1, source_target_pairs={{0,1},{1,0},{2,3},{3,2},{4,5},{5,4},{6,7},{7,6},{8,9},{9,8},{10,11... | collective-permute-start | bytes 2359304 | tf_op jit(solution)/shard_map/ppermute | solution.py:298
  25.5 4.8 %collective-permute-start.3 = (bf16[768,512]{1,0:T(8,128)(2,1)S(1)}, bf16[768,512]{1,0:T(8,128)(2,1)S(1)}, u32[]{:S(2)}, u32[]{:S(2)}) collective-permute-start(bf16[768,512]{1,0:T(8,128)(2,1)S(1)} %get-tuple-element.89), channel_id=1, source_target_pairs={{0,1},{1,0},{2,3},{3,2},{4,5},{5,4},{6,7},{7,6},{8,9},{9,8},{10,11... | collective-permute-start | bytes 2359304 | tf_op jit(solution)/shard_map/ppermute | solution.py:298
  28.8 14.6 %collective-permute-start.6 = (bf16[768,512]{1,0:T(8,128)(2,1)S(1)}, bf16[768,512]{1,0:T(8,128)(2,1)S(1)}, u32[]{:S(2)}, u32[]{:S(2)}) collective-permute-start(bf16[768,512]{1,0:T(8,128)(2,1)S(1)} %get-tuple-element.112), channel_id=1, source_target_pairs={{0,1},{1,0},{2,3},{3,2},{4,5},{5,4},{6,7},{7,6},{8,9},{9,8},{10,11... | collective-permute-start | bytes 2359304 | tf_op jit(solution)/shard_map/ppermute | solution.py:298
  34.3 33.5 %collective-permute-start.8 = (bf16[768,768]{1,0:T(8,128)(2,1)S(1)}, bf16[768,768]{1,0:T(8,128)(2,1)S(1)}, u32[]{:S(2)}, u32[]{:S(2)}) collective-permute-start(bf16[768,768]{1,0:T(8,128)(2,1)S(1)} %relay.3), channel_id=1, source_target_pairs={{0,4},{1,5},{2,6},{3,7},{4,0},{5,1},{6,2},{7,3},{8,12},{9,13},{10,... | collective-permute-start | bytes 3538952 | tf_op jit(solution)/shard_map/ppermute | solution.py:298
  35.8 32.0 %collective-permute-start.7 = (bf16[768,768]{1,0:T(8,128)(2,1)S(1)}, bf16[768,768]{1,0:T(8,128)(2,1)S(1)}, u32[]{:S(2)}, u32[]{:S(2)}) collective-permute-start(bf16[768,768]{1,0:T(8,128)(2,1)S(1)} %relay.2), channel_id=1, source_target_pairs={{0,2},{1,3},{2,0},{3,1},{4,6},{5,7},{6,4},{7,5},{8,10},{9,11},{10,... | collective-permute-start | bytes 3538952 | tf_op jit(solution)/shard_map/ppermute | solution.py:298
  43.5 24.3 %collective-permute-start.9 = (bf16[8,64,768]{2,1,0:T(8,128)(2,1)S(1)}, bf16[8,64,768]{2,1,0:T(8,128)(2,1)S(1)}, u32[]{:S(2)}, u32[]{:S(2)}) collective-permute-start(bf16[8,64,768]{2,1,0:T(8,128)(2,1)S(1)} %get-tuple-element.129), channel_id=1, source_target_pairs={{8,0},{16,8},{24,16},{9,1},{17,9},{25,17},{10,2},{18,10},{26,18},{... | collective-permute-start | bytes 2359304 | tf_op jit(solution)/shard_map/ppermute | solution.py:294

commit v5 on v4

v5 whole, which is shorter than its diff:
```python
import jax
import jax.numpy as jnp
from jax import lax
from jax.experimental import pallas as pl
from jax.experimental.pallas import tpu as pltpu
from jax.sharding import PartitionSpec as P

root_half = 0.7071067811865476
inv_root_two_pi = 0.3989422804014327
f32 = jnp.float32
bf16 = jnp.bfloat16
LANES = 128
EDGE = 8
VMEM_LIMIT = 12 * 1024 * 1024


def struct(shape, dtype):
    return jax.ShapeDtypeStruct(shape, dtype)


def call(body, out_shape, *args, name, aliases=None, scratch=(), scalars=0, in_specs=None, cost=None):
    vmem = pl.BlockSpec(memory_space=pltpu.VMEM)
    smem = pl.BlockSpec(memory_space=pltpu.SMEM)
    specs = [smem] * scalars + [vmem] * (len(args) - scalars) if in_specs is None else in_specs
    return pl.pallas_call(
        body,
        out_shape=out_shape,
        in_specs=specs,
        out_specs=jax.tree.map(lambda _: vmem, out_shape),
        scratch_shapes=list(scratch),
        input_output_aliases=aliases or {},
        compiler_params=pltpu.CompilerParams(vmem_limit_bytes=VMEM_LIMIT),
        cost_estimate=cost,
        name=name,
    )(*args)


def estimate(flops, nbytes):
    return pl.CostEstimate(flops=int(flops), transcendentals=0, bytes_accessed=int(nbytes))


def dot(a, b):
    return jnp.dot(a, b, preferred_element_type=f32)


def dot_last(a, b):
    return lax.dot_general(a, b, (((1,), (1,)), ((), ())), preferred_element_type=f32)


def place():
    me = lax.axis_index("dp")
    return lax.shift_right_logical(me, 1), lax.bitwise_and(me, 1)


def expand_taps(w_ref, wexp, blocks):
    count = w_ref.shape[0]
    for c in range(blocks):
        rows = [w_ref[k : k + 1, c * LANES : (c + 1) * LANES].astype(f32) for k in range(count)]
        for k in range(count):
            wexp[c, k] = jnp.broadcast_to(rows[k], (8, LANES))
        for i in range(6):
            for j in range(7):
                wexp[c, count + 7 * i + j] = jnp.broadcast_to(rows[7 * i + j] + rows[7 * i + 7 + j], (8, LANES))


def zero_edges(buf, blocks, rows, cols):
    zero = jnp.zeros((rows, EDGE, LANES), f32)
    for c in range(blocks):
        buf[c, :, 0:EDGE, :] = zero
        buf[c, :, EDGE + cols : EDGE + cols + EDGE, :] = zero


def conv_block(src, c, wexp, rows, start, width, flip):
    groups = width // 8
    pairs = rows // 2
    tap = lambda k: 3 - k if flip else k + 3
    lone = lambda k, j: wexp[c, 7 * tap(k) + j]
    both = lambda k, j: wexp[c, 49 + 7 * min(tap(k), tap(k + 1)) + j]
    odd, even, mixed = [None] * pairs, [None] * (pairs + 1), [None] * pairs

    def put(acc, a, term):
        acc[a] = term if acc[a] is None else acc[a] + term

    for j in range(7):
        at = start + EDGE + (3 - j if flip else j - 3)
        for b in range(pairs):
            x0, x1 = (src[c, 2 * b + k, at : at + width, :].reshape(groups, 8, LANES) for k in range(2))
            for d in range(-1, 2):
                if 0 <= b - d < pairs:
                    put(odd, b - d, x1 * lone(2 * d, j))
            for d in range(-2, 2):
                if 0 <= b - d <= pairs:
                    put(even, b - d, x0 * lone(2 * d + 1, j))
            x0 = x0 + x1
            for d in range(-2, 2):
                if 0 <= b - d < pairs:
                    put(mixed, b - d, x0 * (lone(-3, j) if d == -2 else both(2 * d, j)))
    acc = []
    for a in range(pairs):
        acc += [mixed[a] - odd[a] - even[a], odd[a] + even[a + 1]]
    return acc


def load_kernel(x_hbm, g_hbm, w_hbm, db_hbm, gain_hbm, shift_hbm, scale_hbm, bb_hbm,
                gp_ref, xp_ref, vecs_ref, wexp, g_ref, tmp_ref, x_ref, w_ref, sems):
    rows, cols, chans = x_ref.shape
    blocks = chans // LANES
    moves = [(w_hbm, w_ref), (scale_hbm, tmp_ref.at[3:4]), (g_hbm, g_ref), (x_hbm, x_ref), (db_hbm, tmp_ref.at[0:1]),
             (gain_hbm, tmp_ref.at[1:2]), (shift_hbm, tmp_ref.at[2:3]), (bb_hbm, tmp_ref.at[4:5])]
    copies = [pltpu.make_async_copy(src, dst, sems.at[k]) for k, (src, dst) in enumerate(moves)]
    for copy in copies:
        copy.start()
    zero_edges(xp_ref, blocks, rows, cols)
    copies[0].wait()
    expand_taps(w_ref, wexp, blocks)
    copies[1].wait()
    copies[2].wait()
    b2, gs = [], []
    for c in range(blocks):
        lanes = slice(c * LANES, (c + 1) * LANES)
        g = g_ref[:, :, lanes].astype(f32).reshape(rows * cols, LANES)
        gp = (g * tmp_ref[3:4, lanes]).astype(bf16)
        gp_ref[:, lanes] = gp
        b2.append(jnp.sum(gp.astype(f32), axis=0, keepdims=True))
        gs.append(jnp.sum(g, axis=0, keepdims=True))
    copies[3].wait()
    for c in range(blocks):
        xp_ref[c, :, EDGE : EDGE + cols, :] = x_ref[:, :, c * LANES : (c + 1) * LANES].astype(f32)
    for copy in copies[4:]:
        copy.wait()
    vecs_ref[0:1, :] = tmp_ref[1:2, :]
    vecs_ref[1:2, :] = tmp_ref[3:4, :]
    vecs_ref[2:3, :] = tmp_ref[4:5, :]
    vecs_ref[3:4, :] = jnp.concatenate(b2, axis=1)
    vecs_ref[4:5, :] = jnp.concatenate(gs, axis=1)
    vecs_ref[5:8, :] = jnp.zeros((3, chans), f32)


def front_kernel(xp_ref, wexp, tmp_ref, w1_hbm, b1_hbm, w2_hbm,
                 yn_ref, normed_ref, rstd_ref, w1_ref, b1_ref, w2_ref, mean_ref, sems):
    blocks, rows, padded, _ = xp_ref.shape
    cols = padded - 2 * EDGE
    chans = blocks * LANES
    half = cols // 4
    moves = [(w1_hbm, w1_ref), (b1_hbm, b1_ref), (w2_hbm, w2_ref)]
    copies = [pltpu.make_async_copy(src, dst, sems.at[k]) for k, (src, dst) in enumerate(moves)]
    for copy in copies:
        copy.start()
    mean_ref[...] = jnp.zeros(mean_ref.shape, f32)

    def conv_step(c, carry):
        lanes = pl.ds(pl.multiple_of(c * LANES, LANES), LANES)
        for part in range(4):
            acc = conv_block(xp_ref, c, wexp, rows, part * half, half, False)
            bias = tmp_ref[0:1, lanes]
            for h in range(rows):
                at = slice(h * cols + part * half, h * cols + part * half + half)
                value = acc[h].reshape(half, LANES) + bias
                normed_ref[at, lanes] = value
                mean_ref[at, :] = mean_ref[at, :] + value
        return carry

    lax.fori_loop(0, blocks, conv_step, 0)
    mean_ref[...] = jnp.broadcast_to(jnp.sum(mean_ref[...], axis=-1, keepdims=True) * (1.0 / chans), mean_ref.shape)

    def spread_step(r, carry):
        at = pl.ds(pl.multiple_of(r * cols, cols), cols)
        mean = mean_ref[at, :]
        total = jnp.zeros((cols, LANES), f32)
        for c in range(blocks):
            d = normed_ref[at, c * LANES : (c + 1) * LANES] - mean
            total = total + d * d
        rstd_ref[at, :] = total
        return carry

    lax.fori_loop(0, rows, spread_step, 0)
    var = jnp.sum(rstd_ref[...], axis=-1, keepdims=True) * (1.0 / chans)
    rstd_ref[...] = jnp.broadcast_to(lax.rsqrt(var + 1e-06), rstd_ref.shape)
    gain, shift = tmp_ref[1:2, :], tmp_ref[2:3, :]

    def norm_step(r, carry):
        at = pl.ds(pl.multiple_of(r * cols, cols), cols)
        mean, rs = mean_ref[at, :], rstd_ref[at, :]
        for c in range(blocks):
            lanes = slice(c * LANES, (c + 1) * LANES)
            normed = (normed_ref[at, lanes] - mean) * rs
            normed_ref[at, lanes] = normed
            yn_ref[at, lanes] = (normed * gain[:, lanes] + shift[:, lanes]).astype(bf16)
        return carry

    lax.fori_loop(0, rows, norm_step, 0)
    for copy in copies:
        copy.wait()


def gate(pre):
    return 0.5 * (1.0 + lax.erf(pre * root_half))


def split_store(core, part, value, keep_ref, send_ref, row):
    for side in range(2):
        @pl.when(core == side)
        def _(side=side):
            k, s = side * part, (1 - side) * part
            keep_ref[row : row + part, :] = value[k : k + part, :]
            send_ref[row : row + part, :] = value[s : s + part, :]


def slope_of(pre, cdf):
    density = jnp.exp(-0.5 * pre * pre) * inv_root_two_pi
    return cdf + pre * density


def open_kernel(yn_ref, w1_ref, b1_ref, rise_ref, keep_ref, send_ref, *, slot):
    wide = rise_ref.shape[1]
    chip, core = place()
    at = pl.multiple_of(slot(chip) * wide, wide)
    pre = dot_last(yn_ref[...], w1_ref[pl.ds(at, wide), :]) + b1_ref[:, pl.ds(at, wide)]
    cdf = gate(pre)
    rise_ref[...] = slope_of(pre, cdf)
    split_store(core, wide // 2, (pre * cdf).astype(bf16).T, keep_ref, send_ref, 0)


def close_kernel(gp_ref, rise_ref, w2_ref, gpre_ref, keep_ref, send_ref, *, slot):
    wide = rise_ref.shape[1]
    chip, core = place()
    at = pl.multiple_of(slot(chip) * wide, wide)
    gpre = (dot(gp_ref[...], w2_ref[:, pl.ds(at, wide)]) * rise_ref[...]).astype(bf16)
    gpre_ref[...] = gpre
    split_store(core, wide // 2, gpre.T, keep_ref, send_ref, 0)


def wide_kernel(yn_ref, gp_ref, w1_ref, b1_ref, w2_ref, *rest, mode, slot, other):
    *more, bsum_ref, keep_ref, send_ref = rest
    wide = bsum_ref.shape[1]
    part = wide // 2
    chip, core = place()
    at = pl.multiple_of(slot(chip) * wide, wide)
    w1 = w1_ref[pl.ds(at, wide), :]
    w2 = w2_ref[:, pl.ds(at, wide)]
    pre = dot_last(yn_ref[...], w1) + b1_ref[:, pl.ds(at, wide)]
    cdf = gate(pre)
    hidden = (pre * cdf).astype(bf16)
    gpre = (dot(gp_ref[...], w2) * slope_of(pre, cdf)).astype(bf16)
    bsum_ref[...] = jnp.broadcast_to(jnp.sum(gpre.astype(f32), axis=0, keepdims=True), (8, wide))
    gn = dot(gpre, w1)
    if mode == "first":
        (gn_ref,) = more
        gn_ref[...] = gn
    elif mode == "next":
        gin_ref, gn_ref = more
        gn_ref[...] = gin_ref[...] + gn
    else:
        gpre_ref, gn_ref, osum_ref = more
        back = pl.multiple_of(other(chip) * wide, wide)
        gn_ref[...] = gn + dot(gpre_ref[...], w1_ref[pl.ds(back, wide), :])
        total = jnp.sum(gpre_ref[...].astype(f32), axis=0, keepdims=True)
        osum_ref[...] = jnp.broadcast_to(total, (8, wide))
    split_store(core, part, gpre.T, keep_ref, send_ref, 0)
    split_store(core, part, hidden.T, keep_ref, send_ref, part)


def half_kernel(own_ref, sib_ref, keep_ref, got_ref, *rest, slot):
    if slot is None:
        (d_ref,) = rest
    else:
        w2_ref, d_ref, scale_ref = rest
    d = dot(keep_ref[...], own_ref[...]) + dot(got_ref[...], sib_ref[...])
    d_ref[...] = d.astype(d_ref.dtype)
    if slot is not None:
        part, chans = d.shape
        chip, core = place()
        at = pl.multiple_of((2 * slot(chip) + core) * part, part)
        prod = d * w2_ref[:, pl.ds(at, part)].T.astype(f32)
        scale_ref[...] = jnp.sum(prod.reshape(part // 8, 8, chans), axis=0)


def share_kernel(w2_ref, yo_ref, ys_ref, go_ref, gs_ref, keep_ref, got_ref, d1_ref, d2_ref, scale_ref, *, slot):
    part = keep_ref.shape[0] // 2
    first, second = slice(0, part), slice(part, 2 * part)
    half_kernel(yo_ref, ys_ref, keep_ref.at[first, :], got_ref.at[first, :], d1_ref, slot=None)
    half_kernel(go_ref, gs_ref, keep_ref.at[second, :], got_ref.at[second, :], w2_ref, d2_ref, scale_ref, slot=slot)


def relay_kernel(direct_ref, base_ref, more_ref, pack_ref):
    part = direct_ref.shape[0]
    pack_ref[0:part, :] = direct_ref[...]
    pack_ref[part:, :] = (base_ref[...] + more_ref[...].astype(f32)).astype(bf16)


def slope_kernel(gn_ref, normed_ref, rstd_ref, vecs_ref, gd_ref, sums_ref):
    blocks, rows, padded, _ = gd_ref.shape
    cols = padded - 2 * EDGE
    chans = blocks * LANES
    zero_edges(gd_ref, blocks, rows, cols)
    gain = vecs_ref[0:1, :]

    def norm_step(r, carry):
        at = pl.ds(pl.multiple_of(r * cols, cols), cols)
        gn = gn_ref[at, :]
        normed = normed_ref[at, :]
        prod = gn * normed
        scaled = gn * gain
        mean_a = jnp.mean(scaled, axis=-1, keepdims=True)
        mean_b = jnp.mean(prod * gain, axis=-1, keepdims=True)
        rs = rstd_ref[at, 0:1]
        gd = rs * (scaled - mean_a - normed * mean_b)
        for c in range(blocks):
            gd_ref[c, r, EDGE : EDGE + cols, :] = gd[:, c * LANES : (c + 1) * LANES]
        fold = lambda v: jnp.sum(v.reshape(cols // 8, 8, chans), axis=0)
        return carry[0] + fold(gd), carry[1] + fold(prod), carry[2] + fold(gn)

    zero = jnp.zeros((8, chans), f32)
    sums = lax.fori_loop(0, rows, norm_step, (zero, zero, zero))
    for k in range(3):
        sums_ref[k : k + 1, :] = jnp.sum(sums[k], axis=0, keepdims=True)
    sums_ref[3:8, :] = jnp.zeros((5, chans), f32)


def back_kernel(gd_ref, g_ref, wexp, gi_ref):
    rows, cols, chans = g_ref.shape
    blocks = chans // LANES
    half = cols // 4

    def conv_step(c, carry):
        lanes = pl.ds(pl.multiple_of(c * LANES, LANES), LANES)
        for part in range(4):
            acc = conv_block(gd_ref, c, wexp, rows, part * half, half, True)
            for h in range(rows):
                span = slice(part * half, part * half + half)
                gi_ref[h, span, lanes] = (g_ref[h, span, lanes].astype(f32) + acc[h].reshape(half, LANES)).astype(bf16)
        return carry

    lax.fori_loop(0, blocks, conv_step, 0)


def tap_kernel(xp_ref, gd_ref, vecs_ref, sums_ref, *rest, taps, fast):
    *more, small_ref = rest
    blocks, rows, padded, _ = xp_ref.shape
    cols = padded - 2 * EDGE
    chans = blocks * LANES

    def step(c, carry):
        lanes = pl.ds(pl.multiple_of(c * LANES, LANES), LANES)
        for j in range(7):
            acc = [None] * 7
            for b in range(0, cols, 16):
                grads = [gd_ref[c, h, EDGE + b : EDGE + b + 16, :].reshape(2, 8, LANES) for h in range(rows)]
                for hp in range(rows):
                    at = EDGE + b + j - 3
                    piece = xp_ref[c, hp, at : at + 16, :].reshape(2, 8, LANES)
                    for h in range(max(0, hp - 3), min(rows, hp + 4)):
                        i = hp - h + 3
                        term = grads[h] * piece
                        term = term[0] + term[1]
                        acc[i] = term if acc[i] is None else acc[i] + term
            for i in range(7):
                small_ref[7 * i + j : 7 * i + j + 1, lanes] = jnp.sum(acc[i], axis=0, keepdims=True)
        return carry

    small_ref[taps:, :] = jnp.zeros((small_ref.shape[0] - taps, chans), f32)
    lax.fori_loop(0, blocks, step, 0)
    small_ref[taps : taps + 3, :] = sums_ref[0:3, :]
    small_ref[taps + 3 : taps + 4, :] = vecs_ref[3:4, :]
    if fast:
        scales, bsums = more[:4], more[4:]
        total = scales[0][...] + scales[1][...] + scales[2][...] + scales[3][...]
        row = jnp.sum(total, axis=0, keepdims=True) / vecs_ref[1:2, :] + vecs_ref[2:3, :] * vecs_ref[4:5, :]
        small_ref[taps + 4 : taps + 5, :] = row
        chip, _ = place()
        for k in range(4):
            small_ref[pl.ds(taps + 5 + lax.bitwise_xor(chip, k), 1), :] = bsums[k][0:1, :]


def merge_kernel(o1_ref, o2_ref, x_ref, y_ref, gi_ref, out1_ref, out2_ref, recv_hbm, sem, *, factor):
    part = o1_ref.shape[0]
    move = pltpu.make_async_copy(gi_ref, recv_hbm, sem)
    move.start()
    out1_ref[...] = (o1_ref[...] + x_ref[0:part, :].astype(f32) + y_ref[part:, :].astype(f32)) * factor
    out2_ref[...] = ((o2_ref[...] + x_ref[part:, :].astype(f32) + y_ref[0:part, :].astype(f32)) * factor).T
    move.wait()


def pair_kernel(own_ref, got_ref, total_ref, sent_ref):
    total = own_ref[...] + got_ref[...]
    total_ref[...] = total
    sent_ref[...] = total.astype(bf16)


def small_kernel(total_ref, a_ref, b_ref, c_ref, bias_ref, small_ref, stage_ref, *, factor):
    chans = total_ref.shape[1]
    rows = small_ref.shape[0]
    more = a_ref[...].astype(f32) + b_ref[...].astype(f32) + c_ref[...].astype(f32)
    stage_ref[...] = (total_ref[...] + more) * factor
    for k in range(rows):
        small_ref[k] = stage_ref[k : k + 1, :]
    for k in range(bias_ref.shape[1] // chans):
        bias_ref[:, k * chans : (k + 1) * chans] = stage_ref[rows + k : rows + k + 1, :]


def shifted(block, axis, distance):
    devices = range(lax.axis_size(axis))
    route = [(i - distance, i) for i in devices if i - distance in devices]
    return lax.ppermute(block, axis, route)


def swap(value, bit, count):
    return lax.ppermute(value, "dp", [(i, i ^ bit) for i in range(count)])


def shards(
    block_input,
    grad_output,
    depth_weight,
    depth_bias,
    norm_gain,
    norm_shift,
    pw1_weight,
    pw1_bias,
    pw2_weight,
    pw2_bias,
    layer_scale,
):
    x, g = block_input[0, 0], grad_output[0, 0]
    rows, cols, chans = x.shape
    cells = rows * cols
    blocks = chans // LANES
    taps = depth_weight.shape[1]
    w1, w2 = pw1_weight[0], pw2_weight[0]
    units = w1.shape[0]
    replicas = lax.axis_size("dp")
    factor = 1.0 / replicas
    wide = 768
    part = wide // 2
    fast = replicas == 8 and units == 4 * wide

    wexp = struct((blocks, taps + 42, 8, LANES), f32)
    padded = struct((blocks, rows, cols + 2 * EDGE, LANES), f32)
    like = lambda v: struct(v.shape, v.dtype)
    hbm = pl.BlockSpec(memory_space=pltpu.HBM)
    pin = lambda *vs: tuple(pltpu.with_memory_space_constraint(v, pltpu.HBM) for v in vs)
    vmem = pl.BlockSpec(memory_space=pltpu.VMEM)
    gp, xp, vecs, wexp, gv, tmp = call(
        load_kernel,
        (struct((cells, chans), bf16), padded, struct((8, chans), f32), wexp, like(g), struct((8, chans), f32)),
        *pin(x, g, depth_weight[0], depth_bias, norm_gain, norm_shift, layer_scale, pw2_bias),
        name="load", in_specs=[hbm] * 8, cost=estimate(1e10, 1e6),
        scratch=[pltpu.VMEM(x.shape, bf16), pltpu.VMEM((taps, chans), bf16), pltpu.SemaphoreType.DMA((8,))],
    )
    yn, normed, rstd, w1, b1, w2 = call(
        front_kernel,
        (struct((cells, chans), bf16), struct((cells, chans), f32), struct((cells, LANES), f32),
         like(w1), like(pw1_bias), like(w2)),
        xp, wexp, tmp, *pin(w1, pw1_bias, w2),
        name="front", in_specs=[vmem] * 3 + [hbm] * 3, cost=estimate(1e10, 1e6),
        scratch=[pltpu.VMEM((cells, LANES), f32), pltpu.SemaphoreType.DMA((3,))],
    )

    def wide_step(slot, mode, *more, other=None):
        sums = struct((8, wide), f32)
        outs = (struct((cells, chans), f32),) + ((sums,) if mode == "join" else ()) + (
            sums, struct((wide, cells), bf16), struct((wide, cells), bf16))
        return call(
            lambda *refs: wide_kernel(*refs, mode=mode, slot=slot, other=other), outs, yn, gp, w1, b1, w2, *more,
            name="wide", aliases={5: 0} if mode == "next" else {}, cost=estimate(1e10, 1e6),
        )

    def flip(k):
        return lambda chip: lax.bitwise_xor(chip, k)

    def slope(gn):
        return call(slope_kernel, (padded, struct((8, chans), f32)), gn, normed, rstd, vecs,
                    name="slope", cost=estimate(1e6, 1e3))

    if fast:
        gp_s, yn_s = swap(gp, 1, replicas), swap(yn, 1, replicas)
        part_rows = struct((part, cells), bf16)

        def share(k, keep, got, types):
            outs = (struct((part, chans), types[0]), struct((part, chans), types[1]), struct((8, chans), f32))
            return call(lambda *refs: share_kernel(*refs, slot=flip(k)), outs,
                        w2, yn, yn_s, gp, gp_s, keep, got, name="share", cost=estimate(1e6, 1e3))

        rise, keep_h, send_h = call(
            lambda *refs: open_kernel(*refs, slot=flip(3)), (struct((cells, wide), f32), part_rows, part_rows),
            yn, w1, b1, name="open", cost=estimate(1e6, 1e3))
        got_h = swap(send_h, 1, replicas)
        gpre, keep_g, send_g = call(
            lambda *refs: close_kernel(*refs, slot=flip(3)), (struct((cells, wide), bf16), part_rows, part_rows),
            gp, rise, w2, name="close", cost=estimate(1e6, 1e3))
        got_g = swap(send_g, 1, replicas)
        grad = struct((part, chans), bf16)
        gpre, got_h = lax.optimization_barrier((gpre, got_h))
        d2, sc_d = call(lambda *refs: half_kernel(*refs, slot=flip(3)), (grad, struct((8, chans), f32)),
                        gp, gp_s, keep_h, got_h, w2, name="half", cost=estimate(1e6, 1e3))
        d2, got_g = lax.optimization_barrier((d2, got_g))
        d1 = call(lambda *refs: half_kernel(*refs, slot=None), (grad,), yn, yn_s, keep_g, got_g,
                  name="half", cost=estimate(1e6, 1e3))[0]
        gpre, d1 = lax.optimization_barrier((gpre, d1))
        d1_in, d2_in = swap(d1, 2, replicas), swap(d2, 4, replicas)
        gn, bd, bx, keep_x, send_x = wide_step(flip(1), "join", gpre, other=flip(3))
        got_x = swap(send_x, 1, replicas)
        gn, by, keep_y, send_y = wide_step(flip(2), "next", gn)
        got_y = swap(send_y, 1, replicas)
        gn, bo, keep_o, send_o = wide_step(flip(0), "next", gn)
        got_o = swap(send_o, 1, replicas)
        gn, got_x = lax.optimization_barrier((gn, got_x))
        x1, x2, sc_x = share(1, keep_x, got_x, (bf16, f32))
        x1, got_y = lax.optimization_barrier((x1, got_y))
        y1, y2, sc_y = share(2, keep_y, got_y, (f32, bf16))
        y1, gn = lax.optimization_barrier((y1, gn))
        gd, sums = slope(gn)
        gd, x1, x2, y1, y2, d1_in, d2_in = lax.optimization_barrier((gd, x1, x2, y1, y2, d1_in, d2_in))

        def relay(direct, base, more):
            return call(relay_kernel, struct((wide, chans), bf16), direct, base, more,
                        name="relay", cost=estimate(1e6, 1e3))

        pack_x = relay(x1, x2, d2_in)
        y2, pack_x = lax.optimization_barrier((y2, pack_x))
        pack_y = relay(y2, y1, d1_in)
        gd, pack_y = lax.optimization_barrier((gd, pack_y))
        x_in, y_in = swap(pack_x, 2, replicas), swap(pack_y, 4, replicas)
    else:
        core = lax.axis_index("dp") % 2
        gn, bsums, g1, g2 = None, [], [], []
        for p in range(units // wide):
            gn, bsum, keep, send = wide_step(lambda chip, p=p: jnp.int32(p), *(("next", gn) if p else ("first",)))
            lo, hi = jnp.where(core == 0, keep, send), jnp.where(core == 0, send, keep)
            bsums.append(bsum[0:1])
            g1 += [dot(v[:part], yn) for v in (lo, hi)]
            g2 += [dot(v[part:], gp) for v in (lo, hi)]
        g1, g2 = jnp.concatenate(g1, axis=0), jnp.concatenate(g2, axis=0).T

    if not fast:
        gd, sums = slope(gn)
    gi = call(back_kernel, struct((rows, cols, chans), bf16), gd, gv, wexp, name="back", cost=estimate(1e6, 1e3))
    received = shifted(gi, "section", -1)

    if fast:
        o1, o2, sc_o = share(0, keep_o, got_o, (f32, f32))
        more = (sc_d, sc_x, sc_y, sc_o, bo, bx, by, bd)
    else:
        more = ()
    total_rows = -(-(taps + 5 + units // chans) // 8) * 8
    small = call(lambda *refs: tap_kernel(*refs, taps=taps, fast=fast), struct((total_rows, chans), f32),
                 xp, gd, vecs, sums, *more, name="taps", cost=estimate(1e6, 1e3))

    if fast:
        rows_all = struct(small.shape, f32)
        total, sent = call(pair_kernel, (rows_all, struct(small.shape, bf16)), small, swap(small, 1, replicas),
                           name="pair", cost=estimate(1e6, 1e3))
        parts = [swap(sent, bits, replicas) for bits in (2, 4)]
        sent, received = lax.optimization_barrier((sent, received))
        parts.append(swap(sent, 6, replicas))
        out1, out2, received = pl.pallas_call(
            lambda *refs: merge_kernel(*refs, factor=factor),
            out_shape=(struct((part, chans), f32), struct((chans, part), f32), like(gi)),
            in_specs=[vmem] * 5,
            out_specs=(vmem, vmem, hbm),
            scratch_shapes=[pltpu.SemaphoreType.DMA],
            compiler_params=pltpu.CompilerParams(vmem_limit_bytes=VMEM_LIMIT),
            name="merge",
        )(o1, o2, x_in, y_in, received)
        out1, total = lax.optimization_barrier((out1, total))
        bias, small = call(
            lambda *refs: small_kernel(*refs, factor=factor),
            (struct((1, units), f32), struct((taps + 5, 1, chans), f32)), total, *parts,
            name="small", scratch=[pltpu.VMEM(small.shape, f32)], cost=estimate(1e6, 1e3))
        small = jnp.transpose(small, (1, 0, 2))
    else:
        scale_sum = jnp.sum(g2 * w2.astype(f32), axis=1)
        gscale = scale_sum / layer_scale[0] + pw2_bias[0] * vecs[4]
        small = jnp.concatenate([small[: taps + 4], gscale[None], *bsums], axis=0)
        small = lax.psum(small, "dp")
        out1 = lax.psum_scatter(g1, "dp", scatter_dimension=0, tiled=True) * factor
        out2 = lax.psum_scatter(g2, "dp", scatter_dimension=1, tiled=True) * factor
        small = small * factor
        bias, small = small[taps + 5 :].reshape(1, -1), small[None, : taps + 5]
    return (out1[None], out2[None], bias, small, received[None, None])


def solution(mesh):
    in_specs = (
        P("section", "dp", None, None, None),
        P("section", "dp", None, None, None),
        P("section", None, None),
        P("section", None),
        P("section", None),
        P("section", None),
        P("section", None, None),
        P("section", None),
        P("section", None, None),
        P("section", None),
        P("section", None),
    )
    out_specs = (
        P("section", "dp", None),
        P("section", None, "dp"),
        P("section", None),
        P("section", None, None),
        P("section", "dp", None, None, None),
    )
    return jax.shard_map(shards, mesh=mesh, in_specs=in_specs, out_specs=out_specs, check_vma=False)
```

time: 70.5 us -> 68 us (0.965)
  blocking collectives: 15.8 us -> 0 us
  waiting for transfers between devices: 4.44 us -> 13.3 us
  starting transfers between devices: 8.97 us -> 13.6 us
    all_gather x1 -> x0, blocking collectives: 15.8 us -> none  [shards(): every = lax.all_gather(small.astype(bf16), 'dp')]
    ppermute x1, waiting for transfers between devices: 0.01 us -> 9.58 us  [shifted(): return lax.ppermute(block, axis, route)]
    ppermute x9 -> x15, starting transfers between devices: 7.68 us -> 12.3 us  [swap(): return lax.ppermute(value, 'dp', [(i, i ^ bit) for i in range(count)])]
    ppermute x9 -> x15, waiting for transfers between devices: 4.43 us -> 3.7 us  [swap(): return lax.ppermute(value, 'dp', [(i, i ^ bit) for i in range(count)])]
    pallas_call x13 -> x19, Pallas kernels: 37.8 us -> 37.8 us  [call(): pl.pallas_call(body, out_shape=out_shape, in_specs=specs, out_specs=jax.t...]
  transfers between devices with their start and end apart: 10 -> 16, of which waited for: 3 -> 5; matrix products, arithmetic and copies ran while one was open for 0% -> 0% of each run, Pallas kernels for 40% -> 54%
where the time goes in v5:
time: 68 us; the launch traced here: 67.9 us
  Pallas kernels  40.1 us (59%)
  starting transfers between devices  13.6 us (20%)
  waiting for transfers between devices  13.3 us (20%)
  between operations  0.84 us (1%)
    pallas_call x19, Pallas kernels, call(): pl.pallas_call(body, out_shape=out_shape, in_specs=specs, out_specs=jax.t...  37.8 us
    ppermute x15, starting transfers between devices, swap(): return lax.ppermute(value, 'dp', [(i, i ^ bit) for i in range(count)])  12.3 us
    ppermute x1, waiting for transfers between devices, shifted(): return lax.ppermute(block, axis, route)  9.58 us
    ppermute x15, waiting for transfers between devices, swap(): return lax.ppermute(value, 'dp', [(i, i ^ bit) for i in range(count)])  3.7 us
    pallas_call x1, Pallas kernels, shards(): pl.pallas_call(lambda *refs: merge_kernel(*refs, factor=factor), out_shap...  2.33 us
  transfers between devices with their start and end apart: 16, of which 5 were waited for; matrix products, arithmetic and copies ran while one was open for 0% of the time, Pallas kernels for 54%

profile of v5, /device:TPU:0, one launch (start us, length us, event | category | flops | bytes accessed | tf_op | source)
XLA Modules:
  0.0 67.9 jit_solution(17825862955174598901)
XLA Ops:
  0.6 1.8 %load.1 = (bf16[512,768]{1,0:T(8,128)(2,1)S(1)}, f32[6,8,80,128]{3,2,1,0:T(8,128)S(1)}, f32[8,768]{1,0:T(8,128)S(1)}, f32[6,91,8,128]{3,2,1,0:T(8,128)S(1)}, bf1...) custom-call(bf16[8,64,768]{2,1,0:T(8,128)(2,1)} %bitcast.13, bf16[8,64,768]{2,1,0:T(8,128)(2,1)} %bitcast.14, ...), custom_call_target="tpu_custom_call" | custom-call | flops 10000000000 | bytes 1000000 | tf_op jit(solution)/shard_map/load/pallas_call | solution.py:25
  2.9 5.8 %front.1 = (bf16[512,768]{1,0:T(8,128)(2,1)S(1)}, f32[512,768]{1,0:T(8,128)S(1)}, f32[512,128]{1,0:T(8,128)S(1)}, bf16[3072,768]{1,0:T(8,128)(2,1)S(1)}, f32[1,3...) custom-call(f32[6,8,80,128]{3,2,1,0:T(8,128)S(1)} %get-tuple-element.83.xp_ref.refs_0_, ...), custom_call_target="tpu_custom_call" | custom-call | flops 10000000000 | bytes 1000000 | tf_op jit(solution)/shard_map/front/pallas_call | solution.py:25
  8.9 1.3 %open.1 = (f32[512,768]{1,0:T(8,128)S(1)}, bf16[384,512]{1,0:T(8,128)(2,1)S(1)}, bf16[384,512]{1,0:T(8,128)(2,1)S(1)}) custom-call(bf16[512,768]{1,0:T(8,128)(2,1)S(1)} %get-tuple-element.87.refs_0_.refs_1_, bf16[3072,768]{1,0:T(8,128)(2,1)S(1)} %get-tuple-element.89.refs_1_.refs_2_, f32[1,3072]{1,0:T(1,128)S(1)} %get-tuple-element.90.refs_2_.refs_3_), custom_call_target="tpu_custom_call" | custom-call | flops 1000000 | bytes 1000 | tf_op jit(solution)/shard_map/open/pallas_call | solution.py:25
  10.2 0.5 collective-permute-start.2
  10.7 0.9 %close.1 = (bf16[512,768]{1,0:T(8,128)(2,1)S(1)}, bf16[384,512]{1,0:T(8,128)(2,1)S(1)}, bf16[384,512]{1,0:T(8,128)(2,1)S(1)}) custom-call(bf16[512,768]{1,0:T(8,128)(2,1)S(1)} %get-tuple-element.88.refs_0_.refs_1_.refs_3_, f32[512,768]{1,0:T(8,128)S(1)} %get-tuple-element.91.refs_1_, bf16[768,3072]{1,0:T(8,128)(2,1)S(1)} %get-tuple-element.86.refs_2_.refs_4_.refs_0_), custom_call_target="tpu_custom_call" | custom-call | flops 1000000 | bytes 1000 | tf_op jit(solution)/shard_map/close/pallas_call | solution.py:25
  12.1 0.8 %half.2 = (bf16[384,768]{1,0:T(8,128)(2,1)S(1)}, f32[8,768]{1,0:T(8,128)S(1)}) custom-call(bf16[512,768]{1,0:T(8,128)(2,1)S(1)} %get-tuple-element.88.refs_0_.refs_1_.refs_3_, bf16[512,768]{1,0:T(8,128)(2,1)S(1)} %collective-permute-done.1.refs_1_.refs_4_, bf16[384,512]{1,0:T(8,128)(2,1)S(1)} %get-tuple-element.96.refs_2_, ...), custom_call_target="tpu_custom_call" | custom-call | flops 1000000 | bytes 1000 | tf_op jit(solution)/shard_map/half/pallas_call | solution.py:25
  12.9 0.6 collective-permute-done.3.refs_3_
  13.4 0.8 %half.3 = bf16[384,768]{1,0:T(8,128)(2,1)S(1)} custom-call(bf16[512,768]{1,0:T(8,128)(2,1)S(1)} %get-tuple-element.87.refs_0_.refs_1_, bf16[512,768]{1,0:T(8,128)(2,1)S(1)} %collective-permute-done.refs_1_.refs_2_, bf16[384,512]{1,0:T(8,128)(2,1)S(1)} %get-tuple-element.95.refs_2_, bf16[384,512]{1,0:T(8,128)(2,1)S(1)} %collective-permute-done.3.refs_3_), custom_call_target="tpu_custom_call" | custom-call | flops 1000000 | bytes 1000 | tf_op jit(solution)/shard_map/half/pallas_call | solution.py:25
  14.2 2.7 %collective-permute-start.7 = (bf16[384,768]{1,0:T(8,128)(2,1)S(1)}, bf16[384,768]{1,0:T(8,128)(2,1)S(1)}, u32[]{:S(2)}, u32[]{:S(2)}) collective-permute-start(bf16[384,768]{1,0:T(8,128)(2,1)S(1)} %half.3), channel_id=1, source_target_pairs={{0,2},{1,3},{2,0},{3,1},{4,6},{5,7},{6,4},{7,5},{8,10},{9,11},{10,... | collective-permute-start | bytes 1769480 | tf_op jit(solution)/shard_map/ppermute | solution.py:408
  16.9 1.5 %collective-permute-start.8 = (bf16[384,768]{1,0:T(8,128)(2,1)S(1)}, bf16[384,768]{1,0:T(8,128)(2,1)S(1)}, u32[]{:S(2)}, u32[]{:S(2)}) collective-permute-start(bf16[384,768]{1,0:T(8,128)(2,1)S(1)} %get-tuple-element.128), channel_id=1, source_target_pairs={{0,4},{1,5},{2,6},{3,7},{4,0},{5,1},{6,2},{7,3},{8,12},{9,13},{10,... | collective-permute-start | bytes 1769480 | tf_op jit(solution)/shard_map/ppermute | solution.py:408
  18.4 3.4 %wide.3 = (f32[512,768]{1,0:T(8,128)S(1)}, f32[8,768]{1,0:T(8,128)S(1)}, f32[8,768]{1,0:T(8,128)S(1)}, bf16[768,512]{1,0:T(8,128)(2,1)S(1)}, bf16[768,512]{1,0:T(8,128)(2,1)S(1)}) custom-call(bf16[512,768]{1,0:T(8,128)(2,1)S(1)} %get-tuple-element.87.refs_0_.refs_1_, bf16[512,768]{1,0:T(8,128)(2,1)S(1)} %get-tuple-element.88.refs_0_.refs_1_.refs_3_, ...), custom_call_target="tpu_custom_call" | custom-call | flops 10000000000 | bytes 1000000 | tf_op jit(solution)/shard_map/wide/pallas_call | solution.py:25
  21.9 2.9 %wide.4 = (f32[512,768]{1,0:T(8,128)S(1)}, f32[8,768]{1,0:T(8,128)S(1)}, bf16[768,512]{1,0:T(8,128)(2,1)S(1)}, bf16[768,512]{1,0:T(8,128)(2,1)S(1)}) custom-call(bf16[512,768]{1,0:T(8,128)(2,1)S(1)} %get-tuple-element.87.refs_0_.refs_1_, bf16[512,768]{1,0:T(8,128)(2,1)S(1)} %get-tuple-element.88.refs_0_.refs_1_.refs_3_, ...), custom_call_target="tpu_custom_call", output_to_operand_aliasing={{0}: (5, {})} | custom-call | flops 10000000000 | bytes 1000000 | tf_op jit(solution)/shard_map/wide/pallas_call | solution.py:25
  24.8 0.5 collective-permute-start.6
  25.4 2.7 %wide.5 = (f32[512,768]{1,0:T(8,128)S(1)}, f32[8,768]{1,0:T(8,128)S(1)}, bf16[768,512]{1,0:T(8,128)(2,1)S(1)}, bf16[768,512]{1,0:T(8,128)(2,1)S(1)}) custom-call(bf16[512,768]{1,0:T(8,128)(2,1)S(1)} %get-tuple-element.87.refs_0_.refs_1_, bf16[512,768]{1,0:T(8,128)(2,1)S(1)} %get-tuple-element.88.refs_0_.refs_1_.refs_3_, ...), custom_call_target="tpu_custom_call", output_to_operand_aliasing={{0}: (5, {})} | custom-call | flops 10000000000 | bytes 1000000 | tf_op jit(solution)/shard_map/wide/pallas_call | solution.py:25
  28.1 1.4 %share.4 = (bf16[384,768]{1,0:T(8,128)(2,1)S(1)}, f32[384,768]{1,0:T(8,128)S(1)}, f32[8,768]{1,0:T(8,128)S(1)}) custom-call(bf16[768,3072]{1,0:T(8,128)(2,1)S(1)} %get-tuple-element.86.refs_2_.refs_4_.refs_0_, bf16[512,768]{1,0:T(8,128)(2,1)S(1)} %get-tuple-element.87.refs_0_.refs_1_, bf16[512,768]{1,0:T(8,128)(2,1)S(1)} %collective-permute-done.refs_1_.refs_2_, ...), custom_call_target="tpu_custom_call" | custom-call | flops 1000000 | bytes 1000 | tf_op jit(solution)/shard_map/share/pallas_call | solution.py:25
  29.5 1.4 %share.5 = (f32[384,768]{1,0:T(8,128)S(1)}, bf16[384,768]{1,0:T(8,128)(2,1)S(1)}, f32[8,768]{1,0:T(8,128)S(1)}) custom-call(bf16[768,3072]{1,0:T(8,128)(2,1)S(1)} %get-tuple-element.86.refs_2_.refs_4_.refs_0_, bf16[512,768]{1,0:T(8,128)(2,1)S(1)} %get-tuple-element.87.refs_0_.refs_1_, bf16[512,768]{1,0:T(8,128)(2,1)S(1)} %collective-permute-done.refs_1_.refs_2_, ...), custom_call_target="tpu_custom_call" | custom-call | flops 1000000 | bytes 1000 | tf_op jit(solution)/shard_map/share/pallas_call | solution.py:25
  30.9 1.3 %slope.1 = (f32[6,8,80,128]{3,2,1,0:T(8,128)S(1)}, f32[8,768]{1,0:T(8,128)S(1)}) custom-call(f32[512,768]{1,0:T(8,128)S(1)} %get-tuple-element.118.gn_ref, f32[512,768]{1,0:T(8,128)S(1)} %get-tuple-element.119.normed_ref, f32[512,128]{1,0:T(8,128)S(1)} %get-tuple-element.120.rstd_ref, f32[8,768]{1,0:T(8,128)S(1)} %get-tuple-element.121.vecs_ref.refs_2_), custom_call_target="tpu_custom_call" | custom-call | flops 1000000 | bytes 1000 | tf_op jit(solution)/shard_map/slope/pallas_call | solution.py:25
  32.6 1.6 %collective-permute-start.10 = (bf16[768,768]{1,0:T(8,128)(2,1)S(1)}, bf16[768,768]{1,0:T(8,128)(2,1)S(1)}, u32[]{:S(2)}, u32[]{:S(2)}) collective-permute-start(bf16[768,768]{1,0:T(8,128)(2,1)S(1)} %relay.3), channel_id=1, source_target_pairs={{0,4},{1,5},{2,6},{3,7},{4,0},{5,1},{6,2},{7,3},{8,12},{9,13},{10,... | collective-permute-start | bytes 3538952 | tf_op jit(solution)/shard_map/ppermute | solution.py:408
  34.1 0.5 collective-permute-start.9
  34.7 5.0 %back.1 = bf16[8,64,768]{2,1,0:T(8,128)(2,1)S(1)} custom-call(f32[6,8,80,128]{3,2,1,0:T(8,128)S(1)} %get-tuple-element.139.refs_1_.gd_ref, bf16[8,64,768]{2,1,0:T(8,128)(2,1)S(1)} %get-tuple-element.150.g_ref, f32[6,91,8,128]{3,2,1,0:T(8,128)S(1)} %get-tuple-element.84.wexp), custom_call_target="tpu_custom_call" | custom-call | flops 1000000 | bytes 1000 | tf_op jit(solution)/shard_map/back/pallas_call | solution.py:25
  39.7 1.3 %collective-permute-start.12 = (bf16[8,64,768]{2,1,0:T(8,128)(2,1)S(1)}, bf16[8,64,768]{2,1,0:T(8,128)(2,1)S(1)}, u32[]{:S(2)}, u32[]{:S(2)}) collective-permute-start(bf16[8,64,768]{2,1,0:T(8,128)(2,1)S(1)} %back.1), channel_id=1, source_target_pairs={{8,0},{16,8},{24,16},{9,1},{17,9},{25,17},{10,2},{18,10},{26,18},{... | collective-permute-start | bytes 2359304 | tf_op jit(solution)/shard_map/ppermute | solution.py:404
  41.0 1.4 %share.3 = (f32[384,768]{1,0:T(8,128)S(1)}, f32[384,768]{1,0:T(8,128)S(1)}, f32[8,768]{1,0:T(8,128)S(1)}) custom-call(bf16[768,3072]{1,0:T(8,128)(2,1)S(1)} %get-tuple-element.86.refs_2_.refs_4_.refs_0_, bf16[512,768]{1,0:T(8,128)(2,1)S(1)} %get-tuple-element.87.refs_0_.refs_1_, bf16[512,768]{1,0:T(8,128)(2,1)S(1)} %collective-permute-done.refs_1_.refs_2_, ...), custom_call_target="tpu_custom_call" | custom-call | flops 1000000 | bytes 1000 | tf_op jit(solution)/shard_map/share/pallas_call | solution.py:25
  42.4 5.8 %taps.1.own_ref = f32[64,768]{1,0:T(8,128)S(1)} custom-call(f32[6,8,80,128]{3,2,1,0:T(8,128)S(1)} %get-tuple-element.83.xp_ref.refs_0_, f32[6,8,80,128]{3,2,1,0:T(8,128)S(1)} %get-tuple-element.139.refs_1_.gd_ref, f32[8,768]{1,0:T(8,128)S(1)} %get-tuple-element.121.vecs_ref.refs_2_, f32[8,768]{1,0:T(8,128)S(1)} %get-tuple-element.140.refs_3_, ...), custom_call_target="tpu_custom_call" | custom-call | flops 1000000 | bytes 1000 | tf_op jit(solution)/shard_map/taps/pallas_call | solution.py:25
  48.2 0.6 collective-permute-start.11
  48.8 1.1 %collective-permute-done.11.got_ref = f32[64,768]{1,0:T(8,128)S(1)} collective-permute-done((f32[64,768]{1,0:T(8,128)S(1)}, f32[64,768]{1,0:T(8,128)S(1)}, u32[]{:S(2)}, u32[]{:S(2)}) %collective-permute-start.11) | collective-permute-done | bytes 196640 | tf_op jit(solution)/shard_map/ppermute | solution.py:408
  49.9 0.6 collective-permute-start.14
  50.5 1.5 %collective-permute-start.13 = (bf16[64,768]{1,0:T(8,128)(2,1)S(1)}, bf16[64,768]{1,0:T(8,128)(2,1)S(1)}, u32[]{:S(2)}, u32[]{:S(2)}) collective-permute-start(bf16[64,768]{1,0:T(8,128)(2,1)S(1)} %get-tuple-element.157), channel_id=1, source_target_pairs={{0,2},{1,3},{2,0},{3,1},{4,6},{5,7},{6,4},{7,5},{8,10},{9,11},{10,... | collective-permute-start | bytes 294920 | tf_op jit(solution)/shard_map/ppermute | solution.py:408
  52.0 9.6 %collective-permute-done.12.refs_4_ = bf16[8,64,768]{2,1,0:T(8,128)(2,1)S(1)} collective-permute-done((bf16[8,64,768]{2,1,0:T(8,128)(2,1)S(1)}, bf16[8,64,768]{2,1,0:T(8,128)(2,1)S(1)}, u32[]{:S(2)}, u32[]{:S(2)}) %collective-permute-start.12) | collective-permute-done | bytes 786464 | tf_op jit(solution)/shard_map/ppermute | solution.py:404
  61.6 1.4 %collective-permute-start.15 = (bf16[64,768]{1,0:T(8,128)(2,1)S(1)}, bf16[64,768]{1,0:T(8,128)(2,1)S(1)}, u32[]{:S(2)}, u32[]{:S(2)}) collective-permute-start(bf16[64,768]{1,0:T(8,128)(2,1)S(1)} %get-tuple-element.157), channel_id=1, source_target_pairs={{0,6},{1,7},{2,4},{3,5},{4,2},{5,3},{6,0},{7,1},{8,14},{9,15},{10,... | collective-permute-start | bytes 294920 | tf_op jit(solution)/shard_map/ppermute | solution.py:408
  63.0 2.3 %merge.1 = (f32[384,768]{1,0:T(8,128)}, f32[768,384]{1,0:T(8,128)}, bf16[8,64,768]{2,1,0:T(8,128)(2,1)}) custom-call(f32[384,768]{1,0:T(8,128)S(1)} %get-tuple-element.106.refs_0_, f32[384,768]{1,0:T(8,128)S(1)} %get-tuple-element.107.refs_1_, bf16[768,768]{1,0:T(8,128)(2,1)S(1)} %collective-permute-done.9.refs_2_, ...), custom_call_target="tpu_custom_call" | custom-call | tf_op jit(solution)/shard_map/merge/pallas_call | solution.py:556
  65.4 1.7 %collective-permute-done.15.refs_3_ = bf16[64,768]{1,0:T(8,128)(2,1)S(1)} collective-permute-done((bf16[64,768]{1,0:T(8,128)(2,1)S(1)}, bf16[64,768]{1,0:T(8,128)(2,1)S(1)}, u32[]{:S(2)}, u32[]{:S(2)}) %collective-permute-start.15) | collective-permute-done | bytes 98336 | tf_op jit(solution)/shard_map/ppermute | solution.py:408
  67.1 0.8 %small.1 = (f32[1,3072]{1,0:T(1,128)}, f32[54,1,768]{2,1,0:T(1,128)}) custom-call(f32[64,768]{1,0:T(8,128)S(1)} %get-tuple-element.156.refs_0_, bf16[64,768]{1,0:T(8,128)(2,1)S(1)} %collective-permute-done.13.refs_1_, bf16[64,768]{1,0:T(8,128)(2,1)S(1)} %collective-permute-done.14.refs_2_, bf16[64,768]{1,0:T(8,128)(2,1)S(1)} %collective-permute-done.15.refs_3_), custom_call_target="tpu_custom_call" | custom-call | flops 1000000 | bytes 1000 | tf_op jit(solution)/shard_map/small/pallas_call | solution.py:25
  (20 shorter events, 1.5 us)
Async XLA Ops:
  2.4 9.7 %collective-permute-start.1 = (bf16[512,768]{1,0:T(8,128)(2,1)S(1)}, bf16[512,768]{1,0:T(8,128)(2,1)S(1)}, u32[]{:S(2)}, u32[]{:S(2)}) collective-permute-start(bf16[512,768]{1,0:T(8,128)(2,1)S(1)} %get-tuple-element.88.refs_0_.refs_1_.refs_3_), channel_id=1, source_target_pairs={{0,1},{1,0},{2,3},{3,2},{4,5},{5,4},{6,7},{7,6},{8,9},{9,8},{10,11... | collective-permute-start | bytes 2359304 | tf_op jit(solution)/shard_map/ppermute | solution.py:408
  8.8 4.7 %collective-permute-start = (bf16[512,768]{1,0:T(8,128)(2,1)S(1)}, bf16[512,768]{1,0:T(8,128)(2,1)S(1)}, u32[]{:S(2)}, u32[]{:S(2)}) collective-permute-start(bf16[512,768]{1,0:T(8,128)(2,1)S(1)} %get-tuple-element.87.refs_0_.refs_1_), channel_id=1, source_target_pairs={{0,1},{1,0},{2,3},{3,2},{4,5},{5,4},{6,7},{7,6},{8,9},{9,8},{10,11... | collective-permute-start | bytes 2359304 | tf_op jit(solution)/shard_map/ppermute | solution.py:408
  10.2 1.9 %collective-permute-start.2 = (bf16[384,512]{1,0:T(8,128)(2,1)S(1)}, bf16[384,512]{1,0:T(8,128)(2,1)S(1)}, u32[]{:S(2)}, u32[]{:S(2)}) collective-permute-start(bf16[384,512]{1,0:T(8,128)(2,1)S(1)} %get-tuple-element.93), channel_id=1, source_target_pairs={{0,1},{1,0},{2,3},{3,2},{4,5},{5,4},{6,7},{7,6},{8,9},{9,8},{10,11... | collective-permute-start | bytes 1179656 | tf_op jit(solution)/shard_map/ppermute | solution.py:408
  11.7 1.8 %collective-permute-start.3 = (bf16[384,512]{1,0:T(8,128)(2,1)S(1)}, bf16[384,512]{1,0:T(8,128)(2,1)S(1)}, u32[]{:S(2)}, u32[]{:S(2)}) collective-permute-start(bf16[384,512]{1,0:T(8,128)(2,1)S(1)} %get-tuple-element.99), channel_id=1, source_target_pairs={{0,1},{1,0},{2,3},{3,2},{4,5},{5,4},{6,7},{7,6},{8,9},{9,8},{10,11... | collective-permute-start | bytes 1179656 | tf_op jit(solution)/shard_map/ppermute | solution.py:408
  14.2 18.0 %collective-permute-start.7 = (bf16[384,768]{1,0:T(8,128)(2,1)S(1)}, bf16[384,768]{1,0:T(8,128)(2,1)S(1)}, u32[]{:S(2)}, u32[]{:S(2)}) collective-permute-start(bf16[384,768]{1,0:T(8,128)(2,1)S(1)} %half.3), channel_id=1, source_target_pairs={{0,2},{1,3},{2,0},{3,1},{4,6},{5,7},{6,4},{7,5},{8,10},{9,11},{10,... | collective-permute-start | bytes 1769480 | tf_op jit(solution)/shard_map/ppermute | solution.py:408
  16.9 15.3 %collective-permute-start.8 = (bf16[384,768]{1,0:T(8,128)(2,1)S(1)}, bf16[384,768]{1,0:T(8,128)(2,1)S(1)}, u32[]{:S(2)}, u32[]{:S(2)}) collective-permute-start(bf16[384,768]{1,0:T(8,128)(2,1)S(1)} %get-tuple-element.128), channel_id=1, source_target_pairs={{0,4},{1,5},{2,6},{3,7},{4,0},{5,1},{6,2},{7,3},{8,12},{9,13},{10,... | collective-permute-start | bytes 1769480 | tf_op jit(solution)/shard_map/ppermute | solution.py:408
  21.8 6.2 %collective-permute-start.5 = (bf16[768,512]{1,0:T(8,128)(2,1)S(1)}, bf16[768,512]{1,0:T(8,128)(2,1)S(1)}, u32[]{:S(2)}, u32[]{:S(2)}) collective-permute-start(bf16[768,512]{1,0:T(8,128)(2,1)S(1)} %get-tuple-element.111), channel_id=1, source_target_pairs={{0,1},{1,0},{2,3},{3,2},{4,5},{5,4},{6,7},{7,6},{8,9},{9,8},{10,11... | collective-permute-start | bytes 2359304 | tf_op jit(solution)/shard_map/ppermute | solution.py:408
  24.8 4.7 %collective-permute-start.6 = (bf16[768,512]{1,0:T(8,128)(2,1)S(1)}, bf16[768,512]{1,0:T(8,128)(2,1)S(1)}, u32[]{:S(2)}, u32[]{:S(2)}) collective-permute-start(bf16[768,512]{1,0:T(8,128)(2,1)S(1)} %get-tuple-element.114), channel_id=1, source_target_pairs={{0,1},{1,0},{2,3},{3,2},{4,5},{5,4},{6,7},{7,6},{8,9},{9,8},{10,11... | collective-permute-start | bytes 2359304 | tf_op jit(solution)/shard_map/ppermute | solution.py:408
  32.6 30.4 %collective-permute-start.10 = (bf16[768,768]{1,0:T(8,128)(2,1)S(1)}, bf16[768,768]{1,0:T(8,128)(2,1)S(1)}, u32[]{:S(2)}, u32[]{:S(2)}) collective-permute-start(bf16[768,768]{1,0:T(8,128)(2,1)S(1)} %relay.3), channel_id=1, source_target_pairs={{0,4},{1,5},{2,6},{3,7},{4,0},{5,1},{6,2},{7,3},{8,12},{9,13},{10,... | collective-permute-start | bytes 3538952 | tf_op jit(solution)/shard_map/ppermute | solution.py:408
  34.1 28.9 %collective-permute-start.9 = (bf16[768,768]{1,0:T(8,128)(2,1)S(1)}, bf16[768,768]{1,0:T(8,128)(2,1)S(1)}, u32[]{:S(2)}, u32[]{:S(2)}) collective-permute-start(bf16[768,768]{1,0:T(8,128)(2,1)S(1)} %relay.2), channel_id=1, source_target_pairs={{0,2},{1,3},{2,0},{3,1},{4,6},{5,7},{6,4},{7,5},{8,10},{9,11},{10,... | collective-permute-start | bytes 3538952 | tf_op jit(solution)/shard_map/ppermute | solution.py:408
  34.7 6.3 %collective-permute-start.4 = (bf16[768,512]{1,0:T(8,128)(2,1)S(1)}, bf16[768,512]{1,0:T(8,128)(2,1)S(1)}, u32[]{:S(2)}, u32[]{:S(2)}) collective-permute-start(bf16[768,512]{1,0:T(8,128)(2,1)S(1)} %get-tuple-element.105), channel_id=1, source_target_pairs={{0,1},{1,0},{2,3},{3,2},{4,5},{5,4},{6,7},{7,6},{8,9},{9,8},{10,11... | collective-permute-start | bytes 2359304 | tf_op jit(solution)/shard_map/ppermute | solution.py:408
  39.7 21.8 %collective-permute-start.12 = (bf16[8,64,768]{2,1,0:T(8,128)(2,1)S(1)}, bf16[8,64,768]{2,1,0:T(8,128)(2,1)S(1)}, u32[]{:S(2)}, u32[]{:S(2)}) collective-permute-start(bf16[8,64,768]{2,1,0:T(8,128)(2,1)S(1)} %back.1), channel_id=1, source_target_pairs={{8,0},{16,8},{24,16},{9,1},{17,9},{25,17},{10,2},{18,10},{26,18},{... | collective-permute-start | bytes 2359304 | tf_op jit(solution)/shard_map/ppermute | solution.py:404
  48.2 1.7 %collective-permute-start.11 = (f32[64,768]{1,0:T(8,128)S(1)}, f32[64,768]{1,0:T(8,128)S(1)}, u32[]{:S(2)}, u32[]{:S(2)}) collective-permute-start(f32[64,768]{1,0:T(8,128)S(1)} %taps.1.own_ref), channel_id=1, source_target_pairs={{0,1},{1,0},{2,3},{3,2},{4,5},{5,4},{6,7},{7,6},{8,9},{9,8},{10,11... | collective-permute-start | bytes 589832 | tf_op jit(solution)/shard_map/ppermute | solution.py:408
  49.9 15.4 %collective-permute-start.14 = (bf16[64,768]{1,0:T(8,128)(2,1)S(1)}, bf16[64,768]{1,0:T(8,128)(2,1)S(1)}, u32[]{:S(2)}, u32[]{:S(2)}) collective-permute-start(bf16[64,768]{1,0:T(8,128)(2,1)S(1)} %get-tuple-element.157), channel_id=1, source_target_pairs={{0,4},{1,5},{2,6},{3,7},{4,0},{5,1},{6,2},{7,3},{8,12},{9,13},{10,... | collective-permute-start | bytes 294920 | tf_op jit(solution)/shard_map/ppermute | solution.py:408
  50.5 14.9 %collective-permute-start.13 = (bf16[64,768]{1,0:T(8,128)(2,1)S(1)}, bf16[64,768]{1,0:T(8,128)(2,1)S(1)}, u32[]{:S(2)}, u32[]{:S(2)}) collective-permute-start(bf16[64,768]{1,0:T(8,128)(2,1)S(1)} %get-tuple-element.157), channel_id=1, source_target_pairs={{0,2},{1,3},{2,0},{3,1},{4,6},{5,7},{6,4},{7,5},{8,10},{9,11},{10,... | collective-permute-start | bytes 294920 | tf_op jit(solution)/shard_map/ppermute | solution.py:408
  61.6 5.5 %collective-permute-start.15 = (bf16[64,768]{1,0:T(8,128)(2,1)S(1)}, bf16[64,768]{1,0:T(8,128)(2,1)S(1)}, u32[]{:S(2)}, u32[]{:S(2)}) collective-permute-start(bf16[64,768]{1,0:T(8,128)(2,1)S(1)} %get-tuple-element.157), channel_id=1, source_target_pairs={{0,6},{1,7},{2,4},{3,5},{4,2},{5,3},{6,0},{7,1},{8,14},{9,15},{10,... | collective-permute-start | bytes 294920 | tf_op jit(solution)/shard_map/ppermute | solution.py:408

commit v6 on v5

--- a/solution.py
+++ b/solution.py
@@ -372,13 +372,10 @@
             small_ref[pl.ds(taps + 5 + lax.bitwise_xor(chip, k), 1), :] = bsums[k][0:1, :]
 
 
-def merge_kernel(o1_ref, o2_ref, x_ref, y_ref, gi_ref, out1_ref, out2_ref, recv_hbm, sem, *, factor):
+def merge_kernel(o1_ref, o2_ref, x_ref, y_ref, out1_ref, out2_ref, *, factor):
     part = o1_ref.shape[0]
-    move = pltpu.make_async_copy(gi_ref, recv_hbm, sem)
-    move.start()
     out1_ref[...] = (o1_ref[...] + x_ref[0:part, :].astype(f32) + y_ref[part:, :].astype(f32)) * factor
     out2_ref[...] = ((o2_ref[...] + x_ref[part:, :].astype(f32) + y_ref[0:part, :].astype(f32)) * factor).T
-    move.wait()
 
 
 def pair_kernel(own_ref, got_ref, total_ref, sent_ref):
@@ -387,11 +384,25 @@
     sent_ref[...] = total.astype(bf16)
 
 
-def small_kernel(total_ref, a_ref, b_ref, c_ref, bias_ref, small_ref, stage_ref, *, factor):
-    chans = total_ref.shape[1]
+def gather_kernel(total_ref, near_ref, far_ref, some_ref):
+    _, core = place()
+    some_ref[...] = near_ref[...].astype(f32)
+
+    @pl.when(core == 0)
+    def _():
+        some_ref[...] = some_ref[...] + total_ref[...] + far_ref[...].astype(f32)
+
+
+def emit_kernel(gi_ref, recv_hbm, sem):
+    move = pltpu.make_async_copy(gi_ref, recv_hbm, sem)
+    move.start()
+    move.wait()
+
+
+def small_kernel(own_ref, got_ref, bias_ref, small_ref, stage_ref, *, factor):
+    chans = own_ref.shape[1]
     rows = small_ref.shape[0]
-    more = a_ref[...].astype(f32) + b_ref[...].astype(f32) + c_ref[...].astype(f32)
-    stage_ref[...] = (total_ref[...] + more) * factor
+    stage_ref[...] = (own_ref[...] + got_ref[...]) * factor
     for k in range(rows):
         small_ref[k] = stage_ref[k : k + 1, :]
     for k in range(bias_ref.shape[1] // chans):
@@ -550,22 +561,25 @@
         rows_all = struct(small.shape, f32)
         total, sent = call(pair_kernel, (rows_all, struct(small.shape, bf16)), small, swap(small, 1, replicas),
                            name="pair", cost=estimate(1e6, 1e3))
-        parts = [swap(sent, bits, replicas) for bits in (2, 4)]
-        sent, received = lax.optimization_barrier((sent, received))
-        parts.append(swap(sent, 6, replicas))
-        out1, out2, received = pl.pallas_call(
+        near = lax.ppermute(sent, "dp", [(i, i ^ (4 if i % 2 else 2)) for i in range(replicas)])
+        far = lax.ppermute(sent, "dp", [(i, i ^ 6) for i in range(0, replicas, 2)])
+        out1, out2 = call(
             lambda *refs: merge_kernel(*refs, factor=factor),
-            out_shape=(struct((part, chans), f32), struct((chans, part), f32), like(gi)),
-            in_specs=[vmem] * 5,
-            out_specs=(vmem, vmem, hbm),
+            (struct((part, chans), f32), struct((chans, part), f32)),
+            o1, o2, x_in, y_in, name="merge", cost=estimate(1e6, 1e3))
+        out1, total = lax.optimization_barrier((out1, total))
+        some = call(gather_kernel, rows_all, total, near, far, name="gather", cost=estimate(1e6, 1e3))
+        some_in = swap(some, 1, replicas)
+        some, received = lax.optimization_barrier((some, received))
+        received = pl.pallas_call(
+            emit_kernel, out_shape=like(gi), in_specs=[vmem], out_specs=hbm,
             scratch_shapes=[pltpu.SemaphoreType.DMA],
-            compiler_params=pltpu.CompilerParams(vmem_limit_bytes=VMEM_LIMIT),
-            name="merge",
-        )(o1, o2, x_in, y_in, received)
-        out1, total = lax.optimization_barrier((out1, total))
+            compiler_params=pltpu.CompilerParams(vmem_limit_bytes=VMEM_LIMIT), name="emit",
+        )(received)
+        some, received = lax.optimization_barrier((some, received))
         bias, small = call(
             lambda *refs: small_kernel(*refs, factor=factor),
-            (struct((1, units), f32), struct((taps + 5, 1, chans), f32)), total, *parts,
+            (struct((1, units), f32), struct((taps + 5, 1, chans), f32)), some, some_in,
             name="small", scratch=[pltpu.VMEM(small.shape, f32)], cost=estimate(1e6, 1e3))
         small = jnp.transpose(small, (1, 0, 2))
     else:

time: 68 us -> 65.9 us (0.969)
  waiting for transfers between devices: 13.3 us -> 10.1 us
    ppermute x1, waiting for transfers between devices: 9.58 us -> 0.01 us  [shifted(): return lax.ppermute(block, axis, route)]
    ppermute x15 -> x13, waiting for transfers between devices: 3.7 us -> 10.1 us  [swap(): return lax.ppermute(value, 'dp', [(i, i ^ bit) for i in range(count)])]
    ppermute x0 -> x2, starting transfers between devices: none -> 3.92 us  [the longest x1 3.35 us: shards(): far = lax.ppermute(sent, 'dp', [(i, i ^ 6) for i in range(0, replicas, 2)])]
    ppermute x15 -> x13, starting transfers between devices: 12.3 us -> 8.88 us  [swap(): return lax.ppermute(value, 'dp', [(i, i ^ bit) for i in range(count)])]
    pallas_call x19 -> x21, Pallas kernels: 37.8 us -> 39.7 us  [call(): pl.pallas_call(body, out_shape=out_shape, in_specs=specs, out_specs=jax.t...]
    pallas_call x1, Pallas kernels: 2.33 us -> 0.89 us  [shards(): pl.pallas_call(emit_kernel, out_shape=like(gi), in_specs=[vmem], out_spec...]
  transfers between devices with their start and end apart: 16 -> 16, of which waited for: 5 -> 5; matrix products, arithmetic and copies ran while one was open for 0% -> 0% of each run, Pallas kernels for 54% -> 56%
where the time goes in v6:
time: 65.9 us; the launch traced here: 65.7 us
  Pallas kernels  40.6 us (62%)
  starting transfers between devices  14.1 us (21%)
  waiting for transfers between devices  10.1 us (15%)
  between operations  0.86 us (1%)
    pallas_call x21, Pallas kernels, call(): pl.pallas_call(body, out_shape=out_shape, in_specs=specs, out_specs=jax.t...  39.7 us
    ppermute x13, waiting for transfers between devices, swap(): return lax.ppermute(value, 'dp', [(i, i ^ bit) for i in range(count)])  10.1 us
    ppermute x13, starting transfers between devices, swap(): return lax.ppermute(value, 'dp', [(i, i ^ bit) for i in range(count)])  8.88 us
    ppermute x1, starting transfers between devices, shards(): far = lax.ppermute(sent, 'dp', [(i, i ^ 6) for i in range(0, replicas, 2)])  3.35 us
  transfers between devices with their start and end apart: 16, of which 5 were waited for; matrix products, arithmetic and copies ran while one was open for 0% of the time, Pallas kernels for 56%

profile of v6, /device:TPU:0, one launch (start us, length us, event | category | flops | bytes accessed | tf_op | source)
XLA Modules:
  0.0 65.7 jit_solution(1036189604066401818)
XLA Ops:
  0.6 1.8 %load.1 = (bf16[512,768]{1,0:T(8,128)(2,1)S(1)}, f32[6,8,80,128]{3,2,1,0:T(8,128)S(1)}, f32[8,768]{1,0:T(8,128)S(1)}, f32[6,91,8,128]{3,2,1,0:T(8,128)S(1)}, bf1...) custom-call(bf16[8,64,768]{2,1,0:T(8,128)(2,1)} %bitcast.14, bf16[8,64,768]{2,1,0:T(8,128)(2,1)} %bitcast.15, ...), custom_call_target="tpu_custom_call" | custom-call | flops 10000000000 | bytes 1000000 | tf_op jit(solution)/shard_map/load/pallas_call | solution.py:25
  2.9 5.8 %front.1 = (bf16[512,768]{1,0:T(8,128)(2,1)S(1)}, f32[512,768]{1,0:T(8,128)S(1)}, f32[512,128]{1,0:T(8,128)S(1)}, bf16[3072,768]{1,0:T(8,128)(2,1)S(1)}, f32[1,3...) custom-call(f32[6,8,80,128]{3,2,1,0:T(8,128)S(1)} %get-tuple-element.84.xp_ref.refs_0_, ...), custom_call_target="tpu_custom_call" | custom-call | flops 10000000000 | bytes 1000000 | tf_op jit(solution)/shard_map/front/pallas_call | solution.py:25
  8.9 1.3 %open.1 = (f32[512,768]{1,0:T(8,128)S(1)}, bf16[384,512]{1,0:T(8,128)(2,1)S(1)}, bf16[384,512]{1,0:T(8,128)(2,1)S(1)}) custom-call(bf16[512,768]{1,0:T(8,128)(2,1)S(1)} %get-tuple-element.88.refs_0_.refs_1_, bf16[3072,768]{1,0:T(8,128)(2,1)S(1)} %get-tuple-element.90.refs_1_.refs_2_, f32[1,3072]{1,0:T(1,128)S(1)} %get-tuple-element.91.refs_2_.refs_3_), custom_call_target="tpu_custom_call" | custom-call | flops 1000000 | bytes 1000 | tf_op jit(solution)/shard_map/open/pallas_call | solution.py:25
  10.2 0.5 collective-permute-start.2
  10.7 0.9 %close.1 = (bf16[512,768]{1,0:T(8,128)(2,1)S(1)}, bf16[384,512]{1,0:T(8,128)(2,1)S(1)}, bf16[384,512]{1,0:T(8,128)(2,1)S(1)}) custom-call(bf16[512,768]{1,0:T(8,128)(2,1)S(1)} %get-tuple-element.89.refs_0_.refs_1_.refs_3_, f32[512,768]{1,0:T(8,128)S(1)} %get-tuple-element.92.refs_1_, bf16[768,3072]{1,0:T(8,128)(2,1)S(1)} %get-tuple-element.87.refs_2_.refs_4_.refs_0_), custom_call_target="tpu_custom_call" | custom-call | flops 1000000 | bytes 1000 | tf_op jit(solution)/shard_map/close/pallas_call | solution.py:25
  12.1 0.8 %half.2 = (bf16[384,768]{1,0:T(8,128)(2,1)S(1)}, f32[8,768]{1,0:T(8,128)S(1)}) custom-call(bf16[512,768]{1,0:T(8,128)(2,1)S(1)} %get-tuple-element.89.refs_0_.refs_1_.refs_3_, bf16[512,768]{1,0:T(8,128)(2,1)S(1)} %collective-permute-done.1.refs_1_.refs_4_, bf16[384,512]{1,0:T(8,128)(2,1)S(1)} %get-tuple-element.97.refs_2_, ...), custom_call_target="tpu_custom_call" | custom-call | flops 1000000 | bytes 1000 | tf_op jit(solution)/shard_map/half/pallas_call | solution.py:25
  12.9 0.6 collective-permute-done.3.refs_3_
  13.4 0.8 %half.3 = bf16[384,768]{1,0:T(8,128)(2,1)S(1)} custom-call(bf16[512,768]{1,0:T(8,128)(2,1)S(1)} %get-tuple-element.88.refs_0_.refs_1_, bf16[512,768]{1,0:T(8,128)(2,1)S(1)} %collective-permute-done.refs_1_.refs_2_, bf16[384,512]{1,0:T(8,128)(2,1)S(1)} %get-tuple-element.96.refs_2_, bf16[384,512]{1,0:T(8,128)(2,1)S(1)} %collective-permute-done.3.refs_3_), custom_call_target="tpu_custom_call" | custom-call | flops 1000000 | bytes 1000 | tf_op jit(solution)/shard_map/half/pallas_call | solution.py:25
  14.2 2.7 %collective-permute-start.7 = (bf16[384,768]{1,0:T(8,128)(2,1)S(1)}, bf16[384,768]{1,0:T(8,128)(2,1)S(1)}, u32[]{:S(2)}, u32[]{:S(2)}) collective-permute-start(bf16[384,768]{1,0:T(8,128)(2,1)S(1)} %half.3), channel_id=1, source_target_pairs={{0,2},{1,3},{2,0},{3,1},{4,6},{5,7},{6,4},{7,5},{8,10},{9,11},{10,... | collective-permute-start | bytes 1769480 | tf_op jit(solution)/shard_map/ppermute | solution.py:419
  16.9 1.5 %collective-permute-start.8 = (bf16[384,768]{1,0:T(8,128)(2,1)S(1)}, bf16[384,768]{1,0:T(8,128)(2,1)S(1)}, u32[]{:S(2)}, u32[]{:S(2)}) collective-permute-start(bf16[384,768]{1,0:T(8,128)(2,1)S(1)} %get-tuple-element.129), channel_id=1, source_target_pairs={{0,4},{1,5},{2,6},{3,7},{4,0},{5,1},{6,2},{7,3},{8,12},{9,13},{10,... | collective-permute-start | bytes 1769480 | tf_op jit(solution)/shard_map/ppermute | solution.py:419
  18.4 3.4 %wide.3 = (f32[512,768]{1,0:T(8,128)S(1)}, f32[8,768]{1,0:T(8,128)S(1)}, f32[8,768]{1,0:T(8,128)S(1)}, bf16[768,512]{1,0:T(8,128)(2,1)S(1)}, bf16[768,512]{1,0:T(8,128)(2,1)S(1)}) custom-call(bf16[512,768]{1,0:T(8,128)(2,1)S(1)} %get-tuple-element.88.refs_0_.refs_1_, bf16[512,768]{1,0:T(8,128)(2,1)S(1)} %get-tuple-element.89.refs_0_.refs_1_.refs_3_, ...), custom_call_target="tpu_custom_call" | custom-call | flops 10000000000 | bytes 1000000 | tf_op jit(solution)/shard_map/wide/pallas_call | solution.py:25
  21.9 2.9 %wide.4 = (f32[512,768]{1,0:T(8,128)S(1)}, f32[8,768]{1,0:T(8,128)S(1)}, bf16[768,512]{1,0:T(8,128)(2,1)S(1)}, bf16[768,512]{1,0:T(8,128)(2,1)S(1)}) custom-call(bf16[512,768]{1,0:T(8,128)(2,1)S(1)} %get-tuple-element.88.refs_0_.refs_1_, bf16[512,768]{1,0:T(8,128)(2,1)S(1)} %get-tuple-element.89.refs_0_.refs_1_.refs_3_, ...), custom_call_target="tpu_custom_call", output_to_operand_aliasing={{0}: (5, {})} | custom-call | flops 10000000000 | bytes 1000000 | tf_op jit(solution)/shard_map/wide/pallas_call | solution.py:25
  24.8 0.5 collective-permute-start.6
  25.4 2.7 %wide.5 = (f32[512,768]{1,0:T(8,128)S(1)}, f32[8,768]{1,0:T(8,128)S(1)}, bf16[768,512]{1,0:T(8,128)(2,1)S(1)}, bf16[768,512]{1,0:T(8,128)(2,1)S(1)}) custom-call(bf16[512,768]{1,0:T(8,128)(2,1)S(1)} %get-tuple-element.88.refs_0_.refs_1_, bf16[512,768]{1,0:T(8,128)(2,1)S(1)} %get-tuple-element.89.refs_0_.refs_1_.refs_3_, ...), custom_call_target="tpu_custom_call", output_to_operand_aliasing={{0}: (5, {})} | custom-call | flops 10000000000 | bytes 1000000 | tf_op jit(solution)/shard_map/wide/pallas_call | solution.py:25
  28.1 1.4 %share.4 = (bf16[384,768]{1,0:T(8,128)(2,1)S(1)}, f32[384,768]{1,0:T(8,128)S(1)}, f32[8,768]{1,0:T(8,128)S(1)}) custom-call(bf16[768,3072]{1,0:T(8,128)(2,1)S(1)} %get-tuple-element.87.refs_2_.refs_4_.refs_0_, bf16[512,768]{1,0:T(8,128)(2,1)S(1)} %get-tuple-element.88.refs_0_.refs_1_, bf16[512,768]{1,0:T(8,128)(2,1)S(1)} %collective-permute-done.refs_1_.refs_2_, ...), custom_call_target="tpu_custom_call" | custom-call | flops 1000000 | bytes 1000 | tf_op jit(solution)/shard_map/share/pallas_call | solution.py:25
  29.5 1.4 %share.5 = (f32[384,768]{1,0:T(8,128)S(1)}, bf16[384,768]{1,0:T(8,128)(2,1)S(1)}, f32[8,768]{1,0:T(8,128)S(1)}) custom-call(bf16[768,3072]{1,0:T(8,128)(2,1)S(1)} %get-tuple-element.87.refs_2_.refs_4_.refs_0_, bf16[512,768]{1,0:T(8,128)(2,1)S(1)} %get-tuple-element.88.refs_0_.refs_1_, bf16[512,768]{1,0:T(8,128)(2,1)S(1)} %collective-permute-done.refs_1_.refs_2_, ...), custom_call_target="tpu_custom_call" | custom-call | flops 1000000 | bytes 1000 | tf_op jit(solution)/shard_map/share/pallas_call | solution.py:25
  30.9 1.3 %slope.1 = (f32[6,8,80,128]{3,2,1,0:T(8,128)S(1)}, f32[8,768]{1,0:T(8,128)S(1)}) custom-call(f32[512,768]{1,0:T(8,128)S(1)} %get-tuple-element.119.gn_ref, f32[512,768]{1,0:T(8,128)S(1)} %get-tuple-element.120.normed_ref, f32[512,128]{1,0:T(8,128)S(1)} %get-tuple-element.121.rstd_ref, f32[8,768]{1,0:T(8,128)S(1)} %get-tuple-element.122.vecs_ref.refs_2_), custom_call_target="tpu_custom_call" | custom-call | flops 1000000 | bytes 1000 | tf_op jit(solution)/shard_map/slope/pallas_call | solution.py:25
  32.6 1.6 %collective-permute-start.10 = (bf16[768,768]{1,0:T(8,128)(2,1)S(1)}, bf16[768,768]{1,0:T(8,128)(2,1)S(1)}, u32[]{:S(2)}, u32[]{:S(2)}) collective-permute-start(bf16[768,768]{1,0:T(8,128)(2,1)S(1)} %relay.3), channel_id=1, source_target_pairs={{0,4},{1,5},{2,6},{3,7},{4,0},{5,1},{6,2},{7,3},{8,12},{9,13},{10,... | collective-permute-start | bytes 3538952 | tf_op jit(solution)/shard_map/ppermute | solution.py:419
  34.1 0.5 collective-permute-start.9
  34.7 5.0 %back.1 = bf16[8,64,768]{2,1,0:T(8,128)(2,1)S(1)} custom-call(f32[6,8,80,128]{3,2,1,0:T(8,128)S(1)} %get-tuple-element.141.refs_1_.gd_ref, bf16[8,64,768]{2,1,0:T(8,128)(2,1)S(1)} %get-tuple-element.156.g_ref, f32[6,91,8,128]{3,2,1,0:T(8,128)S(1)} %get-tuple-element.85.wexp), custom_call_target="tpu_custom_call" | custom-call | flops 1000000 | bytes 1000 | tf_op jit(solution)/shard_map/back/pallas_call | solution.py:25
  39.7 1.3 %collective-permute-start.14 = (bf16[8,64,768]{2,1,0:T(8,128)(2,1)S(1)}, bf16[8,64,768]{2,1,0:T(8,128)(2,1)S(1)}, u32[]{:S(2)}, u32[]{:S(2)}) collective-permute-start(bf16[8,64,768]{2,1,0:T(8,128)(2,1)S(1)} %back.1), channel_id=1, source_target_pairs={{8,0},{16,8},{24,16},{9,1},{17,9},{25,17},{10,2},{18,10},{26,18},{... | collective-permute-start | bytes 2359304 | tf_op jit(solution)/shard_map/ppermute | solution.py:415
  41.0 1.4 %share.3 = (f32[384,768]{1,0:T(8,128)S(1)}, f32[384,768]{1,0:T(8,128)S(1)}, f32[8,768]{1,0:T(8,128)S(1)}) custom-call(bf16[768,3072]{1,0:T(8,128)(2,1)S(1)} %get-tuple-element.87.refs_2_.refs_4_.refs_0_, bf16[512,768]{1,0:T(8,128)(2,1)S(1)} %get-tuple-element.88.refs_0_.refs_1_, bf16[512,768]{1,0:T(8,128)(2,1)S(1)} %collective-permute-done.refs_1_.refs_2_, ...), custom_call_target="tpu_custom_call" | custom-call | flops 1000000 | bytes 1000 | tf_op jit(solution)/shard_map/share/pallas_call | solution.py:25
  42.4 5.8 %taps.1.own_ref = f32[64,768]{1,0:T(8,128)S(1)} custom-call(f32[6,8,80,128]{3,2,1,0:T(8,128)S(1)} %get-tuple-element.84.xp_ref.refs_0_, f32[6,8,80,128]{3,2,1,0:T(8,128)S(1)} %get-tuple-element.141.refs_1_.gd_ref, f32[8,768]{1,0:T(8,128)S(1)} %get-tuple-element.122.vecs_ref.refs_2_, f32[8,768]{1,0:T(8,128)S(1)} %get-tuple-element.142.refs_3_, ...), custom_call_target="tpu_custom_call" | custom-call | flops 1000000 | bytes 1000 | tf_op jit(solution)/shard_map/taps/pallas_call | solution.py:25
  48.2 0.6 collective-permute-start.11
  48.8 1.1 %collective-permute-done.11.got_ref = f32[64,768]{1,0:T(8,128)S(1)} collective-permute-done((f32[64,768]{1,0:T(8,128)S(1)}, f32[64,768]{1,0:T(8,128)S(1)}, u32[]{:S(2)}, u32[]{:S(2)}) %collective-permute-start.11) | collective-permute-done | bytes 196640 | tf_op jit(solution)/shard_map/ppermute | solution.py:419
  49.9 3.3 %collective-permute-start.13 = (bf16[64,768]{1,0:T(8,128)(2,1)S(1)}, bf16[64,768]{1,0:T(8,128)(2,1)S(1)}, u32[]{:S(2)}, u32[]{:S(2)}) collective-permute-start(bf16[64,768]{1,0:T(8,128)(2,1)S(1)} %get-tuple-element.155), channel_id=1, source_target_pairs={{0,6},{2,4},{4,2},{6,0},{8,14},{10,12},{12,10},{14,8},{16,22},{18,... | collective-permute-start | bytes 294920 | tf_op jit(solution)/shard_map/ppermute | solution.py:565
  53.3 0.6 collective-permute-start.12
  53.8 7.6 %collective-permute-done.10.refs_3_ = bf16[768,768]{1,0:T(8,128)(2,1)S(1)} collective-permute-done((bf16[768,768]{1,0:T(8,128)(2,1)S(1)}, bf16[768,768]{1,0:T(8,128)(2,1)S(1)}, u32[]{:S(2)}, u32[]{:S(2)}) %collective-permute-start.10) | collective-permute-done | bytes 1179680 | tf_op jit(solution)/shard_map/ppermute | solution.py:419
  61.5 1.9 %merge.1 = (f32[384,768]{1,0:T(8,128)}, f32[768,384]{1,0:T(8,128)}) custom-call(f32[384,768]{1,0:T(8,128)S(1)} %get-tuple-element.107.refs_0_, f32[384,768]{1,0:T(8,128)S(1)} %get-tuple-element.108.refs_1_, bf16[768,768]{1,0:T(8,128)(2,1)S(1)} %collective-permute-done.9.refs_2_, bf16[768,768]{1,0:T(8,128)(2,1)S(1)} %collective-permute-done.10.refs_3_), custom_call_target="tpu_custom_call" | custom-call | flops 1000000 | bytes 1000 | tf_op jit(solution)/shard_map/merge/pallas_call | solution.py:25
  63.6 0.9 %emit.1 = bf16[8,64,768]{2,1,0:T(8,128)(2,1)} custom-call(bf16[8,64,768]{2,1,0:T(8,128)(2,1)S(1)} %collective-permute-done.14.gi_ref), custom_call_target="tpu_custom_call" | custom-call | tf_op jit(solution)/shard_map/emit/pallas_call | solution.py:574
  64.5 0.5 collective-permute-done.15.refs_1_
  65.0 0.7 %small.1 = (f32[1,3072]{1,0:T(1,128)}, f32[54,1,768]{2,1,0:T(1,128)}) custom-call(f32[64,768]{1,0:T(8,128)S(1)} %gather.1.refs_0_, f32[64,768]{1,0:T(8,128)S(1)} %collective-permute-done.15.refs_1_), custom_call_target="tpu_custom_call" | custom-call | flops 1000000 | bytes 1000 | tf_op jit(solution)/shard_map/small/pallas_call | solution.py:25
  (22 shorter events, 1.6 us)
Async XLA Ops:
  2.4 9.7 %collective-permute-start.1 = (bf16[512,768]{1,0:T(8,128)(2,1)S(1)}, bf16[512,768]{1,0:T(8,128)(2,1)S(1)}, u32[]{:S(2)}, u32[]{:S(2)}) collective-permute-start(bf16[512,768]{1,0:T(8,128)(2,1)S(1)} %get-tuple-element.89.refs_0_.refs_1_.refs_3_), channel_id=1, source_target_pairs={{0,1},{1,0},{2,3},{3,2},{4,5},{5,4},{6,7},{7,6},{8,9},{9,8},{10,11... | collective-permute-start | bytes 2359304 | tf_op jit(solution)/shard_map/ppermute | solution.py:419
  8.8 4.7 %collective-permute-start = (bf16[512,768]{1,0:T(8,128)(2,1)S(1)}, bf16[512,768]{1,0:T(8,128)(2,1)S(1)}, u32[]{:S(2)}, u32[]{:S(2)}) collective-permute-start(bf16[512,768]{1,0:T(8,128)(2,1)S(1)} %get-tuple-element.88.refs_0_.refs_1_), channel_id=1, source_target_pairs={{0,1},{1,0},{2,3},{3,2},{4,5},{5,4},{6,7},{7,6},{8,9},{9,8},{10,11... | collective-permute-start | bytes 2359304 | tf_op jit(solution)/shard_map/ppermute | solution.py:419
  10.2 1.9 %collective-permute-start.2 = (bf16[384,512]{1,0:T(8,128)(2,1)S(1)}, bf16[384,512]{1,0:T(8,128)(2,1)S(1)}, u32[]{:S(2)}, u32[]{:S(2)}) collective-permute-start(bf16[384,512]{1,0:T(8,128)(2,1)S(1)} %get-tuple-element.94), channel_id=1, source_target_pairs={{0,1},{1,0},{2,3},{3,2},{4,5},{5,4},{6,7},{7,6},{8,9},{9,8},{10,11... | collective-permute-start | bytes 1179656 | tf_op jit(solution)/shard_map/ppermute | solution.py:419
  11.7 1.8 %collective-permute-start.3 = (bf16[384,512]{1,0:T(8,128)(2,1)S(1)}, bf16[384,512]{1,0:T(8,128)(2,1)S(1)}, u32[]{:S(2)}, u32[]{:S(2)}) collective-permute-start(bf16[384,512]{1,0:T(8,128)(2,1)S(1)} %get-tuple-element.100), channel_id=1, source_target_pairs={{0,1},{1,0},{2,3},{3,2},{4,5},{5,4},{6,7},{7,6},{8,9},{9,8},{10,11... | collective-permute-start | bytes 1179656 | tf_op jit(solution)/shard_map/ppermute | solution.py:419
  14.2 18.0 %collective-permute-start.7 = (bf16[384,768]{1,0:T(8,128)(2,1)S(1)}, bf16[384,768]{1,0:T(8,128)(2,1)S(1)}, u32[]{:S(2)}, u32[]{:S(2)}) collective-permute-start(bf16[384,768]{1,0:T(8,128)(2,1)S(1)} %half.3), channel_id=1, source_target_pairs={{0,2},{1,3},{2,0},{3,1},{4,6},{5,7},{6,4},{7,5},{8,10},{9,11},{10,... | collective-permute-start | bytes 1769480 | tf_op jit(solution)/shard_map/ppermute | solution.py:419
  16.9 15.3 %collective-permute-start.8 = (bf16[384,768]{1,0:T(8,128)(2,1)S(1)}, bf16[384,768]{1,0:T(8,128)(2,1)S(1)}, u32[]{:S(2)}, u32[]{:S(2)}) collective-permute-start(bf16[384,768]{1,0:T(8,128)(2,1)S(1)} %get-tuple-element.129), channel_id=1, source_target_pairs={{0,4},{1,5},{2,6},{3,7},{4,0},{5,1},{6,2},{7,3},{8,12},{9,13},{10,... | collective-permute-start | bytes 1769480 | tf_op jit(solution)/shard_map/ppermute | solution.py:419
  21.8 6.2 %collective-permute-start.5 = (bf16[768,512]{1,0:T(8,128)(2,1)S(1)}, bf16[768,512]{1,0:T(8,128)(2,1)S(1)}, u32[]{:S(2)}, u32[]{:S(2)}) collective-permute-start(bf16[768,512]{1,0:T(8,128)(2,1)S(1)} %get-tuple-element.112), channel_id=1, source_target_pairs={{0,1},{1,0},{2,3},{3,2},{4,5},{5,4},{6,7},{7,6},{8,9},{9,8},{10,11... | collective-permute-start | bytes 2359304 | tf_op jit(solution)/shard_map/ppermute | solution.py:419
  24.8 4.7 %collective-permute-start.6 = (bf16[768,512]{1,0:T(8,128)(2,1)S(1)}, bf16[768,512]{1,0:T(8,128)(2,1)S(1)}, u32[]{:S(2)}, u32[]{:S(2)}) collective-permute-start(bf16[768,512]{1,0:T(8,128)(2,1)S(1)} %get-tuple-element.115), channel_id=1, source_target_pairs={{0,1},{1,0},{2,3},{3,2},{4,5},{5,4},{6,7},{7,6},{8,9},{9,8},{10,11... | collective-permute-start | bytes 2359304 | tf_op jit(solution)/shard_map/ppermute | solution.py:419
  32.6 28.9 %collective-permute-start.10 = (bf16[768,768]{1,0:T(8,128)(2,1)S(1)}, bf16[768,768]{1,0:T(8,128)(2,1)S(1)}, u32[]{:S(2)}, u32[]{:S(2)}) collective-permute-start(bf16[768,768]{1,0:T(8,128)(2,1)S(1)} %relay.3), channel_id=1, source_target_pairs={{0,4},{1,5},{2,6},{3,7},{4,0},{5,1},{6,2},{7,3},{8,12},{9,13},{10,... | collective-permute-start | bytes 3538952 | tf_op jit(solution)/shard_map/ppermute | solution.py:419
  34.1 27.3 %collective-permute-start.9 = (bf16[768,768]{1,0:T(8,128)(2,1)S(1)}, bf16[768,768]{1,0:T(8,128)(2,1)S(1)}, u32[]{:S(2)}, u32[]{:S(2)}) collective-permute-start(bf16[768,768]{1,0:T(8,128)(2,1)S(1)} %relay.2), channel_id=1, source_target_pairs={{0,2},{1,3},{2,0},{3,1},{4,6},{5,7},{6,4},{7,5},{8,10},{9,11},{10,... | collective-permute-start | bytes 3538952 | tf_op jit(solution)/shard_map/ppermute | solution.py:419
  34.7 6.3 %collective-permute-start.4 = (bf16[768,512]{1,0:T(8,128)(2,1)S(1)}, bf16[768,512]{1,0:T(8,128)(2,1)S(1)}, u32[]{:S(2)}, u32[]{:S(2)}) collective-permute-start(bf16[768,512]{1,0:T(8,128)(2,1)S(1)} %get-tuple-element.106), channel_id=1, source_target_pairs={{0,1},{1,0},{2,3},{3,2},{4,5},{5,4},{6,7},{7,6},{8,9},{9,8},{10,11... | collective-permute-start | bytes 2359304 | tf_op jit(solution)/shard_map/ppermute | solution.py:419
  39.7 23.8 %collective-permute-start.14 = (bf16[8,64,768]{2,1,0:T(8,128)(2,1)S(1)}, bf16[8,64,768]{2,1,0:T(8,128)(2,1)S(1)}, u32[]{:S(2)}, u32[]{:S(2)}) collective-permute-start(bf16[8,64,768]{2,1,0:T(8,128)(2,1)S(1)} %back.1), channel_id=1, source_target_pairs={{8,0},{16,8},{24,16},{9,1},{17,9},{25,17},{10,2},{18,10},{26,18},{... | collective-permute-start | bytes 2359304 | tf_op jit(solution)/shard_map/ppermute | solution.py:415
  48.2 1.7 %collective-permute-start.11 = (f32[64,768]{1,0:T(8,128)S(1)}, f32[64,768]{1,0:T(8,128)S(1)}, u32[]{:S(2)}, u32[]{:S(2)}) collective-permute-start(f32[64,768]{1,0:T(8,128)S(1)} %taps.1.own_ref), channel_id=1, source_target_pairs={{0,1},{1,0},{2,3},{3,2},{4,5},{5,4},{6,7},{7,6},{8,9},{9,8},{10,11... | collective-permute-start | bytes 589832 | tf_op jit(solution)/shard_map/ppermute | solution.py:419
  49.9 13.5 %collective-permute-start.13 = (bf16[64,768]{1,0:T(8,128)(2,1)S(1)}, bf16[64,768]{1,0:T(8,128)(2,1)S(1)}, u32[]{:S(2)}, u32[]{:S(2)}) collective-permute-start(bf16[64,768]{1,0:T(8,128)(2,1)S(1)} %get-tuple-element.155), channel_id=1, source_target_pairs={{0,6},{2,4},{4,2},{6,0},{8,14},{10,12},{12,10},{14,8},{16,22},{18,... | collective-permute-start | bytes 294920 | tf_op jit(solution)/shard_map/ppermute | solution.py:565
  53.3 10.2 %collective-permute-start.12 = (bf16[64,768]{1,0:T(8,128)(2,1)S(1)}, bf16[64,768]{1,0:T(8,128)(2,1)S(1)}, u32[]{:S(2)}, u32[]{:S(2)}) collective-permute-start(bf16[64,768]{1,0:T(8,128)(2,1)S(1)} %get-tuple-element.155), channel_id=1, source_target_pairs={{0,2},{1,5},{2,0},{3,7},{4,6},{5,1},{6,4},{7,3},{8,10},{9,13},{10,... | collective-permute-start | bytes 294920 | tf_op jit(solution)/shard_map/ppermute | solution.py:564
  63.5 1.5 %collective-permute-start.15 = (f32[64,768]{1,0:T(8,128)S(1)}, f32[64,768]{1,0:T(8,128)S(1)}, u32[]{:S(2)}, u32[]{:S(2)}) collective-permute-start(f32[64,768]{1,0:T(8,128)S(1)} %gather.1.refs_0_), channel_id=1, source_target_pairs={{0,1},{1,0},{2,3},{3,2},{4,5},{5,4},{6,7},{7,6},{8,9},{9,8},{10,11... | collective-permute-start | bytes 589832 | tf_op jit(solution)/shard_map/ppermute | solution.py:419

commit v7 on v6

--- a/solution.py
+++ b/solution.py
@@ -115,14 +115,10 @@
     expand_taps(w_ref, wexp, blocks)
     copies[1].wait()
     copies[2].wait()
-    b2, gs = [], []
     for c in range(blocks):
         lanes = slice(c * LANES, (c + 1) * LANES)
         g = g_ref[:, :, lanes].astype(f32).reshape(rows * cols, LANES)
-        gp = (g * tmp_ref[3:4, lanes]).astype(bf16)
-        gp_ref[:, lanes] = gp
-        b2.append(jnp.sum(gp.astype(f32), axis=0, keepdims=True))
-        gs.append(jnp.sum(g, axis=0, keepdims=True))
+        gp_ref[:, lanes] = (g * tmp_ref[3:4, lanes]).astype(bf16)
     copies[3].wait()
     for c in range(blocks):
         xp_ref[c, :, EDGE : EDGE + cols, :] = x_ref[:, :, c * LANES : (c + 1) * LANES].astype(f32)
@@ -131,13 +127,11 @@
     vecs_ref[0:1, :] = tmp_ref[1:2, :]
     vecs_ref[1:2, :] = tmp_ref[3:4, :]
     vecs_ref[2:3, :] = tmp_ref[4:5, :]
-    vecs_ref[3:4, :] = jnp.concatenate(b2, axis=1)
-    vecs_ref[4:5, :] = jnp.concatenate(gs, axis=1)
-    vecs_ref[5:8, :] = jnp.zeros((3, chans), f32)
+    vecs_ref[3:8, :] = jnp.zeros((5, chans), f32)
 
 
 def front_kernel(xp_ref, wexp, tmp_ref, w1_hbm, b1_hbm, w2_hbm,
-                 yn_ref, normed_ref, rstd_ref, w1_ref, b1_ref, w2_ref, mean_ref, sems):
+                 yn_ref, normed_ref, rstd_ref, mean_ref, w1_ref, b1_ref, w2_ref, sems):
     blocks, rows, padded, _ = xp_ref.shape
     cols = padded - 2 * EDGE
     chans = blocks * LANES
@@ -184,7 +178,6 @@
         for c in range(blocks):
             lanes = slice(c * LANES, (c + 1) * LANES)
             normed = (normed_ref[at, lanes] - mean) * rs
-            normed_ref[at, lanes] = normed
             yn_ref[at, lanes] = (normed * gain[:, lanes] + shift[:, lanes]).astype(bf16)
         return carry
 
@@ -288,7 +281,7 @@
     pack_ref[part:, :] = (base_ref[...] + more_ref[...].astype(f32)).astype(bf16)
 
 
-def slope_kernel(gn_ref, normed_ref, rstd_ref, vecs_ref, gd_ref, sums_ref):
+def slope_kernel(gn_ref, raw_ref, mean_ref, rstd_ref, vecs_ref, gp_ref, g_ref, gd_ref, sums_ref):
     blocks, rows, padded, _ = gd_ref.shape
     cols = padded - 2 * EDGE
     chans = blocks * LANES
@@ -298,23 +291,24 @@
     def norm_step(r, carry):
         at = pl.ds(pl.multiple_of(r * cols, cols), cols)
         gn = gn_ref[at, :]
-        normed = normed_ref[at, :]
+        rs = rstd_ref[at, 0:1]
+        normed = (raw_ref[at, :] - mean_ref[at, 0:1]) * rs
         prod = gn * normed
         scaled = gn * gain
         mean_a = jnp.mean(scaled, axis=-1, keepdims=True)
         mean_b = jnp.mean(prod * gain, axis=-1, keepdims=True)
-        rs = rstd_ref[at, 0:1]
         gd = rs * (scaled - mean_a - normed * mean_b)
         for c in range(blocks):
             gd_ref[c, r, EDGE : EDGE + cols, :] = gd[:, c * LANES : (c + 1) * LANES]
         fold = lambda v: jnp.sum(v.reshape(cols // 8, 8, chans), axis=0)
-        return carry[0] + fold(gd), carry[1] + fold(prod), carry[2] + fold(gn)
+        parts = (gd, prod, gn, gp_ref[at, :].astype(f32), g_ref[r].astype(f32))
+        return tuple(old + fold(part) for old, part in zip(carry, parts))
 
     zero = jnp.zeros((8, chans), f32)
-    sums = lax.fori_loop(0, rows, norm_step, (zero, zero, zero))
-    for k in range(3):
+    sums = lax.fori_loop(0, rows, norm_step, (zero,) * 5)
+    for k in range(5):
         sums_ref[k : k + 1, :] = jnp.sum(sums[k], axis=0, keepdims=True)
-    sums_ref[3:8, :] = jnp.zeros((5, chans), f32)
+    sums_ref[5:8, :] = jnp.zeros((3, chans), f32)
 
 
 def back_kernel(gd_ref, g_ref, wexp, gi_ref):
@@ -361,11 +355,11 @@
     small_ref[taps:, :] = jnp.zeros((small_ref.shape[0] - taps, chans), f32)
     lax.fori_loop(0, blocks, step, 0)
     small_ref[taps : taps + 3, :] = sums_ref[0:3, :]
-    small_ref[taps + 3 : taps + 4, :] = vecs_ref[3:4, :]
+    small_ref[taps + 3 : taps + 4, :] = sums_ref[3:4, :]
     if fast:
         scales, bsums = more[:4], more[4:]
         total = scales[0][...] + scales[1][...] + scales[2][...] + scales[3][...]
-        row = jnp.sum(total, axis=0, keepdims=True) / vecs_ref[1:2, :] + vecs_ref[2:3, :] * vecs_ref[4:5, :]
+        row = jnp.sum(total, axis=0, keepdims=True) / vecs_ref[1:2, :] + vecs_ref[2:3, :] * sums_ref[4:5, :]
         small_ref[taps + 4 : taps + 5, :] = row
         chip, _ = place()
         for k in range(4):
@@ -458,13 +452,13 @@
         name="load", in_specs=[hbm] * 8, cost=estimate(1e10, 1e6),
         scratch=[pltpu.VMEM(x.shape, bf16), pltpu.VMEM((taps, chans), bf16), pltpu.SemaphoreType.DMA((8,))],
     )
-    yn, normed, rstd, w1, b1, w2 = call(
+    yn, normed, rstd, mean, w1, b1, w2 = call(
         front_kernel,
         (struct((cells, chans), bf16), struct((cells, chans), f32), struct((cells, LANES), f32),
-         like(w1), like(pw1_bias), like(w2)),
+         struct((cells, LANES), f32), like(w1), like(pw1_bias), like(w2)),
         xp, wexp, tmp, *pin(w1, pw1_bias, w2),
         name="front", in_specs=[vmem] * 3 + [hbm] * 3, cost=estimate(1e10, 1e6),
-        scratch=[pltpu.VMEM((cells, LANES), f32), pltpu.SemaphoreType.DMA((3,))],
+        scratch=[pltpu.SemaphoreType.DMA((3,))],
     )
 
     def wide_step(slot, mode, *more, other=None):
@@ -480,7 +474,7 @@
         return lambda chip: lax.bitwise_xor(chip, k)
 
     def slope(gn):
-        return call(slope_kernel, (padded, struct((8, chans), f32)), gn, normed, rstd, vecs,
+        return call(slope_kernel, (padded, struct((8, chans), f32)), gn, normed, mean, rstd, vecs, gp, gv,
                     name="slope", cost=estimate(1e6, 1e3))
 
     if fast:
@@ -584,7 +578,7 @@
         small = jnp.transpose(small, (1, 0, 2))
     else:
         scale_sum = jnp.sum(g2 * w2.astype(f32), axis=1)
-        gscale = scale_sum / layer_scale[0] + pw2_bias[0] * vecs[4]
+        gscale = scale_sum / layer_scale[0] + pw2_bias[0] * sums[4]
         small = jnp.concatenate([small[: taps + 4], gscale[None], *bsums], axis=0)
         small = lax.psum(small, "dp")
         out1 = lax.psum_scatter(g1, "dp", scatter_dimension=0, tiled=True) * factor

time: 65.9 us -> 66.1 us (level)
  transfers between devices with their start and end apart: 16 -> 16, of which waited for: 5 -> 5; matrix products, arithmetic and copies ran while one was open for 0% -> 0% of each run, Pallas kernels for 56% -> 57%
where the time goes in v7:
time: 66.1 us; the launch traced here: 65.9 us
  Pallas kernels  40.8 us (62%)
  starting transfers between devices  14.1 us (21%)
  waiting for transfers between devices  10.1 us (15%)
  between operations  0.87 us (1%)
    pallas_call x21, Pallas kernels, call(): pl.pallas_call(body, out_shape=out_shape, in_specs=specs, out_specs=jax.t...  39.9 us
    ppermute x13, waiting for transfers between devices, swap(): return lax.ppermute(value, 'dp', [(i, i ^ bit) for i in range(count)])  10.1 us
    ppermute x13, starting transfers between devices, swap(): return lax.ppermute(value, 'dp', [(i, i ^ bit) for i in range(count)])  8.53 us
    ppermute x1, starting transfers between devices, shards(): far = lax.ppermute(sent, 'dp', [(i, i ^ 6) for i in range(0, replicas, 2)])  3.69 us
  transfers between devices with their start and end apart: 16, of which 5 were waited for; matrix products, arithmetic and copies ran while one was open for 0% of the time, Pallas kernels for 57%

profile of v7, /device:TPU:0, one launch (start us, length us, event | category | flops | bytes accessed | tf_op | source)
XLA Modules:
  0.0 65.9 jit_solution(555336356355898513)
XLA Ops:
  0.6 1.6 %load.1 = (bf16[512,768]{1,0:T(8,128)(2,1)S(1)}, f32[6,8,80,128]{3,2,1,0:T(8,128)S(1)}, f32[8,768]{1,0:T(8,128)S(1)}, f32[6,91,8,128]{3,2,1,0:T(8,128)S(1)}, bf1...) custom-call(bf16[8,64,768]{2,1,0:T(8,128)(2,1)} %bitcast.14, bf16[8,64,768]{2,1,0:T(8,128)(2,1)} %bitcast.15, ...), custom_call_target="tpu_custom_call" | custom-call | flops 10000000000 | bytes 1000000 | tf_op jit(solution)/shard_map/load/pallas_call | solution.py:25
  2.3 0.5 collective-permute-start.1
  2.8 5.8 %front.1 = (bf16[512,768]{1,0:T(8,128)(2,1)S(1)}, f32[512,768]{1,0:T(8,128)S(1)}, f32[512,128]{1,0:T(8,128)S(1)}, f32[512,128]{1,0:T(8,128)S(1)}, bf16[3072,768]...) custom-call(f32[6,8,80,128]{3,2,1,0:T(8,128)S(1)} %get-tuple-element.85.xp_ref.refs_0_, ...), custom_call_target="tpu_custom_call" | custom-call | flops 10000000000 | bytes 1000000 | tf_op jit(solution)/shard_map/front/pallas_call | solution.py:25
  8.7 1.3 %open.1 = (f32[512,768]{1,0:T(8,128)S(1)}, bf16[384,512]{1,0:T(8,128)(2,1)S(1)}, bf16[384,512]{1,0:T(8,128)(2,1)S(1)}) custom-call(bf16[512,768]{1,0:T(8,128)(2,1)S(1)} %get-tuple-element.89.refs_0_.refs_1_, bf16[3072,768]{1,0:T(8,128)(2,1)S(1)} %get-tuple-element.91.refs_1_.refs_2_, f32[1,3072]{1,0:T(1,128)S(1)} %get-tuple-element.92.refs_2_.refs_3_), custom_call_target="tpu_custom_call" | custom-call | flops 1000000 | bytes 1000 | tf_op jit(solution)/shard_map/open/pallas_call | solution.py:25
  10.6 0.9 %close.1 = (bf16[512,768]{1,0:T(8,128)(2,1)S(1)}, bf16[384,512]{1,0:T(8,128)(2,1)S(1)}, bf16[384,512]{1,0:T(8,128)(2,1)S(1)}) custom-call(bf16[512,768]{1,0:T(8,128)(2,1)S(1)} %get-tuple-element.90.refs_0_.refs_1_.refs_3_.gp_ref, f32[512,768]{1,0:T(8,128)S(1)} %get-tuple-element.93.refs_1_, bf16[768,3072]{1,0:T(8,128)(2,1)S(1)} %get-tuple-element.88.refs_2_.refs_4_.refs_0_), custom_call_target="tpu_custom_call" | custom-call | flops 1000000 | bytes 1000 | tf_op jit(solution)/shard_map/close/pallas_call | solution.py:25
  11.9 0.8 %half.2 = (bf16[384,768]{1,0:T(8,128)(2,1)S(1)}, f32[8,768]{1,0:T(8,128)S(1)}) custom-call(bf16[512,768]{1,0:T(8,128)(2,1)S(1)} %get-tuple-element.90.refs_0_.refs_1_.refs_3_.gp_ref, bf16[512,768]{1,0:T(8,128)(2,1)S(1)} %collective-permute-done.1.refs_1_.refs_4_, bf16[384,512]{1,0:T(8,128)(2,1)S(1)} %get-tuple-element.98.refs_2_, ...), custom_call_target="tpu_custom_call" | custom-call | flops 1000000 | bytes 1000 | tf_op jit(solution)/shard_map/half/pallas_call | solution.py:25
  12.7 0.6 collective-permute-done.3.refs_3_
  13.3 0.8 %half.3 = bf16[384,768]{1,0:T(8,128)(2,1)S(1)} custom-call(bf16[512,768]{1,0:T(8,128)(2,1)S(1)} %get-tuple-element.89.refs_0_.refs_1_, bf16[512,768]{1,0:T(8,128)(2,1)S(1)} %collective-permute-done.refs_1_.refs_2_, bf16[384,512]{1,0:T(8,128)(2,1)S(1)} %get-tuple-element.97.refs_2_, bf16[384,512]{1,0:T(8,128)(2,1)S(1)} %collective-permute-done.3.refs_3_), custom_call_target="tpu_custom_call" | custom-call | flops 1000000 | bytes 1000 | tf_op jit(solution)/shard_map/half/pallas_call | solution.py:25
  14.1 2.7 %collective-permute-start.7 = (bf16[384,768]{1,0:T(8,128)(2,1)S(1)}, bf16[384,768]{1,0:T(8,128)(2,1)S(1)}, u32[]{:S(2)}, u32[]{:S(2)}) collective-permute-start(bf16[384,768]{1,0:T(8,128)(2,1)S(1)} %half.3), channel_id=1, source_target_pairs={{0,2},{1,3},{2,0},{3,1},{4,6},{5,7},{6,4},{7,5},{8,10},{9,11},{10,... | collective-permute-start | bytes 1769480 | tf_op jit(solution)/shard_map/ppermute | solution.py:413
  16.8 1.5 %collective-permute-start.8 = (bf16[384,768]{1,0:T(8,128)(2,1)S(1)}, bf16[384,768]{1,0:T(8,128)(2,1)S(1)}, u32[]{:S(2)}, u32[]{:S(2)}) collective-permute-start(bf16[384,768]{1,0:T(8,128)(2,1)S(1)} %get-tuple-element.132), channel_id=1, source_target_pairs={{0,4},{1,5},{2,6},{3,7},{4,0},{5,1},{6,2},{7,3},{8,12},{9,13},{10,... | collective-permute-start | bytes 1769480 | tf_op jit(solution)/shard_map/ppermute | solution.py:413
  18.3 3.4 %wide.3 = (f32[512,768]{1,0:T(8,128)S(1)}, f32[8,768]{1,0:T(8,128)S(1)}, f32[8,768]{1,0:T(8,128)S(1)}, bf16[768,512]{1,0:T(8,128)(2,1)S(1)}, bf16[768,512]{1,0:T(8,128)(2,1)S(1)}) custom-call(bf16[512,768]{1,0:T(8,128)(2,1)S(1)} %get-tuple-element.89.refs_0_.refs_1_, bf16[512,768]{1,0:T(8,128)(2,1)S(1)} %get-tuple-element.90.refs_0_.refs_1_.refs_3_.gp_ref, ...), custom_call_target="tpu_custom_call" | custom-call | flops 10000000000 | bytes 1000000 | tf_op jit(solution)/shard_map/wide/pallas_call | solution.py:25
  21.8 2.9 %wide.4 = (f32[512,768]{1,0:T(8,128)S(1)}, f32[8,768]{1,0:T(8,128)S(1)}, bf16[768,512]{1,0:T(8,128)(2,1)S(1)}, bf16[768,512]{1,0:T(8,128)(2,1)S(1)}) custom-call(bf16[512,768]{1,0:T(8,128)(2,1)S(1)} %get-tuple-element.89.refs_0_.refs_1_, bf16[512,768]{1,0:T(8,128)(2,1)S(1)} %get-tuple-element.90.refs_0_.refs_1_.refs_3_.gp_ref, ...), custom_call_target="tpu_custom_call", output_to_operand_aliasing={{0}: (5, {})} | custom-call | flops 10000000000 | bytes 1000000 | tf_op jit(solution)/shard_map/wide/pallas_call | solution.py:25
  24.7 0.5 collective-permute-start.6
  25.2 2.7 %wide.5 = (f32[512,768]{1,0:T(8,128)S(1)}, f32[8,768]{1,0:T(8,128)S(1)}, bf16[768,512]{1,0:T(8,128)(2,1)S(1)}, bf16[768,512]{1,0:T(8,128)(2,1)S(1)}) custom-call(bf16[512,768]{1,0:T(8,128)(2,1)S(1)} %get-tuple-element.89.refs_0_.refs_1_, bf16[512,768]{1,0:T(8,128)(2,1)S(1)} %get-tuple-element.90.refs_0_.refs_1_.refs_3_.gp_ref, ...), custom_call_target="tpu_custom_call", output_to_operand_aliasing={{0}: (5, {})} | custom-call | flops 10000000000 | bytes 1000000 | tf_op jit(solution)/shard_map/wide/pallas_call | solution.py:25
  27.9 1.4 %share.4 = (bf16[384,768]{1,0:T(8,128)(2,1)S(1)}, f32[384,768]{1,0:T(8,128)S(1)}, f32[8,768]{1,0:T(8,128)S(1)}) custom-call(bf16[768,3072]{1,0:T(8,128)(2,1)S(1)} %get-tuple-element.88.refs_2_.refs_4_.refs_0_, bf16[512,768]{1,0:T(8,128)(2,1)S(1)} %get-tuple-element.89.refs_0_.refs_1_, bf16[512,768]{1,0:T(8,128)(2,1)S(1)} %collective-permute-done.refs_1_.refs_2_, ...), custom_call_target="tpu_custom_call" | custom-call | flops 1000000 | bytes 1000 | tf_op jit(solution)/shard_map/share/pallas_call | solution.py:25
  29.3 1.4 %share.5 = (f32[384,768]{1,0:T(8,128)S(1)}, bf16[384,768]{1,0:T(8,128)(2,1)S(1)}, f32[8,768]{1,0:T(8,128)S(1)}) custom-call(bf16[768,3072]{1,0:T(8,128)(2,1)S(1)} %get-tuple-element.88.refs_2_.refs_4_.refs_0_, bf16[512,768]{1,0:T(8,128)(2,1)S(1)} %get-tuple-element.89.refs_0_.refs_1_, bf16[512,768]{1,0:T(8,128)(2,1)S(1)} %collective-permute-done.refs_1_.refs_2_, ...), custom_call_target="tpu_custom_call" | custom-call | flops 1000000 | bytes 1000 | tf_op jit(solution)/shard_map/share/pallas_call | solution.py:25
  30.7 1.7 %slope.1 = (f32[6,8,80,128]{3,2,1,0:T(8,128)S(1)}, f32[8,768]{1,0:T(8,128)S(1)}) custom-call(f32[512,768]{1,0:T(8,128)S(1)} %get-tuple-element.120.gn_ref, f32[512,768]{1,0:T(8,128)S(1)} %get-tuple-element.121.raw_ref, f32[512,128]{1,0:T(8,128)S(1)} %get-tuple-element.122.mean_ref, f32[512,128]{1,0:T(8,128)S(1)} %get-tuple-element.123.rstd_ref, ...), custom_call_target="tpu_custom_call" | custom-call | flops 1000000 | bytes 1000 | tf_op jit(solution)/shard_map/slope/pallas_call | solution.py:25
  32.8 1.2 %collective-permute-start.10 = (bf16[768,768]{1,0:T(8,128)(2,1)S(1)}, bf16[768,768]{1,0:T(8,128)(2,1)S(1)}, u32[]{:S(2)}, u32[]{:S(2)}) collective-permute-start(bf16[768,768]{1,0:T(8,128)(2,1)S(1)} %relay.3), channel_id=1, source_target_pairs={{0,4},{1,5},{2,6},{3,7},{4,0},{5,1},{6,2},{7,3},{8,12},{9,13},{10,... | collective-permute-start | bytes 3538952 | tf_op jit(solution)/shard_map/ppermute | solution.py:413
  34.0 0.5 collective-permute-start.9
  34.5 5.0 %back.1 = bf16[8,64,768]{2,1,0:T(8,128)(2,1)S(1)} custom-call(f32[6,8,80,128]{3,2,1,0:T(8,128)S(1)} %get-tuple-element.144.refs_1_.gd_ref, bf16[8,64,768]{2,1,0:T(8,128)(2,1)S(1)} %get-tuple-element.125.g_ref, f32[6,91,8,128]{3,2,1,0:T(8,128)S(1)} %get-tuple-element.86.wexp), custom_call_target="tpu_custom_call" | custom-call | flops 1000000 | bytes 1000 | tf_op jit(solution)/shard_map/back/pallas_call | solution.py:25
  39.6 1.3 %collective-permute-start.14 = (bf16[8,64,768]{2,1,0:T(8,128)(2,1)S(1)}, bf16[8,64,768]{2,1,0:T(8,128)(2,1)S(1)}, u32[]{:S(2)}, u32[]{:S(2)}) collective-permute-start(bf16[8,64,768]{2,1,0:T(8,128)(2,1)S(1)} %back.1), channel_id=1, source_target_pairs={{8,0},{16,8},{24,16},{9,1},{17,9},{25,17},{10,2},{18,10},{26,18},{... | collective-permute-start | bytes 2359304 | tf_op jit(solution)/shard_map/ppermute | solution.py:409
  40.9 1.4 %share.3 = (f32[384,768]{1,0:T(8,128)S(1)}, f32[384,768]{1,0:T(8,128)S(1)}, f32[8,768]{1,0:T(8,128)S(1)}) custom-call(bf16[768,3072]{1,0:T(8,128)(2,1)S(1)} %get-tuple-element.88.refs_2_.refs_4_.refs_0_, bf16[512,768]{1,0:T(8,128)(2,1)S(1)} %get-tuple-element.89.refs_0_.refs_1_, bf16[512,768]{1,0:T(8,128)(2,1)S(1)} %collective-permute-done.refs_1_.refs_2_, ...), custom_call_target="tpu_custom_call" | custom-call | flops 1000000 | bytes 1000 | tf_op jit(solution)/shard_map/share/pallas_call | solution.py:25
  42.3 5.8 %taps.1.own_ref = f32[64,768]{1,0:T(8,128)S(1)} custom-call(f32[6,8,80,128]{3,2,1,0:T(8,128)S(1)} %get-tuple-element.85.xp_ref.refs_0_, f32[6,8,80,128]{3,2,1,0:T(8,128)S(1)} %get-tuple-element.144.refs_1_.gd_ref, f32[8,768]{1,0:T(8,128)S(1)} %get-tuple-element.124.vecs_ref.refs_2_, f32[8,768]{1,0:T(8,128)S(1)} %get-tuple-element.145.refs_3_, ...), custom_call_target="tpu_custom_call" | custom-call | flops 1000000 | bytes 1000 | tf_op jit(solution)/shard_map/taps/pallas_call | solution.py:25
  48.1 0.6 collective-permute-start.11
  48.7 1.1 %collective-permute-done.11.got_ref = f32[64,768]{1,0:T(8,128)S(1)} collective-permute-done((f32[64,768]{1,0:T(8,128)S(1)}, f32[64,768]{1,0:T(8,128)S(1)}, u32[]{:S(2)}, u32[]{:S(2)}) %collective-permute-start.11) | collective-permute-done | bytes 196640 | tf_op jit(solution)/shard_map/ppermute | solution.py:413
  49.8 3.7 %collective-permute-start.13 = (bf16[64,768]{1,0:T(8,128)(2,1)S(1)}, bf16[64,768]{1,0:T(8,128)(2,1)S(1)}, u32[]{:S(2)}, u32[]{:S(2)}) collective-permute-start(bf16[64,768]{1,0:T(8,128)(2,1)S(1)} %get-tuple-element.158), channel_id=1, source_target_pairs={{0,6},{2,4},{4,2},{6,0},{8,14},{10,12},{12,10},{14,8},{16,22},{18,... | collective-permute-start | bytes 294920 | tf_op jit(solution)/shard_map/ppermute | solution.py:559
  53.5 0.6 collective-permute-start.12
  54.0 7.6 %collective-permute-done.10.refs_3_ = bf16[768,768]{1,0:T(8,128)(2,1)S(1)} collective-permute-done((bf16[768,768]{1,0:T(8,128)(2,1)S(1)}, bf16[768,768]{1,0:T(8,128)(2,1)S(1)}, u32[]{:S(2)}, u32[]{:S(2)}) %collective-permute-start.10) | collective-permute-done | bytes 1179680 | tf_op jit(solution)/shard_map/ppermute | solution.py:413
  61.7 1.9 %merge.1 = (f32[384,768]{1,0:T(8,128)}, f32[768,384]{1,0:T(8,128)}) custom-call(f32[384,768]{1,0:T(8,128)S(1)} %get-tuple-element.108.refs_0_, f32[384,768]{1,0:T(8,128)S(1)} %get-tuple-element.109.refs_1_, bf16[768,768]{1,0:T(8,128)(2,1)S(1)} %collective-permute-done.9.refs_2_, bf16[768,768]{1,0:T(8,128)(2,1)S(1)} %collective-permute-done.10.refs_3_), custom_call_target="tpu_custom_call" | custom-call | flops 1000000 | bytes 1000 | tf_op jit(solution)/shard_map/merge/pallas_call | solution.py:25
  63.8 0.9 %emit.1 = bf16[8,64,768]{2,1,0:T(8,128)(2,1)} custom-call(bf16[8,64,768]{2,1,0:T(8,128)(2,1)S(1)} %collective-permute-done.14.gi_ref), custom_call_target="tpu_custom_call" | custom-call | tf_op jit(solution)/shard_map/emit/pallas_call | solution.py:568
  64.6 0.5 collective-permute-done.15.refs_1_
  65.2 0.7 %small.1 = (f32[1,3072]{1,0:T(1,128)}, f32[54,1,768]{2,1,0:T(1,128)}) custom-call(f32[64,768]{1,0:T(8,128)S(1)} %gather.1.refs_0_, f32[64,768]{1,0:T(8,128)S(1)} %collective-permute-done.15.refs_1_), custom_call_target="tpu_custom_call" | custom-call | flops 1000000 | bytes 1000 | tf_op jit(solution)/shard_map/small/pallas_call | solution.py:25
  (22 shorter events, 1.6 us)
Async XLA Ops:
  2.3 9.7 %collective-permute-start.1 = (bf16[512,768]{1,0:T(8,128)(2,1)S(1)}, bf16[512,768]{1,0:T(8,128)(2,1)S(1)}, u32[]{:S(2)}, u32[]{:S(2)}) collective-permute-start(bf16[512,768]{1,0:T(8,128)(2,1)S(1)} %get-tuple-element.90.refs_0_.refs_1_.refs_3_.gp_ref), channel_id=1, source_target_pairs={{0,1},{1,0},{2,3},{3,2},{4,5},{5,4},{6,7},{7,6},{8,9},{9,8},{10,11... | collective-permute-start | bytes 2359304 | tf_op jit(solution)/shard_map/ppermute | solution.py:413
  8.6 4.7 %collective-permute-start = (bf16[512,768]{1,0:T(8,128)(2,1)S(1)}, bf16[512,768]{1,0:T(8,128)(2,1)S(1)}, u32[]{:S(2)}, u32[]{:S(2)}) collective-permute-start(bf16[512,768]{1,0:T(8,128)(2,1)S(1)} %get-tuple-element.89.refs_0_.refs_1_), channel_id=1, source_target_pairs={{0,1},{1,0},{2,3},{3,2},{4,5},{5,4},{6,7},{7,6},{8,9},{9,8},{10,11... | collective-permute-start | bytes 2359304 | tf_op jit(solution)/shard_map/ppermute | solution.py:413
  10.1 1.9 %collective-permute-start.2 = (bf16[384,512]{1,0:T(8,128)(2,1)S(1)}, bf16[384,512]{1,0:T(8,128)(2,1)S(1)}, u32[]{:S(2)}, u32[]{:S(2)}) collective-permute-start(bf16[384,512]{1,0:T(8,128)(2,1)S(1)} %get-tuple-element.95), channel_id=1, source_target_pairs={{0,1},{1,0},{2,3},{3,2},{4,5},{5,4},{6,7},{7,6},{8,9},{9,8},{10,11... | collective-permute-start | bytes 1179656 | tf_op jit(solution)/shard_map/ppermute | solution.py:413
  11.5 1.8 %collective-permute-start.3 = (bf16[384,512]{1,0:T(8,128)(2,1)S(1)}, bf16[384,512]{1,0:T(8,128)(2,1)S(1)}, u32[]{:S(2)}, u32[]{:S(2)}) collective-permute-start(bf16[384,512]{1,0:T(8,128)(2,1)S(1)} %get-tuple-element.101), channel_id=1, source_target_pairs={{0,1},{1,0},{2,3},{3,2},{4,5},{5,4},{6,7},{7,6},{8,9},{9,8},{10,11... | collective-permute-start | bytes 1179656 | tf_op jit(solution)/shard_map/ppermute | solution.py:413
  14.1 18.3 %collective-permute-start.7 = (bf16[384,768]{1,0:T(8,128)(2,1)S(1)}, bf16[384,768]{1,0:T(8,128)(2,1)S(1)}, u32[]{:S(2)}, u32[]{:S(2)}) collective-permute-start(bf16[384,768]{1,0:T(8,128)(2,1)S(1)} %half.3), channel_id=1, source_target_pairs={{0,2},{1,3},{2,0},{3,1},{4,6},{5,7},{6,4},{7,5},{8,10},{9,11},{10,... | collective-permute-start | bytes 1769480 | tf_op jit(solution)/shard_map/ppermute | solution.py:413
  16.8 15.6 %collective-permute-start.8 = (bf16[384,768]{1,0:T(8,128)(2,1)S(1)}, bf16[384,768]{1,0:T(8,128)(2,1)S(1)}, u32[]{:S(2)}, u32[]{:S(2)}) collective-permute-start(bf16[384,768]{1,0:T(8,128)(2,1)S(1)} %get-tuple-element.132), channel_id=1, source_target_pairs={{0,4},{1,5},{2,6},{3,7},{4,0},{5,1},{6,2},{7,3},{8,12},{9,13},{10,... | collective-permute-start | bytes 1769480 | tf_op jit(solution)/shard_map/ppermute | solution.py:413
  21.7 6.2 %collective-permute-start.5 = (bf16[768,512]{1,0:T(8,128)(2,1)S(1)}, bf16[768,512]{1,0:T(8,128)(2,1)S(1)}, u32[]{:S(2)}, u32[]{:S(2)}) collective-permute-start(bf16[768,512]{1,0:T(8,128)(2,1)S(1)} %get-tuple-element.113), channel_id=1, source_target_pairs={{0,1},{1,0},{2,3},{3,2},{4,5},{5,4},{6,7},{7,6},{8,9},{9,8},{10,11... | collective-permute-start | bytes 2359304 | tf_op jit(solution)/shard_map/ppermute | solution.py:413
  24.7 4.7 %collective-permute-start.6 = (bf16[768,512]{1,0:T(8,128)(2,1)S(1)}, bf16[768,512]{1,0:T(8,128)(2,1)S(1)}, u32[]{:S(2)}, u32[]{:S(2)}) collective-permute-start(bf16[768,512]{1,0:T(8,128)(2,1)S(1)} %get-tuple-element.116), channel_id=1, source_target_pairs={{0,1},{1,0},{2,3},{3,2},{4,5},{5,4},{6,7},{7,6},{8,9},{9,8},{10,11... | collective-permute-start | bytes 2359304 | tf_op jit(solution)/shard_map/ppermute | solution.py:413
  32.8 28.9 %collective-permute-start.10 = (bf16[768,768]{1,0:T(8,128)(2,1)S(1)}, bf16[768,768]{1,0:T(8,128)(2,1)S(1)}, u32[]{:S(2)}, u32[]{:S(2)}) collective-permute-start(bf16[768,768]{1,0:T(8,128)(2,1)S(1)} %relay.3), channel_id=1, source_target_pairs={{0,4},{1,5},{2,6},{3,7},{4,0},{5,1},{6,2},{7,3},{8,12},{9,13},{10,... | collective-permute-start | bytes 3538952 | tf_op jit(solution)/shard_map/ppermute | solution.py:413
  34.0 27.7 %collective-permute-start.9 = (bf16[768,768]{1,0:T(8,128)(2,1)S(1)}, bf16[768,768]{1,0:T(8,128)(2,1)S(1)}, u32[]{:S(2)}, u32[]{:S(2)}) collective-permute-start(bf16[768,768]{1,0:T(8,128)(2,1)S(1)} %relay.2), channel_id=1, source_target_pairs={{0,2},{1,3},{2,0},{3,1},{4,6},{5,7},{6,4},{7,5},{8,10},{9,11},{10,... | collective-permute-start | bytes 3538952 | tf_op jit(solution)/shard_map/ppermute | solution.py:413
  34.5 6.3 %collective-permute-start.4 = (bf16[768,512]{1,0:T(8,128)(2,1)S(1)}, bf16[768,512]{1,0:T(8,128)(2,1)S(1)}, u32[]{:S(2)}, u32[]{:S(2)}) collective-permute-start(bf16[768,512]{1,0:T(8,128)(2,1)S(1)} %get-tuple-element.107), channel_id=1, source_target_pairs={{0,1},{1,0},{2,3},{3,2},{4,5},{5,4},{6,7},{7,6},{8,9},{9,8},{10,11... | collective-permute-start | bytes 2359304 | tf_op jit(solution)/shard_map/ppermute | solution.py:413
  39.6 24.2 %collective-permute-start.14 = (bf16[8,64,768]{2,1,0:T(8,128)(2,1)S(1)}, bf16[8,64,768]{2,1,0:T(8,128)(2,1)S(1)}, u32[]{:S(2)}, u32[]{:S(2)}) collective-permute-start(bf16[8,64,768]{2,1,0:T(8,128)(2,1)S(1)} %back.1), channel_id=1, source_target_pairs={{8,0},{16,8},{24,16},{9,1},{17,9},{25,17},{10,2},{18,10},{26,18},{... | collective-permute-start | bytes 2359304 | tf_op jit(solution)/shard_map/ppermute | solution.py:409
  48.1 1.7 %collective-permute-start.11 = (f32[64,768]{1,0:T(8,128)S(1)}, f32[64,768]{1,0:T(8,128)S(1)}, u32[]{:S(2)}, u32[]{:S(2)}) collective-permute-start(f32[64,768]{1,0:T(8,128)S(1)} %taps.1.own_ref), channel_id=1, source_target_pairs={{0,1},{1,0},{2,3},{3,2},{4,5},{5,4},{6,7},{7,6},{8,9},{9,8},{10,11... | collective-permute-start | bytes 589832 | tf_op jit(solution)/shard_map/ppermute | solution.py:413
  49.8 13.9 %collective-permute-start.13 = (bf16[64,768]{1,0:T(8,128)(2,1)S(1)}, bf16[64,768]{1,0:T(8,128)(2,1)S(1)}, u32[]{:S(2)}, u32[]{:S(2)}) collective-permute-start(bf16[64,768]{1,0:T(8,128)(2,1)S(1)} %get-tuple-element.158), channel_id=1, source_target_pairs={{0,6},{2,4},{4,2},{6,0},{8,14},{10,12},{12,10},{14,8},{16,22},{18,... | collective-permute-start | bytes 294920 | tf_op jit(solution)/shard_map/ppermute | solution.py:559
  53.5 10.2 %collective-permute-start.12 = (bf16[64,768]{1,0:T(8,128)(2,1)S(1)}, bf16[64,768]{1,0:T(8,128)(2,1)S(1)}, u32[]{:S(2)}, u32[]{:S(2)}) collective-permute-start(bf16[64,768]{1,0:T(8,128)(2,1)S(1)} %get-tuple-element.158), channel_id=1, source_target_pairs={{0,2},{1,5},{2,0},{3,7},{4,6},{5,1},{6,4},{7,3},{8,10},{9,13},{10,... | collective-permute-start | bytes 294920 | tf_op jit(solution)/shard_map/ppermute | solution.py:558
  63.7 1.5 %collective-permute-start.15 = (f32[64,768]{1,0:T(8,128)S(1)}, f32[64,768]{1,0:T(8,128)S(1)}, u32[]{:S(2)}, u32[]{:S(2)}) collective-permute-start(f32[64,768]{1,0:T(8,128)S(1)} %gather.1.refs_0_), channel_id=1, source_target_pairs={{0,1},{1,0},{2,3},{3,2},{4,5},{5,4},{6,7},{7,6},{8,9},{9,8},{10,11... | collective-permute-start | bytes 589832 | tf_op jit(solution)/shard_map/ppermute | solution.py:413
